TPU v7x, 32 devices: a whole 2x2x4 slice. The times are simulated.
32 devices in a mesh: region: 4 (over z), tile: 8 (over y, x, core).
Axes of the slice: x: 2, y: 2, z: 4, core: 2. Of those that a mesh axis runs over, the one named last changes fastest.
Arguments:
- movie: bfloat16 [131072, 256], P(('region', 'tile'))
- footprint: float32 [8192, 128], P(('region', 'tile')), may hold values from 0.05 to 1
- support_idx: int32 [8192, 128], P(('region', 'tile')), may hold values from 0 to 4095
- trace_old: float32 [8192, 256], P(('region', 'tile')), may hold values from 0 to 7.5
- ar_coef: float32 [2], replicated, as said below
- border_fp: float32 [1536, 128], P(('region', 'tile')), may hold values from 0.05 to 1
- border_idx: int32 [1536, 128], P(('region', 'tile')), may hold values from 0 to 4095
- border_owner: int32 [1536], P(('region', 'tile')), may hold values from 0 to 255
- border_offset: int32 [1536, 1], P(('region', 'tile')), may hold values from 0 to 6; in each aligned block of 48 rows (0 to 47, 48 to 95, ...) at most 8 rows name the same one
- back_spatial: float32 [131072], P(('region', 'tile')), may hold values from 0.1 to 1
- back_trace: float32 [256], replicated, may hold values from 0.5 to 1.5
Outputs:
- trace_new: float32 [8192, 256], P(('region', 'tile'))
- footprint_new: float32 [8192, 128], P(('region', 'tile'))
- border_new: float32 [1536, 128], P(('region', 'tile'))
- back_new: float32 [256], replicated
Inputs may be any that keep to these rules, and one draw needn't show every extreme that they name: `border_offset`: in the rows of one tile at most 8 border rows name the same offset, a bound that some block reaches. ar_coef = (p + r, -p r) with slow root p and fast root r.
All inputs are finite; a program needn't handle non-finite values.
Results may differ from a plain program's by a relative error of at most 0.0081.
The roundings to bfloat16 on the way count: a program that leaves them out, or rounds other values in their place, can miss the bound.
Values sent between devices are 32-bit elements; how exact they have to be, the bound alone decides.
No kernel may reach another device: no remote copies, remote signals or barrier semaphores. Data moves between devices by JAX's collectives and lax.ppermute only.
A program may use at most 64 MiB of HBM per device.

v0:
```python
import jax
import jax.numpy as jnp
from jax import lax
from jax.sharding import PartitionSpec as P

CAP = 8


RIDGE = 1.0
EXACT = lax.Precision.HIGHEST


def slot_table(own_tile, offsets, tile_count, capacity):
    target = (own_tile + 1 + offsets) % tile_count
    target_hits = (target[:, None] == jnp.arange(tile_count, dtype=jnp.int32)[None, :]).astype(
        jnp.int32
    )
    bucket_rank = jnp.sum((jnp.cumsum(target_hits, axis=0) - target_hits) * target_hits, axis=1)
    slot_index = target * capacity + bucket_rank
    slot_range = jnp.arange(tile_count * capacity, dtype=jnp.int32)
    return (slot_index[:, None] == slot_range[None, :]).astype(jnp.float32)


def dense_map(values, places, voxel_count):
    row_count = values.shape[0]
    columns = jnp.broadcast_to(jnp.arange(row_count, dtype=jnp.int32)[:, None], places.shape)
    dense_grid = jnp.zeros((voxel_count, row_count), jnp.float32)
    dense_grid = dense_grid.at[places.reshape(-1), columns.reshape(-1)].add(values.reshape(-1))
    return dense_grid.astype(jnp.bfloat16)


def impulse_matrix(ar_coef, frame_count):
    prior_step_weight = ar_coef[0]
    earlier_step_weight = ar_coef[1]
    response = [jnp.ones((), jnp.float32), prior_step_weight]
    for position in range(2, frame_count):
        response.append(prior_step_weight * response[-1] + earlier_step_weight * response[-2])
    impulse = jnp.stack(response[:frame_count])
    later = jnp.arange(frame_count, dtype=jnp.int32)[:, None]
    earlier = jnp.arange(frame_count, dtype=jnp.int32)[None, :]
    offset = jnp.clip(later - earlier, 0, frame_count - 1)
    return jnp.where(later >= earlier, impulse[offset], jnp.zeros((), jnp.float32))


def whiten(trace_in, ar_coef):
    prev_one = jnp.pad(trace_in, ((0, 0), (1, 0)))[:, :-1]
    prev_two = jnp.pad(trace_in, ((0, 0), (2, 0)))[:, :-2]
    return trace_in - ar_coef[0] * prev_one - ar_coef[1] * prev_two


def reconstruct(dense_own, dense_in, trace_own, trace_in):
    first = jnp.dot(dense_own, trace_own.astype(jnp.bfloat16), preferred_element_type=jnp.float32)
    return first + jnp.dot(dense_in.astype(jnp.float32), trace_in, precision=EXACT)


def body(
    movie,
    footprint,
    support_idx,
    trace_old,
    ar_coef,
    border_fp,
    border_idx,
    border_owner,
    border_offset,
    back_spatial,
    back_trace,
):
    tiles = lax.axis_size("tile")
    own_tile = lax.axis_index("tile")
    voxel_count = movie.shape[0]
    owned = footprint.shape[0]
    frame_count = movie.shape[1]
    slots = tiles * CAP
    place = slot_table(own_tile, border_offset[:, 0], tiles, CAP)
    place_t = place.T
    send_fp = jnp.dot(place_t, border_fp, precision=EXACT).reshape(tiles, CAP, -1)
    send_idx = jnp.dot(place_t, border_idx.astype(jnp.float32), precision=EXACT).reshape(
        tiles, CAP, -1
    )
    owner_rows = jnp.take(trace_old, border_owner, axis=0)
    send_old = jnp.dot(place_t, owner_rows, precision=EXACT).reshape(tiles, CAP, frame_count)
    send_owner = jnp.dot(place_t, border_owner.astype(jnp.float32), precision=EXACT).reshape(
        tiles, CAP
    )
    in_fp, in_idx, in_old, in_owner = (
        lax.all_to_all(send_fp, "tile", split_axis=0, concat_axis=0, tiled=True),
        lax.all_to_all(send_idx, "tile", split_axis=0, concat_axis=0, tiled=True),
        lax.all_to_all(send_old, "tile", split_axis=0, concat_axis=0, tiled=True),
        lax.all_to_all(send_owner, "tile", split_axis=0, concat_axis=0, tiled=True),
    )
    in_fp = in_fp.reshape(slots, -1)
    in_idx = in_idx.reshape(slots, -1).astype(jnp.int32)
    in_old = in_old.reshape(slots, frame_count)
    in_owner = in_owner.reshape(slots).astype(jnp.int32)
    dense_own = dense_map(footprint, support_idx, voxel_count)
    dense_in = dense_map(in_fp, in_idx, voxel_count)
    recon = (
        reconstruct(dense_own, dense_in, trace_old, in_old)
        + back_spatial[:, None] * back_trace[None, :]
    )
    resid = (movie.astype(jnp.float32) - recon).astype(jnp.bfloat16)
    dims_voxel = (((0,), (0,)), ((), ()))
    proj_own = lax.dot_general(dense_own, resid, dims_voxel, preferred_element_type=jnp.float32)
    proj_in = lax.dot_general(dense_in, resid, dims_voxel, preferred_element_type=jnp.float32)
    returned = lax.all_to_all(
        proj_in.reshape(tiles, CAP, frame_count), "tile", split_axis=0, concat_axis=0, tiled=True
    )
    mine = jnp.dot(place, returned.reshape(slots, frame_count), precision=EXACT)
    owner_hot = (border_owner[:, None] == jnp.arange(owned, dtype=jnp.int32)[None, :]).astype(
        jnp.float32
    )
    gain = proj_own + jnp.dot(owner_hot.T, mine, precision=EXACT)
    energy = jnp.sum(footprint * footprint, axis=1) + jnp.dot(
        owner_hot.T, jnp.sum(border_fp * border_fp, axis=1), precision=EXACT
    )
    raw = trace_old + gain / energy[:, None]
    spikes = jnp.maximum(whiten(raw, ar_coef), 0.0)
    inverse = impulse_matrix(ar_coef, frame_count)
    trace_new = jnp.dot(spikes, inverse.T, precision=EXACT)
    region_rows = lax.all_gather(trace_new, "tile", axis=0, tiled=True)
    source = jnp.arange(slots, dtype=jnp.int32) // CAP
    in_new = jnp.take(region_rows, source * owned + in_owner, axis=0)
    rest = movie.astype(jnp.float32) - reconstruct(dense_own, dense_in, trace_new, in_new)
    partial_value = jnp.dot(back_spatial, rest, precision=EXACT)
    spatial_norm = jnp.sum(back_spatial * back_spatial)
    total_sum, norm_sum = lax.psum((partial_value, spatial_norm), ("region", "tile"))
    back_new = total_sum / norm_sum
    resid2 = (rest - back_spatial[:, None] * back_new[None, :]).astype(jnp.bfloat16)
    dims_frame = (((1,), (1,)), ((), ()))
    grad_own = lax.dot_general(
        trace_new.astype(jnp.bfloat16), resid2, dims_frame, preferred_element_type=jnp.float32
    )
    grad_in = lax.dot_general(
        in_new.astype(jnp.bfloat16), resid2, dims_frame, preferred_element_type=jnp.float32
    )
    denom_own = jnp.sum(trace_new * trace_new, axis=1) + RIDGE
    denom_in = jnp.sum(in_new * in_new, axis=1) + RIDGE
    footprint_new = jnp.maximum(
        footprint + jnp.take_along_axis(grad_own, support_idx, axis=1) / denom_own[:, None], 0.0
    )
    in_next = jnp.maximum(
        in_fp + jnp.take_along_axis(grad_in, in_idx, axis=1) / denom_in[:, None], 0.0
    )
    back_rows = lax.all_to_all(
        in_next.reshape(tiles, CAP, -1), "tile", split_axis=0, concat_axis=0, tiled=True
    )
    border_new = jnp.dot(place, back_rows.reshape(slots, -1), precision=EXACT)
    return (trace_new, footprint_new, border_new, back_new)


def solution(mesh):
    return jax.shard_map(
        body,
        mesh=mesh,
        in_specs=(
            P(("region", "tile"), None),
            P(("region", "tile"), None),
            P(("region", "tile"), None),
            P(("region", "tile"), None),
            P(),
            P(("region", "tile"), None),
            P(("region", "tile"), None),
            P(("region", "tile")),
            P(("region", "tile"), None),
            P(("region", "tile")),
            P(),
        ),
        out_specs=(
            P(("region", "tile"), None),
            P(("region", "tile"), None),
            P(("region", "tile"), None),
            P(),
        ),
        check_vma=False,
    )
```

profile of v0, /device:TPU:0, one launch (start us, length us, event | category | flops | bytes accessed | tf_op | source)
XLA Modules:
  0.0 1599.6 jit_solution(1833381426224288498)
XLA Ops:
  10.5 5.2 all-to-all-start
  205.1 173.5 %scatter_custom_fusion = f32[1048576]{0:T(1024)} fusion(s32[32768]{0:T(1024)S(1)} %broadcast_select_fusion, f32[32768]{0:T(1024)} %bitcast.346, f32[]{:T(128)} %constant.73.clone.1), kind=kCustom, calls=%fused_computation.14 | custom fusion | flops 32768 | bytes 4194816
  378.6 3.8 convert_element_type.105
  519.7 406.1 %gather_fusion.1 = f32[65536]{0:T(1024)S(1)} fusion(f32[256]{0:T(256)S(1)} %stack.1019, s32[65536]{0:T(1024)S(1)} %broadcast_clamp_fusion), kind=kCustom, calls=%fused_computation.1 | custom fusion | bytes 786432 | tf_op jit(solution)/shard_map/gather | solution.py:42
  927.3 4.2 all-to-all-start.1
  932.0 4.4 all-to-all-done.1
  936.4 3.4 all-to-all-start.2
  940.3 47.2 %scatter_custom_fusion.1 = f32[262144]{0:T(1024)S(1)} fusion(s32[8192]{0:T(1024)} %broadcast_select_fusion.1, f32[8192]{0:T(1024)S(1)} %bitcast.349, f32[]{:T(128)} %constant.73.clone.1), kind=kCustom, calls=%fused_computation.27 | custom fusion | flops 8192 | bytes 1049088
  989.7 4.4 fusion.3
  996.5 4.3 all-to-all-start.3
  1000.8 3.2 fusion.78
  1007.3 3.5 multiply_reduce_fusion.1
  1011.7 3.3 all-to-all-start.4
  1015.6 3.8 all-to-all-done.4
  1021.5 3.6 fusion.35
  1025.2 13.9 all-gather.2.cloned.1.call-done
  1039.1 2.9 copy.25
  1044.4 4.2 fusion
  1052.7 39.5 %all-reduce.2 = (f32[256]{0:T(256)S(1)}, f32[]{:T(128)}) all-reduce(f32[256]{0:T(256)S(1)} %bitcast.353, f32[]{:T(128)} %multiply_reduce_fusion.6), channel_id=1, replica_groups=mesh['region'=4,'tile'=8] {'region','tile'}, use_global_device_ids=true, to_apply=%region_6.7 | all-reduce | flops 257 | bytes 2056 | tf_op jit(solution)/shard_map/psum | solution.py:127
  1093.0 2.9 fusion.40
  1096.0 3.0 fusion.33
  1099.1 65.0 %gather_fusion.4 = f32[8192]{0:T(1024)S(1)} fusion(f32[64,4096]{1,0:T(8,128)S(1)} %fusion.40, s32[8192]{0:T(1024)S(1)} %fusion.44), kind=kCustom, calls=%fused_computation.4 | custom fusion | bytes 131072 | tf_op jit(solution)/shard_map/jit(take_along_axis)/gather | solution.py:143
  1164.8 4.7 all-to-all-start.5
  1169.5 421.7 %gather_fusion.3 = f32[32768]{0:T(1024)S(1)} fusion(f32[256,4096]{1,0:T(8,128)} %fusion.33, s32[32768]{0:T(1024)S(1)} %fusion.23), kind=kCustom, calls=%fused_computation.3 | custom fusion | bytes 524288 | tf_op jit(solution)/shard_map/jit(take_along_axis)/gather | solution.py:140
  (105 shorter events, 44.9 us)
Async XLA Ops:
  8.8 379.6 %copy-start.10 = (s32[48]{0:T(128)}, s32[48]{0:T(128)S(1)}, u32[]{:S(2)}) copy-start(s32[48]{0:T(128)S(1)} %fusion.72) | copy-start | bytes 580
  10.5 916.9 %all-to-all-start = ((f32[8,8,128]{2,1,0:T(8,128)}), f32[8,8,128]{2,1,0:T(8,128)S(1)}, u32[]{:S(2)}, u32[]{:S(2)}) async-start(f32[8,8,128]{2,1,0:T(8,128)} %convolution_bitcast_fusion.3), calls=%async_computation | async-start | bytes 65536 | tf_op jit(solution)/shard_map/all_to_all | solution.py:88
  378.6 6.5 copy-start.5
  385.1 3.3 copy-start.15
  519.7 411.9 %copy-start.14 = (s32[2]{0:T(128)S(1)}, s32[2]{0:T(128)}, u32[]{:S(2)}) copy-start(s32[2]{0:T(128)} %constant.139) | copy-start | bytes 28
  519.7 412.1 %copy-start.13 = (s32[2]{0:T(128)S(1)}, s32[2]{0:T(128)}, u32[]{:S(2)}) copy-start(s32[2]{0:T(128)} %constant.136) | copy-start | bytes 28
  925.8 63.9 %copy-start.8 = (f32[4096]{0:T(1024)S(1)}, f32[4096]{0:T(1024)}, u32[]{:S(2)}) copy-start(f32[4096]{0:T(1024)} %param.20) | copy-start | bytes 49156
  927.3 9.0 all-to-all-start.1
  936.4 53.3 %all-to-all-start.2 = ((f32[8,8,256]{2,1,0:T(8,128)}), f32[8,8,256]{2,1,0:T(8,128)S(1)}, u32[]{:S(2)}, u32[]{:S(2)}) async-start(f32[8,8,256]{2,1,0:T(8,128)} %convolution_bitcast_fusion), calls=%async_computation.2 | async-start | bytes 131072 | tf_op jit(solution)/shard_map/all_to_all | solution.py:89
  994.1 1.4 copy-start.2
  995.4 10.4 copy-start.11
  995.4 10.6 copy-start.12
  995.4 10.6 copy-start.16
  996.5 18.5 %copy-start.6 = (s32[256,128]{1,0:T(8,128)S(1)}, s32[256,128]{1,0:T(8,128)}, u32[]{:S(2)}) copy-start(s32[256,128]{1,0:T(8,128)} %param.13) | copy-start | bytes 393220
  996.5 9.3 all-to-all-start.3
  1000.8 38.3 %all-gather.2.cloned.1.call-start = ((), (), s32[]{:S(2)}) async-start(), calls=%async_computation.6 | async-start | bytes 2359296 | tf_op jit(solution)/shard_map/all_gather | solution.py:121
  1011.7 7.8 all-to-all-start.4
  1025.2 19.3 %copy-start.3 = (bf16[4096,256]{1,0:T(8,128)(2,1)S(1)}, bf16[4096,256]{1,0:T(8,128)(2,1)}, u32[]{:S(2)}) copy-start(bf16[4096,256]{1,0:T(8,128)(2,1)} %param.11) | copy-start | bytes 6291460
  1048.6 1.9 copy-start
  1050.5 45.4 %copy-start.4 = (f32[256,256]{0,1:T(8,128)S(1)}, f32[256,256]{0,1:T(8,128)}, u32[]{:S(2)}) copy-start(f32[256,256]{0,1:T(8,128)} %get-tuple-element.21) | copy-start | bytes 786436
  1092.2 3.8 copy-start.1
  1093.0 6.0 copy-start.9
  1164.8 427.1 %all-to-all-start.5 = ((f32[8,8,128]{2,1,0:T(8,128)}), f32[8,8,128]{2,1,0:T(8,128)S(1)}, u32[]{:S(2)}, u32[]{:S(2)}) async-start(f32[8,8,128]{2,1,0:T(8,128)} %fusion.49), calls=%async_computation.5 | async-start | bytes 65536 | tf_op jit(solution)/shard_map/all_to_all | solution.py:145
  1169.5 421.7 %copy-start.7 = (f32[256,128]{1,0:T(8,128)S(1)}, f32[256,128]{1,0:T(8,128)}, u32[]{:S(2)}) copy-start(f32[256,128]{1,0:T(8,128)} %param.12) | copy-start | bytes 393220
Sparse Core Ops, SparseCore 0:
  1010.9 28.1 all-gather.1
where the time goes:
time: 1620 us; the launch traced here: 1600 us
  local copies, waits for them, and re-layouts  912 us (56%)
  between operations  323 us (20%)
  other arithmetic  239 us (15%)
  blocking collectives  39.5 us (2%)
  matrix products  37.5 us (2%)
  starting transfers between devices  25 us (2%)
  waiting for transfers between devices  23.9 us (1%)
    gather x1, local copies, waits for them, and re-layouts, body(): jnp.take_along_axis(grad_own, support_idx, axis=1) / denom_own[:, None]  422 us
    gather x3, local copies, waits for them, and re-layouts, impulse_matrix(): impulse[offset]  407 us
    unnamed x9, other arithmetic  224 us
    gather x1, local copies, waits for them, and re-layouts, body(): jnp.take_along_axis(grad_in, in_idx, axis=1) / denom_in[:, None]  65 us
    psum x1, blocking collectives, body(): lax.psum((partial_value, spatial_norm), ('region', 'tile'))  39.5 us
  transfers between devices with their start and end apart: 7, of which 4 were waited for; matrix products, arithmetic and copies ran while one was open for 68% of the time, Pallas kernels for 0%

commit v1 on v0

v1 whole, which is shorter than its diff:
```python
import jax
import jax.numpy as jnp
from jax import lax
from jax.experimental import pallas as pl
from jax.experimental.pallas import tpu as pltpu
from jax.sharding import PartitionSpec as P

CAP = 8
RIDGE = 1.0
LANES = 128
F32 = jnp.float32
BF16 = jnp.bfloat16
VMEM_BYTES = 28 << 20
CHUNK = 512


def nn(a, b):
    return lax.dot_general(a, b, (((1,), (0,)), ((), ())), preferred_element_type=F32)


def nt(a, b):
    return lax.dot_general(a, b, (((1,), (1,)), ((), ())), preferred_element_type=F32)


def split(x, terms):
    parts = []
    for _ in range(terms):
        part = x.astype(BF16)
        parts.append(part)
        x = x - part.astype(F32)
    return parts


def select_rows(table, x, terms=3):
    total = None
    for part in reversed(split(x, terms)):
        term = nn(table, part)
        total = term if total is None else total + term
    return total


def iota(shape, dim):
    return lax.broadcasted_iota(jnp.int32, shape, dim)


def to_column(row):
    n = row.shape[1]
    return jnp.sum(jnp.where(iota((n, n), 0) == iota((n, n), 1), row, jnp.zeros_like(row)), axis=1, keepdims=True)


def shift_lanes(x, count):
    return jnp.where(iota(x.shape, len(x.shape) - 1) >= count, pltpu.roll(x, count, len(x.shape) - 1), 0.0)


def pack_kernel(tile_ref, bfp_ref, bidx_ref, bown_ref, boff_ref, old_ref, send_ref, pick_ref, pick_t_ref, place_ref):
    tiles = send_ref.shape[0] // CAP
    slots = send_ref.shape[0]
    border = bfp_ref.shape[0]
    owned = old_ref.shape[0]
    support = bfp_ref.shape[1]
    target = boff_ref[...] + (tile_ref[0] + 1)
    target = jnp.where(target >= tiles, target - tiles, target)
    target_col = to_column(target)
    same = target_col == target
    before = iota((border, border), 0) < iota((border, border), 1)
    rank = jnp.sum(jnp.where(jnp.logical_and(same, before), 1, 0), axis=0, keepdims=True)
    slot = target * CAP + rank
    owner = bown_ref[...]
    place_t = iota((slots, border), 0) == slot
    place = iota((border, slots), 1) == to_column(slot)
    owner_col = jnp.sum(jnp.where(place_t, owner + 1, 0), axis=1, keepdims=True) - 1
    owner_row = jnp.sum(jnp.where(place, to_column(owner) + 1, 0), axis=0, keepdims=True) - 1
    pick = jnp.where(iota((slots, owned), 1) == owner_col, 1.0, 0.0).astype(BF16)
    pick_ref[...] = pick
    pick_t_ref[...] = jnp.where(iota((owned, slots), 0) == owner_row, 1.0, 0.0).astype(BF16)
    place_ref[...] = jnp.where(place, 1.0, 0.0).astype(BF16)
    place_t = jnp.where(place_t, 1.0, 0.0).astype(BF16)
    send_ref[:, :support] = select_rows(place_t, bfp_ref[...])
    send_ref[:, support:2 * support] = select_rows(place_t, bidx_ref[...].astype(F32), 2)
    send_ref[:, 2 * support:] = select_rows(pick, old_ref[...])


def scatter_rows(values_ref, index_ref, grid_ref, rows):
    cells = grid_ref.shape[0] // rows
    support = values_ref.shape[1]
    hi_range = iota((cells, support), 0).astype(BF16)
    lo_range = iota((LANES, support), 0).astype(BF16)
    zero_lo = jnp.zeros((LANES, support), BF16)

    def one(row):
        index = index_ref[pl.ds(row, 1), :]
        value = values_ref[pl.ds(row, 1), :]
        high = jnp.broadcast_to((index >> 7).astype(F32), (cells, support)).astype(BF16)
        low = jnp.broadcast_to((index & 127).astype(F32), (LANES, support)).astype(BF16)
        coarse = value.astype(BF16).astype(F32)
        fine = value - coarse
        top = jnp.broadcast_to(coarse, (LANES, support)).astype(BF16)
        rest = jnp.broadcast_to(fine, (LANES, support)).astype(BF16)
        hit = low == lo_range
        left = jnp.where(high == hi_range, jnp.ones((cells, support), BF16), jnp.zeros((cells, support), BF16))
        left = jnp.concatenate([left, left], axis=1)
        right = jnp.concatenate([jnp.where(hit, top, zero_lo), jnp.where(hit, rest, zero_lo)], axis=1)
        grid_ref[pl.ds(row, cells, stride=rows), :] = nt(left, right)

    @pl.loop(0, rows // 8)
    def _(group):
        for k in range(8):
            one(group * 8 + k)


def prepare_kernel(movie_ref, fp_ref, idx_ref, dense_ref, movie_t_ref, grid_ref):
    rows = fp_ref.shape[0]
    voxels, frames = movie_ref.shape
    scatter_rows(fp_ref, idx_ref, grid_ref, rows)

    @pl.loop(0, voxels // LANES)
    def _(cell):
        at = pl.multiple_of(cell * LANES, LANES)
        start = pl.multiple_of(cell * rows, rows)
        dense_ref[:, pl.ds(at, LANES)] = grid_ref[pl.ds(start, rows), :].astype(BF16)

    eye = jnp.where(iota((frames, frames), 0) == iota((frames, frames), 1), 1.0, 0.0).astype(BF16)

    @pl.loop(0, voxels // CHUNK)
    def _(step):
        at = pl.multiple_of(step * CHUNK, CHUNK)
        movie_t_ref[:, pl.ds(at, CHUNK)] = nt(eye, movie_ref[pl.ds(at, CHUNK), :]).astype(BF16)


def project_kernel(recv_ref, movie_t_ref, dense_ref, old_ref, spatial_ref, trace_ref, resid_ref, dense_in_ref, proj_ref, idx_ref, values_ref, grid_ref):
    slots = recv_ref.shape[0]
    frames, voxels = movie_t_ref.shape
    support = values_ref.shape[1]
    values_ref[...] = recv_ref[:, :support]
    idx_ref[...] = recv_ref[:, support:2 * support].astype(jnp.int32)
    scatter_rows(values_ref, idx_ref, grid_ref, slots)

    @pl.loop(0, voxels // LANES)
    def _(cell):
        at = pl.multiple_of(cell * LANES, LANES)
        start = pl.multiple_of(cell * slots, slots)
        part = grid_ref[pl.ds(start, slots), :].astype(BF16)
        for copy in range(3):
            dense_in_ref[copy * slots:(copy + 1) * slots, pl.ds(at, LANES)] = part

    old_t = jnp.transpose(old_ref[...]).astype(BF16)
    in_t = jnp.concatenate([jnp.transpose(part.astype(F32)).astype(BF16) for part in split(recv_ref[:, 2 * support:], 3)], axis=1)
    back = to_column(trace_ref[...])

    @pl.loop(0, voxels // CHUNK)
    def _(step):
        at = pl.multiple_of(step * CHUNK, CHUNK)
        here = pl.ds(at, CHUNK)
        recon = nn(old_t, dense_ref[:, here]) + nn(in_t, dense_in_ref[:, here]) + back * spatial_ref[:, here]
        resid_ref[:, here] = (movie_t_ref[:, here].astype(F32) - recon).astype(BF16)

    proj_ref[:, :frames] = nt(dense_in_ref[:slots, :], resid_ref[...])
    parts = jnp.concatenate(split(jnp.broadcast_to(spatial_ref[...], (8, voxels)), 3), axis=0)
    sums = nt(dense_in_ref[:slots, :], parts)
    proj_ref[:, frames:] = jnp.broadcast_to(sums[:, 0:1] + sums[:, 8:9] + sums[:, 16:17], (slots, LANES))


def own_kernel(ar_ref, dense_ref, resid_ref, movie_ref, spatial_ref, fp_ref, send_ref, pick_t_ref, proj_ref, energy_ref, weight_ref, base_ref, impulse_ref):
    frames, voxels = resid_ref.shape
    owned, support = fp_ref.shape
    proj_ref[...] = nt(dense_ref[...], resid_ref[...])
    spatial = spatial_ref[...]
    parts = jnp.concatenate(split(jnp.broadcast_to(spatial, (8, voxels)), 3), axis=0)
    sums = nt(dense_ref[...], parts)
    weight_ref[...] = jnp.broadcast_to(sums[:, 0:1] + sums[:, 8:9] + sums[:, 16:17], (owned, LANES))
    seen = nn(parts, movie_ref[...])
    seen = seen[0:8] + seen[8:16] + seen[16:24]
    norm = jnp.sum(spatial * spatial, axis=1, keepdims=True)
    row = iota((8, LANES), 0)
    base_ref[...] = jnp.where(row == 0, seen[:, :LANES], jnp.where(row == 1, seen[:, LANES:], jnp.where(row == 2, norm, 0.0)))
    border_fp = send_ref[:, :support]
    square = jnp.broadcast_to(jnp.sum(border_fp * border_fp, axis=1, keepdims=True), (send_ref.shape[0], LANES))
    fp = fp_ref[...]
    energy_ref[...] = jnp.sum(fp * fp, axis=1, keepdims=True) + select_rows(pick_t_ref[...], square)
    near, far = ar_ref[0], ar_ref[1]
    response = jnp.where(iota((8, frames), 1) == 0, 1.0, 0.0)
    step = 1
    while step < frames:
        change = near * shift_lanes(response, step)
        if 2 * step < frames:
            change = change - far * shift_lanes(response, 2 * step)
        response = response + change
        near, far = near * near + 2.0 * far, -far * far
        step *= 2
    wide = jnp.broadcast_to(response[0:1], (frames, frames))
    wide = pltpu.roll(wide, 0, 1, stride=1, stride_axis=0)
    impulse_ref[...] = jnp.where(iota((frames, frames), 1) >= iota((frames, frames), 0), wide, 0.0)


def trace_kernel(ar_ref, back_ref, proj_ref, energy_ref, weight_ref, base_ref, impulse_ref, old_ref, pick_ref, pick_t_ref, new_ref, send_ref):
    owned, frames = old_ref.shape
    returned = select_rows(pick_t_ref[...], back_ref[...])
    gain = proj_ref[...] + returned[:, :frames]
    raw = old_ref[...] + gain / energy_ref[:, 0:1]
    spikes = jnp.maximum(raw - ar_ref[0] * shift_lanes(raw, 1) - ar_ref[1] * shift_lanes(raw, 2), 0.0)
    new = jnp.dot(spikes, impulse_ref[...], precision=lax.Precision.HIGHEST, preferred_element_type=F32)
    new_ref[...] = new
    send_ref[:, :frames] = select_rows(pick_ref[...], new)
    used = weight_ref[:, 0:1] * new.astype(BF16).astype(F32) + returned[:, frames:frames + 1] * new
    used = jnp.sum(used, axis=0, keepdims=True)
    base = base_ref[...]
    row = iota((8, LANES), 0)
    base = base - jnp.where(row == 0, used[:, :LANES], jnp.where(row == 1, used[:, LANES:], 0.0))
    for tile in range(send_ref.shape[0] // CAP):
        send_ref[tile * CAP:(tile + 1) * CAP, frames:] = base


def rest_kernel(recv_ref, movie_t_ref, dense_ref, dense_in_ref, new_ref, rest_ref):
    frames, voxels = movie_t_ref.shape
    new_t = jnp.transpose(new_ref[...]).astype(BF16)
    in_t = jnp.concatenate([jnp.transpose(part.astype(F32)).astype(BF16) for part in split(recv_ref[:, :frames], 3)], axis=1)

    @pl.loop(0, voxels // CHUNK)
    def _(step):
        at = pl.multiple_of(step * CHUNK, CHUNK)
        here = pl.ds(at, CHUNK)
        recon = nn(new_t, dense_ref[:, here]) + nn(in_t, dense_in_ref[:, here])
        rest_ref[:, here] = movie_t_ref[:, here].astype(F32) - recon


def pick_support(grad_ref, idx_ref, out, rows):
    cells = grad_ref.shape[1] // LANES

    @pl.loop(0, rows // 8)
    def _(group):
        start = pl.multiple_of(group * 8, 8)
        here = pl.ds(start, 8)
        index = idx_ref[here, :]
        high = index >> 7
        low = index & 127
        picked = jnp.zeros(index.shape, F32)
        for cell in range(cells):
            found = jnp.take_along_axis(grad_ref[here, cell * LANES:(cell + 1) * LANES], low, axis=1, mode="promise_in_bounds")
            picked = jnp.where(high == cell, found, picked)
        out(here, picked)


def border_kernel(recv0_ref, recv_ref, *refs):
    *totals, spatial_ref, rest_ref, resid_ref, next_ref, back_ref, grad_ref, idx_ref, denom_ref = refs
    frames, voxels = rest_ref.shape
    slots, support = next_ref.shape
    total = totals[0][...]
    for other in totals[1:]:
        total = total + other[...]
    back = total[0:2] / total[2:3, 0:1]
    back_ref[...] = back
    back = to_column(jnp.concatenate([back[0:1], back[1:2]], axis=1))
    new = recv_ref[:, :frames]
    new_low = new.astype(BF16)

    @pl.loop(0, voxels // CHUNK)
    def _(step):
        at = pl.multiple_of(step * CHUNK, CHUNK)
        here = pl.ds(at, CHUNK)
        resid = (rest_ref[:, here] - back * spatial_ref[:, here]).astype(BF16)
        resid_ref[:, here] = resid
        grad_ref[:, here] = nn(new_low, resid)

    idx_ref[...] = recv0_ref[:, support:2 * support].astype(jnp.int32)
    denom_ref[...] = jnp.broadcast_to(jnp.sum(new * new, axis=1, keepdims=True) + RIDGE, (slots, support))

    def out(here, picked):
        next_ref[here, :] = jnp.maximum(recv0_ref[here, :support] + picked / denom_ref[here, :], 0.0)

    pick_support(grad_ref, idx_ref, out, slots)


def footprint_kernel(resid_ref, new_ref, fp_ref, idx_ref, out_ref, grad_ref, denom_ref):
    frames, voxels = resid_ref.shape
    owned, support = fp_ref.shape
    new = new_ref[...]
    new_low = new.astype(BF16)
    denom_ref[...] = jnp.broadcast_to(jnp.sum(new * new, axis=1, keepdims=True) + RIDGE, (owned, support))

    @pl.loop(0, voxels // CHUNK)
    def _(step):
        at = pl.multiple_of(step * CHUNK, CHUNK)
        here = pl.ds(at, CHUNK)
        grad_ref[:, here] = nn(new_low, resid_ref[:, here])

    def out(here, picked):
        out_ref[here, :] = jnp.maximum(fp_ref[here, :] + picked / denom_ref[here, :], 0.0)

    pick_support(grad_ref, idx_ref, out, owned)


def unpack_kernel(place_ref, rows_ref, out_ref):
    out_ref[...] = select_rows(place_ref[...], rows_ref[...])


def call(kernel, outs, scratch=(), name=None, smem=0, inputs=0, flops=0):
    specs = [pl.BlockSpec(memory_space=pltpu.SMEM)] * smem + [pl.BlockSpec(memory_space=pltpu.VMEM)] * (inputs - smem)
    many = len(outs) > 1
    shapes = [jax.ShapeDtypeStruct(s, d) for s, d in outs]
    return pl.pallas_call(
        kernel,
        out_shape=shapes if many else shapes[0],
        in_specs=specs,
        out_specs=[pl.BlockSpec(memory_space=pltpu.VMEM)] * len(outs) if many else pl.BlockSpec(memory_space=pltpu.VMEM),
        scratch_shapes=list(scratch),
        compiler_params=pltpu.CompilerParams(vmem_limit_bytes=VMEM_BYTES),
        name=name,
    )


def exchange(rows, tiles):
    width = rows.shape[1]
    moved = lax.all_to_all(rows.reshape(tiles, CAP, width), "tile", split_axis=0, concat_axis=0, tiled=True)
    return moved.reshape(tiles * CAP, width)


def body(movie, footprint, support_idx, trace_old, ar_coef, border_fp, border_idx, border_owner, border_offset, back_spatial, back_trace):
    tiles = lax.axis_size("tile")
    regions = lax.axis_size("region")
    tile = lax.axis_index("tile").astype(jnp.int32).reshape(1)
    voxels, frames = movie.shape
    owned, support = footprint.shape
    border = border_fp.shape[0]
    slots = tiles * CAP
    cells = voxels // LANES
    spatial = back_spatial.reshape(1, voxels)

    send, pick, pick_t, place = call(
        pack_kernel,
        [((slots, 2 * support + frames), F32), ((slots, owned), BF16), ((owned, slots), BF16), ((border, slots), BF16)],
        name="pack", smem=1, inputs=6,
    )(tile, border_fp, border_idx, border_owner.reshape(1, border), border_offset.reshape(1, border), trace_old)
    recv = exchange(send, tiles)
    dense, movie_t = call(
        prepare_kernel,
        [((owned, voxels), BF16), ((frames, voxels), BF16)],
        [pltpu.VMEM((cells * owned, LANES), F32)],
        name="prepare", inputs=3,
    )(movie, footprint, support_idx)
    resid, dense_in, proj_in = call(
        project_kernel,
        [((frames, voxels), BF16), ((3 * slots, voxels), BF16), ((slots, frames + LANES), F32)],
        [pltpu.VMEM((slots, support), jnp.int32), pltpu.VMEM((slots, support), F32), pltpu.VMEM((cells * slots, LANES), F32)],
        name="project", inputs=6,
    )(recv, movie_t, dense, trace_old, spatial, back_trace.reshape(1, frames))
    returned = exchange(proj_in, tiles)
    proj, energy, weight, base, impulse = call(
        own_kernel,
        [((owned, frames), F32), ((owned, LANES), F32), ((owned, LANES), F32), ((8, LANES), F32), ((frames, frames), F32)],
        name="own", smem=1, inputs=8,
    )(ar_coef, dense, resid, movie, spatial, footprint, send, pick_t)
    trace_new, send_new = call(
        trace_kernel,
        [((owned, frames), F32), ((slots, frames + LANES), F32)],
        name="trace", smem=1, inputs=10,
    )(ar_coef, returned, proj, energy, weight, base, impulse, trace_old, pick, pick_t)
    recv_new = exchange(send_new, tiles)
    total = jnp.sum(recv_new[:, frames:].reshape(tiles, CAP, LANES), axis=0)
    totals = [total] + [
        lax.ppermute(total, "region", [(i, (i + shift) % regions) for i in range(regions)])
        for shift in range(1, regions)
    ]
    rest = call(
        rest_kernel, [((frames, voxels), F32)], name="rest", inputs=5,
    )(recv_new, movie_t, dense, dense_in, trace_new)
    resid2, in_next, back = call(
        border_kernel,
        [((frames, voxels), BF16), ((slots, support), F32), ((2, LANES), F32)],
        [pltpu.VMEM((slots, voxels), F32), pltpu.VMEM((slots, support), jnp.int32), pltpu.VMEM((slots, support), F32)],
        name="border", inputs=4 + regions,
    )(recv, recv_new, *totals, spatial, rest)
    back_rows = exchange(in_next, tiles)
    footprint_new = call(
        footprint_kernel,
        [((owned, support), F32)],
        [pltpu.VMEM((owned, voxels), F32), pltpu.VMEM((owned, support), F32)],
        name="footprint", inputs=4,
    )(resid2, trace_new, footprint, support_idx)
    border_new = call(unpack_kernel, [((border, support), F32)], name="unpack", inputs=2)(place, back_rows)
    return (trace_new, footprint_new, border_new, back.reshape(frames))


def solution(mesh):
    row = P(("region", "tile"), None)
    flat = P(("region", "tile"))
    return jax.shard_map(
        body,
        mesh=mesh,
        in_specs=(row, row, row, row, P(), row, row, flat, row, flat, P()),
        out_specs=(row, row, row, P()),
        check_vma=False,
    )
```

time: 1620 us -> 87.5 us (0.05); the launches traced: 1600 us -> 86.5 us
  local copies, waits for them, and re-layouts: 912 us -> 21.3 us
  between operations: 323 us -> 0.82 us
  other arithmetic: 239 us -> 0.01 us
  Pallas kernels: 0 us -> 37.9 us
  matrix products: 37.5 us -> 0 us
  blocking collectives: 39.5 us -> 9.17 us
  waiting for transfers between devices: 23.9 us -> 0.02 us
    gather x7 -> x0, local copies, waits for them, and re-layouts: 897 us -> none  [the longest x1 422 us: body(): jnp.take_along_axis(grad_own, support_idx, axis=1) / denom_own[:, None]]
    unnamed x9 -> x0, other arithmetic: 224 us -> none
    psum x1 -> x0, blocking collectives: 39.5 us -> none  [body(): lax.psum((partial_value, spatial_norm), ('region', 'tile'))]
    pallas_call x0 -> x9, Pallas kernels: none -> 37.9 us  [the longest x1 12.2 us: body(): call(prepare_kernel, [((owned, voxels), BF16), ((frames, voxels), BF16)],...]
    dot_general x18 -> x0, matrix products: 37.5 us -> none  [the longest x2 8.52 us: reconstruct(): jnp.dot(dense_in.astype(jnp.float32), trace_in, precision=EXACT)]
  transfers between devices with their start and end apart: 7 -> 6, of which waited for: 4 -> 0; matrix products, arithmetic and copies ran while one was open for 68% -> 0% of each run, Pallas kernels for 0% -> 27%
where the time goes in v1:
time: 87.5 us; the launch traced here: 86.5 us
  Pallas kernels  37.9 us (43%)
  local copies, waits for them, and re-layouts  21.3 us (24%)
  starting transfers between devices  17.3 us (20%)
  blocking collectives  9.17 us (10%)
    unnamed x52, local copies, waits for them, and re-layouts  21.3 us
    all_to_all x3, starting transfers between devices, exchange(): lax.all_to_all(rows.reshape(tiles, CAP, width), 'tile', split_axis=0, con...  12.7 us
    pallas_call x1, Pallas kernels, body(): call(prepare_kernel, [((owned, voxels), BF16), ((frames, voxels), BF16)],...  12.2 us
    all_to_all x1, blocking collectives, exchange(): lax.all_to_all(rows.reshape(tiles, CAP, width), 'tile', split_axis=0, con...  9.17 us
    pallas_call x1, Pallas kernels, body(): call(project_kernel, [((frames, voxels), BF16), ((3 * slots, voxels), BF1...  7.26 us
    pallas_call x1, Pallas kernels, body(): call(footprint_kernel, [((owned, support), F32)], [pltpu.VMEM((owned, vox...  6.13 us
    ppermute x3, starting transfers between devices, body(): lax.ppermute(total, 'region', [(i, (i + shift) % regions) for i in range(...  4.62 us
    pallas_call x1, Pallas kernels, body(): call(border_kernel, [((frames, voxels), BF16), ((slots, support), F32), (...  3.3 us
  transfers between devices with their start and end apart: 6, of which 0 were waited for; matrix products, arithmetic and copies ran while one was open for 0% of the time, Pallas kernels for 27%

profile of v1, /device:TPU:0, one launch (start us, length us, event | category | flops | bytes accessed | tf_op | source)
XLA Modules:
  0.0 86.5 jit_solution(3693579628545299764)
XLA Ops:
  4.4 1.0 %pack.1 = (f32[64,512]{1,0:T(8,128)}, bf16[64,256]{1,0:T(8,128)(2,1)S(1)}, bf16[256,64]{1,0:T(8,128)(2,1)S(1)}, bf16[48,64]{1,0:T(8,128)(2,1)S(1)}) custom-call(s32[1]{0:T(128)} %bitcast.tile_ref, f32[48,128]{1,0:T(8,128)S(1)} %copy-done.20, s32[48,128]{1,0:T(8,128)S(1)} %copy-done.21, s32[1,48]{1,0:T(1,128)S(1)} %bitcast.30, s32[1,48]{1,0:T(1,128)S(1)} %bitcast.31, ...), custom_call_target="tpu_custom_call" | custom-call | tf_op jit(solution)/shard_map/pack/pallas_call | solution.py:328
  5.4 5.2 %all-to-all-start = ((f32[8,8,512]{2,1,0:T(8,128)}), f32[8,8,512]{2,1,0:T(8,128)S(1)}, u32[]{:S(2)}, u32[]{:S(2)}) async-start(f32[8,8,512]{2,1,0:T(8,128)} %bitcast.3), calls=%async_computation | async-start | bytes 262144 | tf_op jit(solution)/shard_map/all_to_all | solution.py:313
  10.6 1.6 %copy-done.3 = bf16[4096,256]{1,0:T(8,128)(2,1)S(1)} copy-done((bf16[4096,256]{1,0:T(8,128)(2,1)S(1)}, bf16[4096,256]{1,0:T(8,128)(2,1)}, u32[]{:S(2)}) %copy-start.3) | copy-done | bytes 2097176
  14.0 12.2 %prepare.1 = (bf16[256,4096]{1,0:T(8,128)(2,1)S(1)}, bf16[256,4096]{1,0:T(8,128)(2,1)S(1)}) custom-call(bf16[4096,256]{1,0:T(8,128)(2,1)S(1)} %copy-done.3, f32[256,128]{1,0:T(8,128)S(1)} %copy-done.11, s32[256,128]{1,0:T(8,128)S(1)} %copy-done.15), custom_call_target="tpu_custom_call" | custom-call | tf_op jit(solution)/shard_map/prepare/pallas_call | solution.py:334
  26.2 1.4 %copy-done = bf16[256,4096]{1,0:T(8,128)(2,1)} copy-done((bf16[256,4096]{1,0:T(8,128)(2,1)}, bf16[256,4096]{1,0:T(8,128)(2,1)S(1)}, u32[]{:S(2)}) %copy-start) | copy-done | bytes 2097176
  27.6 1.6 %copy-done.1 = bf16[256,4096]{1,0:T(8,128)(2,1)S(1)} copy-done((bf16[256,4096]{1,0:T(8,128)(2,1)S(1)}, bf16[256,4096]{1,0:T(8,128)(2,1)}, u32[]{:S(2)}) %copy-start.1) | copy-done | bytes 2097176
  29.2 7.3 %project.1 = (bf16[256,4096]{1,0:T(8,128)(2,1)S(1)}, bf16[192,4096]{1,0:T(8,128)(2,1)S(1)}, f32[64,384]{1,0:T(8,128)}) custom-call(f32[64,512]{1,0:T(8,128)S(1)} %bitcast.18, bf16[256,4096]{1,0:T(8,128)(2,1)S(1)} %copy-done.1, bf16[256,4096]{1,0:T(8,128)(2,1)S(1)} %get-tuple-element.25.dense_ref, f32[256,256]{1,0:T(8,128)S(1)} %copy-done.6, ...), custom_call_target="tpu_custom_call" | custom-call | tf_op jit(solution)/shard_map/project/pallas_call | solution.py:340
  36.5 1.3 %copy-done.7 = bf16[256,4096]{1,0:T(8,128)(2,1)} copy-done((bf16[256,4096]{1,0:T(8,128)(2,1)}, bf16[256,4096]{1,0:T(8,128)(2,1)S(1)}, u32[]{:S(2)}) %copy-start.7) | copy-done | bytes 2097176
  37.8 1.2 %copy-done.9 = bf16[192,4096]{1,0:T(8,128)(2,1)} copy-done((bf16[192,4096]{1,0:T(8,128)(2,1)}, bf16[192,4096]{1,0:T(8,128)(2,1)S(1)}, u32[]{:S(2)}) %copy-start.9) | copy-done | bytes 1572888
  39.0 4.2 %all-to-all-start.1 = ((f32[8,8,384]{2,1,0:T(8,128)}), f32[8,8,384]{2,1,0:T(8,128)S(1)}, u32[]{:S(2)}, u32[]{:S(2)}) async-start(f32[8,8,384]{2,1,0:T(8,128)} %bitcast.7), calls=%async_computation.1 | async-start | bytes 196608 | tf_op jit(solution)/shard_map/all_to_all | solution.py:313
  43.2 1.6 %copy-done.4 = bf16[4096,256]{1,0:T(8,128)(2,1)S(1)} copy-done((bf16[4096,256]{1,0:T(8,128)(2,1)S(1)}, bf16[4096,256]{1,0:T(8,128)(2,1)}, u32[]{:S(2)}) %copy-start.4) | copy-done | bytes 2097176
  44.8 1.6 %copy-done.8 = bf16[256,4096]{1,0:T(8,128)(2,1)S(1)} copy-done((bf16[256,4096]{1,0:T(8,128)(2,1)S(1)}, bf16[256,4096]{1,0:T(8,128)(2,1)}, u32[]{:S(2)}) %copy-start.8) | copy-done | bytes 2097176
  46.4 2.5 %own.1 = (f32[256,256]{1,0:T(8,128)S(1)}, f32[256,128]{1,0:T(8,128)S(1)}, f32[256,128]{1,0:T(8,128)S(1)}, f32[8,128]{1,0:T(8,128)S(1)}, f32[256,256]{1,0:T(8,128)S(1)}) custom-call(f32[2]{0:T(128)S(1)} %copy-done.22, bf16[256,4096]{1,0:T(8,128)(2,1)S(1)} %get-tuple-element.25.dense_ref, bf16[256,4096]{1,0:T(8,128)(2,1)S(1)} %copy-done.8, ...), custom_call_target="tpu_custom_call" | custom-call | tf_op jit(solution)/shard_map/own/pallas_call | solution.py:347
  50.4 2.1 %trace.1 = (f32[256,256]{1,0:T(8,128)}, f32[64,384]{1,0:T(8,128)S(1)}) custom-call(f32[2]{0:T(128)S(1)} %copy-done.22, f32[64,384]{1,0:T(8,128)S(1)} %bitcast.23, f32[256,256]{1,0:T(8,128)S(1)} %get-tuple-element.29.proj_ref, f32[256,128]{1,0:T(8,128)S(1)} %get-tuple-element.30.energy_ref, f32[256,128]{1,0:T(8,128)S(1)} %copy-done.19, ...), custom_call_target="tpu_custom_call" | custom-call | tf_op jit(solution)/shard_map/trace/pallas_call | solution.py:352
  52.5 9.2 %all_to_all.20 = f32[8,8,384]{2,1,0:T(8,128)S(1)} all-to-all(f32[8,8,384]{2,1,0:T(8,128)S(1)} %bitcast.28), channel_id=1, replica_groups=mesh['region'=4,'tile'=8] {'tile'}, dimensions={0} | all-to-all | bytes 196608 | tf_op jit(solution)/shard_map/all_to_all | solution.py:313
  61.7 3.6 %collective-permute-start.2 = (f32[8,128]{1,0:T(8,128)S(1)}, f32[8,128]{1,0:T(8,128)S(1)}, u32[]{:S(2)}, u32[]{:S(2)}) collective-permute-start(f32[8,128]{1,0:T(8,128)S(1)} %fusion.refs_0_), channel_id=1, source_target_pairs={{0,24},{8,0},{16,8},{24,16},{1,25},{9,1},{17,9},{25,17},{2,26},{10... | collective-permute-start | bytes 12296 | tf_op jit(solution)/shard_map/ppermute | solution.py:360
  65.3 1.0 %collective-permute-start = (f32[8,128]{1,0:T(8,128)S(1)}, f32[8,128]{1,0:T(8,128)S(1)}, u32[]{:S(2)}, u32[]{:S(2)}) collective-permute-start(f32[8,128]{1,0:T(8,128)S(1)} %fusion.refs_0_), channel_id=1, source_target_pairs={{0,8},{8,16},{16,24},{24,0},{1,9},{9,17},{17,25},{25,1},{2,10},{10... | collective-permute-start | bytes 12296 | tf_op jit(solution)/shard_map/ppermute | solution.py:360
  66.3 1.6 %copy-done.2 = bf16[256,4096]{1,0:T(8,128)(2,1)S(1)} copy-done((bf16[256,4096]{1,0:T(8,128)(2,1)S(1)}, bf16[256,4096]{1,0:T(8,128)(2,1)}, u32[]{:S(2)}) %copy-start.2) | copy-done | bytes 2097176
  67.9 1.4 %copy-done.10 = bf16[192,4096]{1,0:T(8,128)(2,1)S(1)} copy-done((bf16[192,4096]{1,0:T(8,128)(2,1)S(1)}, bf16[192,4096]{1,0:T(8,128)(2,1)}, u32[]{:S(2)}) %copy-start.10) | copy-done | bytes 1572888
  69.3 0.9 %copy-done.13 = f32[256,256]{1,0:T(8,128)S(1)} copy-done((f32[256,256]{1,0:T(8,128)S(1)}, f32[256,256]{1,0:T(8,128)}, u32[]{:S(2)}) %copy-start.13) | copy-done | bytes 262168
  70.3 2.6 %rest.1.refs_5_ = f32[256,4096]{1,0:T(8,128)S(1)} custom-call(f32[64,384]{1,0:T(8,128)S(1)} %bitcast.21, bf16[256,4096]{1,0:T(8,128)(2,1)S(1)} %copy-done.2, bf16[256,4096]{1,0:T(8,128)(2,1)S(1)} %get-tuple-element.25.dense_ref, bf16[192,4096]{1,0:T(8,128)(2,1)S(1)} %copy-done.10, f32[256,256]{1,0:T(8,128)S(1)} %copy-done.13), custom_call_target="tpu_custom_call" | custom-call | tf_op jit(solution)/shard_map/rest/pallas_call | solution.py:363
  72.9 3.3 %border.1 = (bf16[256,4096]{1,0:T(8,128)(2,1)S(1)}, f32[64,128]{1,0:T(8,128)}, f32[2,128]{1,0:T(2,128)}) custom-call(f32[64,512]{1,0:T(8,128)S(1)} %bitcast.19, f32[64,384]{1,0:T(8,128)S(1)} %bitcast.22, f32[8,128]{1,0:T(8,128)S(1)} %fusion.refs_0_, f32[8,128]{1,0:T(8,128)S(1)} %collective-permute-done.refs_1_, f32[8,128]{1,0:T(8,128)S(1)} %collective-permute-done.1.refs_2_, ...), custom_call_target="tpu_custom_call" | custom-call | tf_op jit(solution)/shard_map/border/pallas_call | solution.py:366
  76.2 3.3 %all-to-all-start.3 = ((f32[8,8,128]{2,1,0:T(8,128)}), f32[8,8,128]{2,1,0:T(8,128)S(1)}, u32[]{:S(2)}, u32[]{:S(2)}) async-start(f32[8,8,128]{2,1,0:T(8,128)} %bitcast.12), calls=%async_computation.3 | async-start | bytes 65536 | tf_op jit(solution)/shard_map/all_to_all | solution.py:313
  79.6 6.1 %footprint.1 = f32[256,128]{1,0:T(8,128)} custom-call(bf16[256,4096]{1,0:T(8,128)(2,1)S(1)} %get-tuple-element.38.resid_ref, f32[256,256]{1,0:T(8,128)S(1)} %copy-done.14, f32[256,128]{1,0:T(8,128)S(1)} %copy-done.12, s32[256,128]{1,0:T(8,128)S(1)} %copy-done.16), custom_call_target="tpu_custom_call" | custom-call | tf_op jit(solution)/shard_map/footprint/pallas_call | solution.py:373
  (51 shorter events, 7.9 us)
Async XLA Ops:
  0.6 27.0 %copy-start.23 = (f32[256]{0:T(256)S(1)}, f32[256]{0:T(256)}, u32[]{:S(2)}) copy-start(f32[256]{0:T(256)} %param.21) | copy-start | bytes 3076
  0.6 1.0 %copy-start.5 = (f32[256,256]{1,0:T(8,128)S(1)}, f32[256,256]{1,0:T(8,128)}, u32[]{:S(2)}) copy-start(f32[256,256]{1,0:T(8,128)} %old_ref.5) | copy-start | bytes 786436
  4.4 23.2 %copy-start.6 = (f32[256,256]{1,0:T(8,128)S(1)}, f32[256,256]{1,0:T(8,128)}, u32[]{:S(2)}) copy-start(f32[256,256]{1,0:T(8,128)} %old_ref.5) | copy-start | bytes 786436
  4.4 23.2 %copy-start.17 = (f32[4096]{0:T(1024)S(1)}, f32[4096]{0:T(1024)}, u32[]{:S(2)}) copy-start(f32[4096]{0:T(1024)} %param.20) | copy-start | bytes 49156
  5.4 22.2 %all-to-all-start = ((f32[8,8,512]{2,1,0:T(8,128)}), f32[8,8,512]{2,1,0:T(8,128)S(1)}, u32[]{:S(2)}, u32[]{:S(2)}) async-start(f32[8,8,512]{2,1,0:T(8,128)} %bitcast.3), calls=%async_computation | async-start | bytes 262144 | tf_op jit(solution)/shard_map/all_to_all | solution.py:313
  10.6 1.6 %copy-start.3 = (bf16[4096,256]{1,0:T(8,128)(2,1)S(1)}, bf16[4096,256]{1,0:T(8,128)(2,1)}, u32[]{:S(2)}) copy-start(bf16[4096,256]{1,0:T(8,128)(2,1)} %movie_ref.3) | copy-start | bytes 6291460
  26.2 1.4 %copy-start = (bf16[256,4096]{1,0:T(8,128)(2,1)}, bf16[256,4096]{1,0:T(8,128)(2,1)S(1)}, u32[]{:S(2)}) copy-start(bf16[256,4096]{1,0:T(8,128)(2,1)S(1)} %get-tuple-element.24.movie_t_ref) | copy-start | bytes 6291460
  27.6 1.6 %copy-start.1 = (bf16[256,4096]{1,0:T(8,128)(2,1)S(1)}, bf16[256,4096]{1,0:T(8,128)(2,1)}, u32[]{:S(2)}) copy-start(bf16[256,4096]{1,0:T(8,128)(2,1)} %copy-done) | copy-start | bytes 6291460
  29.2 14.0 %copy-start.12 = (f32[256,128]{1,0:T(8,128)S(1)}, f32[256,128]{1,0:T(8,128)}, u32[]{:S(2)}) copy-start(f32[256,128]{1,0:T(8,128)} %fp_ref.5) | copy-start | bytes 393220
  29.2 14.0 %copy-start.22 = (f32[2]{0:T(128)S(1)}, f32[2]{0:T(128)}, u32[]{:S(2)}) copy-start(f32[2]{0:T(128)} %ar_ref.3) | copy-start | bytes 28
  36.5 1.3 %copy-start.7 = (bf16[256,4096]{1,0:T(8,128)(2,1)}, bf16[256,4096]{1,0:T(8,128)(2,1)S(1)}, u32[]{:S(2)}) copy-start(bf16[256,4096]{1,0:T(8,128)(2,1)S(1)} %get-tuple-element.27.resid_ref) | copy-start | bytes 6291460
  37.8 1.2 %copy-start.9 = (bf16[192,4096]{1,0:T(8,128)(2,1)}, bf16[192,4096]{1,0:T(8,128)(2,1)S(1)}, u32[]{:S(2)}) copy-start(bf16[192,4096]{1,0:T(8,128)(2,1)S(1)} %get-tuple-element.37.dense_in_ref) | copy-start | bytes 4718596
  39.0 10.6 %all-to-all-start.1 = ((f32[8,8,384]{2,1,0:T(8,128)}), f32[8,8,384]{2,1,0:T(8,128)S(1)}, u32[]{:S(2)}, u32[]{:S(2)}) async-start(f32[8,8,384]{2,1,0:T(8,128)} %bitcast.7), calls=%async_computation.1 | async-start | bytes 196608 | tf_op jit(solution)/shard_map/all_to_all | solution.py:313
  43.2 1.6 %copy-start.4 = (bf16[4096,256]{1,0:T(8,128)(2,1)S(1)}, bf16[4096,256]{1,0:T(8,128)(2,1)}, u32[]{:S(2)}) copy-start(bf16[4096,256]{1,0:T(8,128)(2,1)} %movie_ref.3) | copy-start | bytes 6291460
  44.8 1.6 %copy-start.8 = (bf16[256,4096]{1,0:T(8,128)(2,1)S(1)}, bf16[256,4096]{1,0:T(8,128)(2,1)}, u32[]{:S(2)}) copy-start(bf16[256,4096]{1,0:T(8,128)(2,1)} %copy-done.7) | copy-start | bytes 6291460
  61.7 11.2 %collective-permute-start.2 = (f32[8,128]{1,0:T(8,128)S(1)}, f32[8,128]{1,0:T(8,128)S(1)}, u32[]{:S(2)}, u32[]{:S(2)}) collective-permute-start(f32[8,128]{1,0:T(8,128)S(1)} %fusion.refs_0_), channel_id=1, source_target_pairs={{0,24},{8,0},{16,8},{24,16},{1,25},{9,1},{17,9},{25,17},{2,26},{10... | collective-permute-start | bytes 12296 | tf_op jit(solution)/shard_map/ppermute | solution.py:360
  65.3 7.6 %collective-permute-start.1 = (f32[8,128]{1,0:T(8,128)S(1)}, f32[8,128]{1,0:T(8,128)S(1)}, u32[]{:S(2)}, u32[]{:S(2)}) collective-permute-start(f32[8,128]{1,0:T(8,128)S(1)} %fusion.refs_0_), channel_id=1, source_target_pairs={{0,16},{8,24},{16,0},{24,8},{1,17},{9,25},{17,1},{25,9},{2,18},{10... | collective-permute-start | bytes 12296 | tf_op jit(solution)/shard_map/ppermute | solution.py:360
  65.3 7.6 %collective-permute-start = (f32[8,128]{1,0:T(8,128)S(1)}, f32[8,128]{1,0:T(8,128)S(1)}, u32[]{:S(2)}, u32[]{:S(2)}) collective-permute-start(f32[8,128]{1,0:T(8,128)S(1)} %fusion.refs_0_), channel_id=1, source_target_pairs={{0,8},{8,16},{16,24},{24,0},{1,9},{9,17},{17,25},{25,1},{2,10},{10... | collective-permute-start | bytes 12296 | tf_op jit(solution)/shard_map/ppermute | solution.py:360
  66.3 1.6 %copy-start.2 = (bf16[256,4096]{1,0:T(8,128)(2,1)S(1)}, bf16[256,4096]{1,0:T(8,128)(2,1)}, u32[]{:S(2)}) copy-start(bf16[256,4096]{1,0:T(8,128)(2,1)} %copy-done) | copy-start | bytes 6291460
  67.9 1.4 %copy-start.10 = (bf16[192,4096]{1,0:T(8,128)(2,1)S(1)}, bf16[192,4096]{1,0:T(8,128)(2,1)}, u32[]{:S(2)}) copy-start(bf16[192,4096]{1,0:T(8,128)(2,1)} %copy-done.9) | copy-start | bytes 4718596
  69.3 0.9 %copy-start.13 = (f32[256,256]{1,0:T(8,128)S(1)}, f32[256,256]{1,0:T(8,128)}, u32[]{:S(2)}) copy-start(f32[256,256]{1,0:T(8,128)} %get-tuple-element.19.new_ref) | copy-start | bytes 786436
  72.9 6.7 %copy-start.14 = (f32[256,256]{1,0:T(8,128)S(1)}, f32[256,256]{1,0:T(8,128)}, u32[]{:S(2)}) copy-start(f32[256,256]{1,0:T(8,128)} %get-tuple-element.19.new_ref) | copy-start | bytes 786436
  72.9 6.7 %copy-start.16 = (s32[256,128]{1,0:T(8,128)S(1)}, s32[256,128]{1,0:T(8,128)}, u32[]{:S(2)}) copy-start(s32[256,128]{1,0:T(8,128)} %idx_ref.3) | copy-start | bytes 393220
  76.2 9.5 %all-to-all-start.3 = ((f32[8,8,128]{2,1,0:T(8,128)}), f32[8,8,128]{2,1,0:T(8,128)S(1)}, u32[]{:S(2)}, u32[]{:S(2)}) async-start(f32[8,8,128]{2,1,0:T(8,128)} %bitcast.12), calls=%async_computation.3 | async-start | bytes 65536 | tf_op jit(solution)/shard_map/all_to_all | solution.py:313
  (8 other events, 6.2 us)

commit v2 on v1

v2 whole, which is shorter than its diff:
```python
import jax
import jax.numpy as jnp
from jax import lax
from jax.experimental import pallas as pl
from jax.experimental.pallas import tpu as pltpu
from jax.sharding import PartitionSpec as P

CAP = 8
RIDGE = 1.0
LANES = 128
F32 = jnp.float32
BF16 = jnp.bfloat16
VMEM_BYTES = 40 << 20
CHUNK = 2048
TURN = 512
UNROLL = 64
PAD = 8


def nn(a, b):
    return lax.dot_general(a, b, (((1,), (0,)), ((), ())), preferred_element_type=F32)


def nt(a, b):
    return lax.dot_general(a, b, (((1,), (1,)), ((), ())), preferred_element_type=F32)


def split(x, terms):
    parts = []
    for _ in range(terms):
        part = x.astype(BF16)
        parts.append(part)
        x = x - part.astype(F32)
    return parts


def stack(table, terms=3):
    return jnp.concatenate([table] * terms, axis=1)


def select_rows(table, x, terms=3):
    return nn(stack(table, terms), jnp.concatenate(split(x, terms), axis=0))


def iota(shape, dim):
    return lax.broadcasted_iota(jnp.int32, shape, dim)


def to_column(row):
    n = row.shape[1]
    return jnp.sum(jnp.where(iota((n, n), 0) == iota((n, n), 1), row, jnp.zeros_like(row)), axis=1, keepdims=True)


def to_row(column):
    n = column.shape[0]
    return jnp.sum(jnp.where(iota((n, n), 0) == iota((n, n), 1), column, jnp.zeros_like(column)), axis=0, keepdims=True)


def shift_lanes(x, count):
    return jnp.where(iota(x.shape, len(x.shape) - 1) >= count, pltpu.roll(x, count, len(x.shape) - 1), 0.0)


def pieces(width):
    return [slice(start, start + CHUNK) for start in range(0, width, CHUNK)]


def fetch(source, target, sem):
    copy = pltpu.make_async_copy(source, target, sem)
    copy.start()
    return copy


def fetch_columns(*copies):
    return [
        [fetch(source.at[:, here], target.at[:, here], sems.at[k]) for source, target, sems in copies]
        for k, here in enumerate(pieces(copies[0][0].shape[1]))
    ]


def pack_kernel(tile_ref, bfp_hbm, bidx_hbm, bown_hbm, boff_hbm, old_hbm, send_ref, pick_ref, pick_t_ref, place_ref,
                bfp_ref, bidx_ref, bown_ref, boff_ref, old_ref, sems):
    copies = [
        fetch(source, target, sems.at[k])
        for k, (source, target) in enumerate(
            ((boff_hbm, boff_ref), (bown_hbm, bown_ref), (bfp_hbm, bfp_ref), (bidx_hbm, bidx_ref), (old_hbm, old_ref))
        )
    ]
    slots = send_ref.shape[0]
    tiles = slots // CAP
    border, support = bfp_ref.shape
    owned = old_ref.shape[0]
    copies[0].wait()
    copies[1].wait()
    target = boff_ref[...] + (tile_ref[0] + 1)
    target = jnp.where(target >= tiles, target - tiles, target)
    target_col = to_column(target)
    same = target_col == target
    before = iota((border, border), 0) < iota((border, border), 1)
    rank = jnp.sum(jnp.where(jnp.logical_and(same, before), 1, 0), axis=0, keepdims=True)
    slot = target * CAP + rank
    owner = bown_ref[...]
    place_t = iota((slots, border), 0) == slot
    place = iota((border, slots), 1) == to_column(slot)
    owner_col = jnp.sum(jnp.where(place_t, owner + 1, 0), axis=1, keepdims=True) - 1
    owner_row = jnp.sum(jnp.where(place, to_column(owner) + 1, 0), axis=0, keepdims=True) - 1
    pick = jnp.where(iota((slots, owned), 1) == owner_col, 1.0, 0.0).astype(BF16)
    pick_ref[...] = pick
    pick_t_ref[...] = jnp.where(iota((owned, slots), 0) == owner_row, 1.0, 0.0).astype(BF16)
    place_ref[...] = jnp.where(place, 1.0, 0.0).astype(BF16)
    place_t = jnp.where(place_t, 1.0, 0.0).astype(BF16)
    copies[2].wait()
    send_ref[:, :support] = select_rows(place_t, bfp_ref[...])
    copies[3].wait()
    send_ref[:, support:2 * support] = select_rows(place_t, bidx_ref[...].astype(F32), 2)
    copies[4].wait()
    send_ref[:, 2 * support:] = select_rows(pick, old_ref[...])


def scatter_rows(values_ref, index_ref, grid_ref, rows, stride, first=0):
    cells = grid_ref.shape[0] // stride
    support = values_ref.shape[1]
    hi_range = iota((cells, support), 0).astype(BF16)
    lo_range = iota((LANES, support), 0).astype(BF16)
    zero = jnp.zeros((cells, support), BF16)
    none = jnp.zeros((LANES, support), BF16)
    one = jnp.ones((LANES, support), BF16)

    def factors(row):
        index = index_ref[pl.ds(row, 1), :]
        value = values_ref[pl.ds(row, 1), :]
        high = jnp.broadcast_to((index >> 7).astype(F32), (cells, support)).astype(BF16)
        low = jnp.broadcast_to((index & 127).astype(F32), (LANES, support)).astype(BF16)
        coarse = value.astype(BF16).astype(F32)
        top = jnp.broadcast_to(coarse, (cells, support)).astype(BF16)
        rest = jnp.broadcast_to(value - coarse, (cells, support)).astype(BF16)
        hit = high == hi_range
        return jnp.where(hit, top, zero), jnp.where(hit, rest, zero), jnp.where(low == lo_range, one, none)

    for k in range(0, rows, 2):
        row = first + k
        top, rest, right = factors(row)
        top_next, rest_next, right_next = factors(row + 1)
        left = jnp.concatenate([
            jnp.concatenate([top, rest, zero, zero], axis=0),
            jnp.concatenate([zero, zero, top_next, rest_next], axis=0),
        ], axis=1)
        made = nt(left, jnp.concatenate([right, right_next], axis=1))
        grid_ref[pl.ds(k, cells, stride=stride), :] = made[:cells] + made[cells:2 * cells]
        grid_ref[pl.ds(k + 1, cells, stride=stride), :] = made[2 * cells:3 * cells] + made[3 * cells:]


def prepare_kernel(movie_hbm, fp_hbm, idx_hbm, dense_hbm, movie_t_hbm,
                   movie_ref, fp_ref, idx_ref, dense_ref, movie_t_ref, grid_ref, in_sems, movie_sems, dense_sems, out_sems):
    owned = fp_hbm.shape[0]
    voxels, frames = movie_hbm.shape
    groups = movie_sems.shape[0]
    rows = owned // groups
    width = voxels // groups
    stride = grid_ref.shape[0] // (voxels // LANES)
    loads = [fetch(fp_hbm, fp_ref, in_sems.at[0]), fetch(idx_hbm, idx_ref, in_sems.at[1])]
    for group in range(groups):
        fetch(movie_hbm.at[group * width:(group + 1) * width], movie_ref.at[group * width:(group + 1) * width], movie_sems.at[group])
    eye = jnp.where(iota((frames, frames), 0) == iota((frames, frames), 1), 1.0, 0.0).astype(BF16)
    for copy in loads:
        copy.wait()

    def parts(group):
        return pl.ds(pl.multiple_of(group * rows, rows), rows), pl.ds(pl.multiple_of(group * width, width), width)

    @pl.loop(0, groups)
    def _(group):
        mine, wide = parts(group)
        first = pl.multiple_of(group * rows, rows)
        scatter_rows(fp_ref, idx_ref, grid_ref, rows, stride, first)
        pltpu.make_async_copy(movie_hbm.at[wide], movie_ref.at[wide], movie_sems.at[group]).wait()
        for k in range(width // TURN):
            here = pl.ds(pl.multiple_of(group * width + k * TURN, TURN), TURN)
            movie_t_ref[:, here] = nt(eye, movie_ref[here, :]).astype(BF16)
        for cell in range(voxels // LANES):
            dense_ref[mine, cell * LANES:(cell + 1) * LANES] = grid_ref[cell * stride:cell * stride + rows, :].astype(BF16)
        fetch(dense_ref.at[mine], dense_hbm.at[mine], dense_sems.at[group])
        fetch(movie_t_ref.at[:, wide], movie_t_hbm.at[:, wide], out_sems.at[group])

    for group in range(groups):
        mine, wide = slice(group * rows, (group + 1) * rows), slice(group * width, (group + 1) * width)
        pltpu.make_async_copy(dense_ref.at[mine], dense_hbm.at[mine], dense_sems.at[group]).wait()
        pltpu.make_async_copy(movie_t_ref.at[:, wide], movie_t_hbm.at[:, wide], out_sems.at[group]).wait()


def transposed_parts(x):
    return jnp.concatenate([jnp.transpose(part.astype(F32)).astype(BF16) for part in split(x, 3)], axis=1)


def project_kernel(recv_ref, movie_t_hbm, dense_hbm, old_hbm, spatial_hbm, trace_hbm, resid_hbm, dense_in_hbm, proj_ref, weight_ref, base_ref,
                   movie_t_ref, dense_ref, old_ref, spatial_ref, trace_ref, resid_ref, values_ref, idx_ref,
                   grid_ref, in_sems, movie_sems, dense_sems, resid_sems, out_sem):
    slots = recv_ref.shape[0]
    owned = dense_hbm.shape[0]
    frames, voxels = movie_t_hbm.shape
    support = values_ref.shape[1]
    stride = slots + PAD
    first = [fetch(spatial_hbm, spatial_ref, in_sems.at[1]), fetch(old_hbm, old_ref, in_sems.at[0]), fetch(trace_hbm, trace_ref, in_sems.at[2])]
    loads = fetch_columns((dense_hbm, dense_ref.at[:owned], dense_sems), (movie_t_hbm, movie_t_ref, movie_sems))
    values_ref[...] = recv_ref[:, :support]
    idx_ref[...] = recv_ref[:, support:2 * support].astype(jnp.int32)
    scatter_rows(values_ref, idx_ref, grid_ref, slots, stride)
    for copy in first:
        copy.wait()
    both_t = jnp.concatenate([jnp.transpose(old_ref[...]).astype(BF16), transposed_parts(recv_ref[:, 2 * support:])], axis=1)
    back = to_column(trace_ref[...])
    seen_in = jnp.zeros((slots, LANES), F32)
    for cell in range(voxels // LANES):
        at = cell * LANES
        part = grid_ref[cell * stride:cell * stride + slots, :].astype(BF16)
        for copy in range(3):
            dense_ref[owned + copy * slots:owned + (copy + 1) * slots, at:at + LANES] = part
        seen_in += part.astype(F32) * spatial_ref[:, at:at + LANES]
    mine = dense_ref.at[owned:owned + slots]
    stores = [fetch(mine, dense_in_hbm, out_sem)]
    seen = jnp.zeros((frames, LANES), F32)
    weight = jnp.zeros((owned, LANES), F32)
    for k, here in enumerate(pieces(voxels)):
        for copy in loads[k]:
            copy.wait()
        recon = nn(both_t, dense_ref[:, here]) + back * spatial_ref[:, here]
        resid_ref[:, here] = (movie_t_ref[:, here].astype(F32) - recon).astype(BF16)
        for at in range(here.start, here.stop, LANES):
            profile = spatial_ref[:, at:at + LANES]
            seen += movie_t_ref[:, at:at + LANES].astype(F32) * profile
            weight += dense_ref[:owned, at:at + LANES].astype(F32) * profile
        stores.append(fetch(resid_ref.at[:, here], resid_hbm.at[:, here], resid_sems.at[k]))
    proj_ref[:, :frames] = nt(mine[...], resid_ref[...])
    proj_ref[:, frames:] = jnp.broadcast_to(jnp.sum(seen_in, axis=1, keepdims=True), (slots, LANES))
    weight_ref[...] = jnp.broadcast_to(jnp.sum(weight, axis=1, keepdims=True), (owned, LANES))
    seen = to_row(jnp.sum(seen, axis=1, keepdims=True))
    norm = jnp.sum(spatial_ref[...] * spatial_ref[...], axis=1, keepdims=True)
    row = iota((8, LANES), 0)
    base_ref[...] = jnp.where(row == 0, seen[:, :LANES], jnp.where(row == 1, seen[:, LANES:], jnp.where(row == 2, norm, 0.0)))
    for copy in stores:
        copy.wait()


def own_kernel(ar_ref, dense_hbm, resid_hbm, fp_hbm, old_hbm, send_ref, pick_t_ref, start_ref, scale_ref, impulse_ref,
               dense_ref, resid_ref, fp_ref, old_ref, in_sems):
    frames, voxels = resid_hbm.shape
    owned, support = fp_hbm.shape
    first = [fetch(fp_hbm, fp_ref, in_sems.at[0]), fetch(old_hbm, old_ref, in_sems.at[1])]
    dense_load = fetch(dense_hbm, dense_ref, in_sems.at[2])
    resid_load = fetch(resid_hbm, resid_ref, in_sems.at[3])
    near, far = ar_ref[0], ar_ref[1]
    response = jnp.where(iota((8, frames), 1) == 0, 1.0, 0.0)
    step = 1
    while step < frames:
        change = near * shift_lanes(response, step)
        if 2 * step < frames:
            change = change - far * shift_lanes(response, 2 * step)
        response = response + change
        near, far = near * near + 2.0 * far, -far * far
        step *= 2
    wide = jnp.broadcast_to(response[0:1], (frames, frames))
    wide = pltpu.roll(wide, 0, 1, stride=1, stride_axis=0)
    high, mid, low = split(jnp.where(iota((frames, frames), 1) >= iota((frames, frames), 0), wide, 0.0), 3)
    impulse_ref[...] = jnp.concatenate([high, mid, low, high, mid, high], axis=0)
    for copy in first:
        copy.wait()
    border_fp = send_ref[:, :support]
    square = jnp.broadcast_to(jnp.sum(border_fp * border_fp, axis=1, keepdims=True), (send_ref.shape[0], LANES))
    fp = fp_ref[...]
    share = 1.0 / (jnp.sum(fp * fp, axis=1, keepdims=True) + select_rows(pick_t_ref[...], square)[:, 0:1])
    scale_ref[...] = jnp.broadcast_to(share, (owned, LANES))
    dense_load.wait()
    resid_load.wait()
    start_ref[...] = old_ref[...] + nt(dense_ref[...], resid_ref[...]) * share


def trace_kernel(ar_ref, back_ref, start_ref, scale_ref, weight_ref, base_ref, impulse_ref, pick_ref, pick_t_ref, new_ref, send_ref):
    frames = start_ref.shape[1]
    returned = select_rows(pick_t_ref[...], back_ref[...])
    raw = start_ref[...] + returned[:, :frames] * scale_ref[:, 0:1]
    spikes = jnp.maximum(raw - ar_ref[0] * shift_lanes(raw, 1) - ar_ref[1] * shift_lanes(raw, 2), 0.0)
    high, mid, low = split(spikes, 3)
    new = nn(jnp.concatenate([high, high, high, mid, mid, low], axis=1), impulse_ref[...])
    new_ref[...] = new
    send_ref[:, :frames] = select_rows(pick_ref[...], new)
    used = weight_ref[:, 0:1] * new.astype(BF16).astype(F32) + returned[:, frames:frames + 1] * new
    used = jnp.sum(used, axis=0, keepdims=True)
    base = base_ref[...]
    row = iota((8, LANES), 0)
    base = base - jnp.where(row == 0, used[:, :LANES], jnp.where(row == 1, used[:, LANES:], 0.0))
    for tile in range(send_ref.shape[0] // CAP):
        send_ref[tile * CAP:(tile + 1) * CAP, frames:] = base


def rest_own_kernel(movie_t_hbm, dense_hbm, new_hbm, rest_hbm, movie_t_ref, dense_ref, new_ref, rest_ref, sem, movie_sems, dense_sems, out_sems):
    voxels = movie_t_hbm.shape[1]
    load = fetch(new_hbm, new_ref, sem)
    loads = fetch_columns((dense_hbm, dense_ref, dense_sems), (movie_t_hbm, movie_t_ref, movie_sems))
    load.wait()
    new_t = jnp.transpose(new_ref[...]).astype(BF16)
    stores = []
    for k, here in enumerate(pieces(voxels)):
        for copy in loads[k]:
            copy.wait()
        rest_ref[:, here] = movie_t_ref[:, here].astype(F32) - nn(new_t, dense_ref[:, here])
        stores.append(fetch(rest_ref.at[:, here], rest_hbm.at[:, here], out_sems.at[k]))
    for copy in stores:
        copy.wait()


def pick_support(grad_ref, idx_ref, out, rows):
    cells = grad_ref.shape[1] // LANES

    @pl.loop(0, rows // 64)
    def _(group):
        for k in range(8):
            here = pl.ds(pl.multiple_of(group * 64 + k * 8, 8), 8)
            index = idx_ref[here, :]
            high = index >> 7
            low = index & 127
            picked = jnp.zeros(index.shape, F32)
            for cell in range(cells):
                found = jnp.take_along_axis(grad_ref[here, cell * LANES:(cell + 1) * LANES], low, axis=1, mode="promise_in_bounds")
                picked = jnp.where(high == cell, found, picked)
            out(here, picked)


def rest_in_kernel(recv_ref, own_hbm, dense_in_hbm, rest_ref, own_ref, dense_in_ref, own_sems, *in_sems):
    slots = recv_ref.shape[0]
    frames, voxels = own_hbm.shape
    loads = fetch_columns(
        (own_hbm, own_ref, own_sems),
        *[(dense_in_hbm, dense_in_ref.at[copy * slots:(copy + 1) * slots], sems) for copy, sems in enumerate(in_sems)],
    )
    in_t = transposed_parts(recv_ref[:, :frames])
    for k, here in enumerate(pieces(voxels)):
        for copy in loads[k]:
            copy.wait()
        rest_ref[:, here] = own_ref[:, here] - nn(in_t, dense_in_ref[:, here])


def border_kernel(recv0_ref, recv_ref, *refs):
    *totals, spatial_hbm, rest_ref, resid_ref, next_ref, back_ref, spatial_ref, grad_ref, idx_ref, denom_ref, sem = refs
    frames, voxels = rest_ref.shape
    slots, support = next_ref.shape
    load = fetch(spatial_hbm, spatial_ref, sem)
    total = totals[0][...]
    for other in totals[1:]:
        total = total + other[...]
    back = total[0:2] / total[2:3, 0:1]
    back_ref[...] = back
    back = to_column(jnp.concatenate([back[0:1], back[1:2]], axis=1))
    new = recv_ref[:, :frames]
    idx_ref[...] = recv0_ref[:, support:2 * support].astype(jnp.int32)
    denom_ref[...] = jnp.broadcast_to(jnp.sum(new * new, axis=1, keepdims=True) + RIDGE, (slots, support))
    new_low = new.astype(BF16)
    load.wait()
    for here in pieces(voxels):
        resid = (rest_ref[:, here] - back * spatial_ref[:, here]).astype(BF16)
        resid_ref[:, here] = resid
        grad_ref[:, here] = nn(new_low, resid)

    def out(here, picked):
        next_ref[here, :] = jnp.maximum(recv0_ref[here, :support] + picked / denom_ref[here, :], 0.0)

    pick_support(grad_ref, idx_ref, out, slots)


def footprint_kernel(resid_ref, new_ref, fp_hbm, idx_hbm, out_ref, fp_ref, idx_ref, grad_ref, denom_ref, sems):
    frames, voxels = resid_ref.shape
    owned, support = fp_ref.shape
    first = [fetch(fp_hbm, fp_ref, sems.at[0]), fetch(idx_hbm, idx_ref, sems.at[1])]
    new = new_ref[...]
    new_low = new.astype(BF16)
    denom_ref[...] = jnp.broadcast_to(jnp.sum(new * new, axis=1, keepdims=True) + RIDGE, (owned, support))
    for here in pieces(voxels):
        grad_ref[:, here] = nn(new_low, resid_ref[:, here])
    for copy in first:
        copy.wait()

    def out(here, picked):
        out_ref[here, :] = jnp.maximum(fp_ref[here, :] + picked / denom_ref[here, :], 0.0)

    pick_support(grad_ref, idx_ref, out, owned)


def unpack_kernel(place_ref, rows_ref, out_ref):
    out_ref[...] = select_rows(place_ref[...], rows_ref[...])


def call(kernel, name, micros, ins, outs, scratch, *args):
    space = {"s": pltpu.SMEM, "v": pltpu.VMEM, "h": pltpu.HBM}
    shapes = [pltpu.HBM(shape, dtype) if where == "h" else jax.ShapeDtypeStruct(shape, dtype) for where, shape, dtype in outs]
    args = [pltpu.with_memory_space_constraint(arg, pltpu.HBM) if where == "h" else arg for where, arg in zip(ins, args)]
    places = [pl.BlockSpec(memory_space=space[where]) for where, _, _ in outs]
    many = len(outs) > 1
    return pl.pallas_call(
        kernel,
        out_shape=shapes if many else shapes[0],
        in_specs=[pl.BlockSpec(memory_space=space[where]) for where in ins],
        out_specs=places if many else places[0],
        scratch_shapes=list(scratch),
        cost_estimate=pl.CostEstimate(flops=0, bytes_accessed=int(micros * 3.5e6), transcendentals=0),
        compiler_params=pltpu.CompilerParams(vmem_limit_bytes=VMEM_BYTES),
        name=name,
    )(*args)


def exchange(rows, tiles):
    width = rows.shape[1]
    moved = lax.all_to_all(rows.reshape(tiles, CAP, width), "tile", split_axis=0, concat_axis=0, tiled=True)
    return moved.reshape(tiles * CAP, width)


def body(movie, footprint, support_idx, trace_old, ar_coef, border_fp, border_idx, border_owner, border_offset, back_spatial, back_trace):
    tiles = lax.axis_size("tile")
    regions = lax.axis_size("region")
    tile = lax.axis_index("tile").astype(jnp.int32).reshape(1)
    voxels, frames = movie.shape
    owned, support = footprint.shape
    border = border_fp.shape[0]
    slots = tiles * CAP
    cells = voxels // LANES
    spatial = back_spatial.reshape(1, voxels)
    V, dma, i32 = pltpu.VMEM, pltpu.SemaphoreType.DMA, jnp.int32
    n = voxels // CHUNK
    groups = owned // UNROLL
    wide = frames + LANES

    send, pick, pick_t, place = call(
        pack_kernel, "pack", 2, "shhhhh",
        [("v", (slots, 2 * support + frames), F32), ("v", (slots, owned), BF16), ("v", (owned, slots), BF16), ("v", (border, slots), BF16)],
        [V((border, support), F32), V((border, support), i32), V((1, border), i32), V((1, border), i32), V((owned, frames), F32), dma((5,))],
        tile, border_fp, border_idx, border_owner.reshape(1, border), border_offset.reshape(1, border), trace_old,
    )
    recv = exchange(send, tiles)
    dense, movie_t = call(
        prepare_kernel, "prepare", 7, "hhh",
        [("h", (owned, voxels), BF16), ("h", (frames, voxels), BF16)],
        [V((voxels, frames), BF16), V((owned, support), F32), V((owned, support), i32), V((owned, voxels), BF16), V((frames, voxels), BF16),
         V((cells * (UNROLL + PAD), LANES), F32), dma((2,)), dma((groups,)), dma((groups,)), dma((groups,))],
        movie, footprint, support_idx,
    )
    resid, dense_in, proj_in, weight, base = call(
        project_kernel, "project", 5, "vhhhhh",
        [("h", (frames, voxels), BF16), ("h", (slots, voxels), BF16), ("v", (slots, wide), F32), ("v", (owned, LANES), F32), ("v", (8, LANES), F32)],
        [V((frames, voxels), BF16), V((owned + 3 * slots, voxels), BF16), V((owned, frames), F32), V((1, voxels), F32), V((1, frames), F32),
         V((frames, voxels), BF16), V((slots, support), F32), V((slots, support), i32),
         V((cells * (slots + PAD), LANES), F32), dma((3,)), dma((n,)), dma((n,)), dma((n,)), dma],
        recv, movie_t, dense, trace_old, spatial, back_trace.reshape(1, frames),
    )
    returned = exchange(proj_in, tiles)
    start, scale, impulse = call(
        own_kernel, "own", 4, "shhhhvv",
        [("v", (owned, frames), F32), ("v", (owned, LANES), F32), ("v", (6 * frames, frames), BF16)],
        [V((owned, voxels), BF16), V((frames, voxels), BF16), V((owned, support), F32), V((owned, frames), F32), dma((4,))],
        ar_coef, dense, resid, footprint, trace_old, send, pick_t,
    )
    trace_new, send_new = call(
        trace_kernel, "trace", 2, "svvvvvvvv",
        [("v", (owned, frames), F32), ("v", (slots, wide), F32)], [],
        ar_coef, returned, start, scale, weight, base, impulse, pick, pick_t,
    )
    recv_new = exchange(send_new, tiles)
    rest_own = call(
        rest_own_kernel, "rest_own", 4, "hhh", [("h", (frames, voxels), F32)],
        [V((frames, voxels), BF16), V((owned, voxels), BF16), V((owned, frames), F32), V((frames, voxels), F32), dma, dma((n,)), dma((n,)), dma((n,))],
        movie_t, dense, trace_new,
    )
    recv_new, rest_own = lax.optimization_barrier((recv_new, rest_own))
    total = jnp.sum(recv_new[:, frames:].reshape(tiles, CAP, LANES), axis=0)
    totals = [total] + [
        lax.ppermute(total, "region", [(i, (i + shift) % regions) for i in range(regions)])
        for shift in range(1, regions)
    ]
    rest = call(
        rest_in_kernel, "rest_in", 4, "vhh", [("v", (frames, voxels), F32)],
        [V((frames, voxels), F32), V((3 * slots, voxels), BF16), dma((n,)), dma((n,)), dma((n,)), dma((n,))],
        recv_new, rest_own, dense_in,
    )
    resid2, in_next, back = call(
        border_kernel, "border", 3, "vv" + "v" * regions + "hv",
        [("v", (frames, voxels), BF16), ("v", (slots, support), F32), ("v", (2, LANES), F32)],
        [V((1, voxels), F32), V((slots, voxels), F32), V((slots, support), i32), V((slots, support), F32), dma],
        recv, recv_new, *totals, spatial, rest,
    )
    back_rows = exchange(in_next, tiles)
    footprint_new = call(
        footprint_kernel, "footprint", 4, "vvhh", [("v", (owned, support), F32)],
        [V((owned, support), F32), V((owned, support), i32), V((owned, voxels), F32), V((owned, support), F32), dma((2,))],
        resid2, trace_new, footprint, support_idx,
    )
    border_new = call(unpack_kernel, "unpack", 1, "vv", [("v", (border, support), F32)], [], place, back_rows)
    return (trace_new, footprint_new, border_new, back.reshape(frames))


def solution(mesh):
    row = P(("region", "tile"), None)
    flat = P(("region", "tile"))
    return jax.shard_map(
        body,
        mesh=mesh,
        in_specs=(row, row, row, row, P(), row, row, flat, row, flat, P()),
        out_specs=(row, row, row, P()),
        check_vma=False,
    )
```

time: 87.5 us -> 63.2 us (0.72)
  local copies, waits for them, and re-layouts: 21.3 us -> 0.01 us
  blocking collectives: 9.17 us -> 0 us
  waiting for transfers between devices: 0.02 us -> 4 us
  starting transfers between devices: 17.3 us -> 20.9 us
  Pallas kernels: 37.9 us -> 36.9 us
    unnamed x52 -> x4, local copies, waits for them, and re-layouts: 21.3 us -> 0.01 us
    all_to_all x1 -> x0, blocking collectives: 9.17 us -> none  [exchange(): lax.all_to_all(rows.reshape(tiles, CAP, width), 'tile', split_axis=0, con...]
    all_to_all x3 -> x4, starting transfers between devices: 12.7 us -> 16.3 us  [exchange(): lax.all_to_all(rows.reshape(tiles, CAP, width), 'tile', split_axis=0, con...]
    all_to_all x3 -> x4, waiting for transfers between devices: 0.01 us -> 2.77 us  [exchange(): lax.all_to_all(rows.reshape(tiles, CAP, width), 'tile', split_axis=0, con...]
    ppermute x3, waiting for transfers between devices: 0.01 us -> 1.23 us  [body(): lax.ppermute(total, 'region', [(i, (i + shift) % regions) for i in range(...]
    pallas_call x9 -> x10, Pallas kernels: 37.9 us -> 36.9 us  [call(): pl.pallas_call(kernel, out_shape=shapes if many else shapes[0], in_specs=...]
  transfers between devices with their start and end apart: 6 -> 7, of which waited for: 0 -> 5; matrix products, arithmetic and copies ran while one was open for 0% -> 0% of each run, Pallas kernels for 27% -> 36%
where the time goes in v2:
time: 63.2 us; the launch traced here: 62.5 us
  Pallas kernels  36.9 us (58%)
  starting transfers between devices  20.9 us (33%)
  waiting for transfers between devices  4 us (6%)
  between operations  0.76 us (1%)
    pallas_call x10, Pallas kernels, call(): pl.pallas_call(kernel, out_shape=shapes if many else shapes[0], in_specs=...  36.9 us
    all_to_all x4, starting transfers between devices, exchange(): lax.all_to_all(rows.reshape(tiles, CAP, width), 'tile', split_axis=0, con...  16.3 us
    ppermute x3, starting transfers between devices, body(): lax.ppermute(total, 'region', [(i, (i + shift) % regions) for i in range(...  4.6 us
    all_to_all x4, waiting for transfers between devices, exchange(): lax.all_to_all(rows.reshape(tiles, CAP, width), 'tile', split_axis=0, con...  2.77 us
  transfers between devices with their start and end apart: 7, of which 5 were waited for; matrix products, arithmetic and copies ran while one was open for 0% of the time, Pallas kernels for 36%

profile of v2, /device:TPU:0, one launch (start us, length us, event | category | flops | bytes accessed | tf_op | source)
XLA Modules:
  0.0 62.5 jit_solution(9051273925587971300)
XLA Ops:
  0.6 2.2 %pack.1 = (f32[64,512]{1,0:T(8,128)}, bf16[64,256]{1,0:T(8,128)(2,1)S(1)}, bf16[256,64]{1,0:T(8,128)(2,1)S(1)}, bf16[48,64]{1,0:T(8,128)(2,1)S(1)}) custom-call(s32[1]{0:T(128)} %bitcast.tile_ref, f32[48,128]{1,0:T(8,128)} %bfp_hbm.1, s32[48,128]{1,0:T(8,128)} %bidx_hbm.1, s32[1,48]{1,0:T(1,128)} %bitcast.26, s32[1,48]{1,0:T(1,128)} %bitcast.27, ...), custom_call_target="tpu_custom_call" | custom-call | bytes 7000000 | tf_op jit(solution)/shard_map/pack/pallas_call | solution.py:396
  2.8 5.2 %all-to-all-start = ((f32[8,8,512]{2,1,0:T(8,128)}), f32[8,8,512]{2,1,0:T(8,128)S(1)}, u32[]{:S(2)}, u32[]{:S(2)}) async-start(f32[8,8,512]{2,1,0:T(8,128)} %bitcast.3), calls=%async_computation | async-start | bytes 262144 | tf_op jit(solution)/shard_map/all_to_all | solution.py:410
  8.0 7.0 %prepare.1 = (bf16[256,4096]{1,0:T(8,128)(2,1)}, bf16[256,4096]{1,0:T(8,128)(2,1)}) custom-call(bf16[4096,256]{1,0:T(8,128)(2,1)} %movie_hbm.1, f32[256,128]{1,0:T(8,128)} %fp_hbm.5, s32[256,128]{1,0:T(8,128)} %idx_hbm.3), custom_call_target="tpu_custom_call" | custom-call | bytes 24500000 | tf_op jit(solution)/shard_map/prepare/pallas_call | solution.py:396
  15.0 0.0 all-to-all-done
  15.0 0.0 copy-start.1
  15.0 7.2 %project.1 = (bf16[256,4096]{1,0:T(8,128)(2,1)}, bf16[64,4096]{1,0:T(8,128)(2,1)}, f32[64,384]{1,0:T(8,128)}, f32[256,128]{1,0:T(8,128)S(1)}, f32[8,128]{1,0:T(8,128)S(1)}) custom-call(f32[64,512]{1,0:T(8,128)S(1)} %bitcast.16, bf16[256,4096]{1,0:T(8,128)(2,1)} %get-tuple-element.26.movie_t_hbm, bf16[256,4096]{1,0:T(8,128)(2,1)} %get-tuple-element.27.dense_hbm, ...), custom_call_target="tpu_custom_call" | custom-call | bytes 17500000 | tf_op jit(solution)/shard_map/project/pallas_call | solution.py:396
  22.2 4.2 %all-to-all-start.1 = ((f32[8,8,384]{2,1,0:T(8,128)}), f32[8,8,384]{2,1,0:T(8,128)S(1)}, u32[]{:S(2)}, u32[]{:S(2)}) async-start(f32[8,8,384]{2,1,0:T(8,128)} %bitcast.7), calls=%async_computation.1 | async-start | bytes 196608 | tf_op jit(solution)/shard_map/all_to_all | solution.py:410
  26.4 4.5 %own.1 = (f32[256,256]{1,0:T(8,128)S(1)}, f32[256,128]{1,0:T(8,128)S(1)}, bf16[1536,256]{1,0:T(8,128)(2,1)S(1)}) custom-call(f32[2]{0:T(128)S(1)} %copy-done.1, bf16[256,4096]{1,0:T(8,128)(2,1)} %get-tuple-element.27.dense_hbm, bf16[256,4096]{1,0:T(8,128)(2,1)} %get-tuple-element.29.resid_hbm, f32[256,128]{1,0:T(8,128)} %fp_hbm.5, f32[256,256]{1,0:T(8,128)} %old_hbm.5, ...), custom_call_target="tpu_custom_call" | custom-call | bytes 14000000 | tf_op jit(solution)/shard_map/own/pallas_call | solution.py:396
  30.9 0.7 %all-to-all-done.1 = f32[8,8,384]{2,1,0:T(8,128)S(1)} async-done(((f32[8,8,384]{2,1,0:T(8,128)}), f32[8,8,384]{2,1,0:T(8,128)S(1)}, u32[]{:S(2)}, u32[]{:S(2)}) %all-to-all-start.1) | async-done | bytes 98336 | tf_op jit(solution)/shard_map/all_to_all | solution.py:410
  31.6 2.1 %trace.1 = (f32[256,256]{1,0:T(8,128)}, f32[64,384]{1,0:T(8,128)}) custom-call(f32[2]{0:T(128)S(1)} %copy-done.1, f32[64,384]{1,0:T(8,128)S(1)} %bitcast.21, f32[256,256]{1,0:T(8,128)S(1)} %get-tuple-element.31.start_ref, f32[256,128]{1,0:T(8,128)S(1)} %get-tuple-element.32.scale_ref, f32[256,128]{1,0:T(8,128)S(1)} %get-tuple-element.33.weight_ref, ...), custom_call_target="tpu_custom_call" | custom-call | bytes 7000000 | tf_op jit(solution)/shard_map/trace/pallas_call | solution.py:396
  33.7 3.5 %all-to-all-start.2 = ((f32[8,8,384]{2,1,0:T(8,128)}), f32[8,8,384]{2,1,0:T(8,128)S(1)}, u32[]{:S(2)}, u32[]{:S(2)}) async-start(f32[8,8,384]{2,1,0:T(8,128)} %bitcast.9), calls=%async_computation.2 | async-start | bytes 196608 | tf_op jit(solution)/shard_map/all_to_all | solution.py:410
  37.2 4.2 %rest_own.1.own_hbm = f32[256,4096]{1,0:T(8,128)} custom-call(bf16[256,4096]{1,0:T(8,128)(2,1)} %get-tuple-element.26.movie_t_hbm, bf16[256,4096]{1,0:T(8,128)(2,1)} %get-tuple-element.27.dense_hbm, f32[256,256]{1,0:T(8,128)} %get-tuple-element.21.new_hbm.new_ref), custom_call_target="tpu_custom_call" | custom-call | bytes 14000000 | tf_op jit(solution)/shard_map/rest_own/pallas_call | solution.py:396
  41.4 1.0 %all-to-all-done.2 = f32[8,8,384]{2,1,0:T(8,128)S(1)} async-done(((f32[8,8,384]{2,1,0:T(8,128)}), f32[8,8,384]{2,1,0:T(8,128)S(1)}, u32[]{:S(2)}, u32[]{:S(2)}) %all-to-all-start.2) | async-done | bytes 98336 | tf_op jit(solution)/shard_map/all_to_all | solution.py:410
  42.4 3.6 %collective-permute-start.2 = (f32[8,128]{1,0:T(8,128)S(1)}, f32[8,128]{1,0:T(8,128)S(1)}, u32[]{:S(2)}, u32[]{:S(2)}) collective-permute-start(f32[8,128]{1,0:T(8,128)S(1)} %bitcast_reduce_fusion.refs_0_), channel_id=1, source_target_pairs={{0,24},{8,0},{16,8},{24,16},{1,25},{9,1},{17,9},{25,17},{2,26},{10... | collective-permute-start | bytes 12296 | tf_op jit(solution)/shard_map/ppermute | solution.py:472
  46.0 1.0 %collective-permute-start = (f32[8,128]{1,0:T(8,128)S(1)}, f32[8,128]{1,0:T(8,128)S(1)}, u32[]{:S(2)}, u32[]{:S(2)}) collective-permute-start(f32[8,128]{1,0:T(8,128)S(1)} %bitcast_reduce_fusion.refs_0_), channel_id=1, source_target_pairs={{0,8},{8,16},{16,24},{24,0},{1,9},{9,17},{17,25},{25,1},{2,10},{10... | collective-permute-start | bytes 12296 | tf_op jit(solution)/shard_map/ppermute | solution.py:472
  47.0 3.2 %rest_in.1.refs_5_ = f32[256,4096]{1,0:T(8,128)S(1)} custom-call(f32[64,384]{1,0:T(8,128)S(1)} %bitcast.19, f32[256,4096]{1,0:T(8,128)} %rest_own.1.own_hbm, bf16[64,4096]{1,0:T(8,128)(2,1)} %get-tuple-element.41.dense_in_hbm), custom_call_target="tpu_custom_call" | custom-call | bytes 14000000 | tf_op jit(solution)/shard_map/rest_in/pallas_call | solution.py:396
  50.2 0.0 copy-start
  50.2 0.3 collective-permute-done.1.refs_2_
  50.6 0.9 %collective-permute-done.refs_1_ = f32[8,128]{1,0:T(8,128)S(1)} collective-permute-done((f32[8,128]{1,0:T(8,128)S(1)}, f32[8,128]{1,0:T(8,128)S(1)}, u32[]{:S(2)}, u32[]{:S(2)}) %collective-permute-start) | collective-permute-done | bytes 4128 | tf_op jit(solution)/shard_map/ppermute | solution.py:472
  51.5 2.1 %border.1 = (bf16[256,4096]{1,0:T(8,128)(2,1)S(1)}, f32[64,128]{1,0:T(8,128)}, f32[2,128]{1,0:T(2,128)}) custom-call(f32[64,512]{1,0:T(8,128)S(1)} %bitcast.17, f32[64,384]{1,0:T(8,128)S(1)} %bitcast.20, f32[8,128]{1,0:T(8,128)S(1)} %bitcast_reduce_fusion.refs_0_, f32[8,128]{1,0:T(8,128)S(1)} %collective-permute-done.refs_1_, ...), custom_call_target="tpu_custom_call" | custom-call | bytes 10500000 | tf_op jit(solution)/shard_map/border/pallas_call | solution.py:396
  53.6 3.3 %all-to-all-start.3 = ((f32[8,8,128]{2,1,0:T(8,128)}), f32[8,8,128]{2,1,0:T(8,128)S(1)}, u32[]{:S(2)}, u32[]{:S(2)}) async-start(f32[8,8,128]{2,1,0:T(8,128)} %bitcast.12), calls=%async_computation.3 | async-start | bytes 65536 | tf_op jit(solution)/shard_map/all_to_all | solution.py:410
  57.0 3.7 %footprint.1 = f32[256,128]{1,0:T(8,128)} custom-call(bf16[256,4096]{1,0:T(8,128)(2,1)S(1)} %get-tuple-element.42.resid_ref, f32[256,256]{1,0:T(8,128)S(1)} %copy-done, f32[256,128]{1,0:T(8,128)} %fp_hbm.5, s32[256,128]{1,0:T(8,128)} %idx_hbm.3), custom_call_target="tpu_custom_call" | custom-call | bytes 14000000 | tf_op jit(solution)/shard_map/footprint/pallas_call | solution.py:396
  60.6 1.1 %all-to-all-done.3 = f32[8,8,128]{2,1,0:T(8,128)S(1)} async-done(((f32[8,8,128]{2,1,0:T(8,128)}), f32[8,8,128]{2,1,0:T(8,128)S(1)}, u32[]{:S(2)}, u32[]{:S(2)}) %all-to-all-start.3) | async-done | bytes 32800 | tf_op jit(solution)/shard_map/all_to_all | solution.py:410
  61.7 0.8 %unpack.1 = f32[48,128]{1,0:T(8,128)} custom-call(bf16[48,64]{1,0:T(8,128)(2,1)S(1)} %get-tuple-element.43.place_ref, f32[64,128]{1,0:T(8,128)S(1)} %bitcast.22), custom_call_target="tpu_custom_call" | custom-call | bytes 3500000 | tf_op jit(solution)/shard_map/unpack/pallas_call | solution.py:396
  (5 shorter events, 0.0 us)
Async XLA Ops:
  2.8 12.2 %all-to-all-start = ((f32[8,8,512]{2,1,0:T(8,128)}), f32[8,8,512]{2,1,0:T(8,128)S(1)}, u32[]{:S(2)}, u32[]{:S(2)}) async-start(f32[8,8,512]{2,1,0:T(8,128)} %bitcast.3), calls=%async_computation | async-start | bytes 262144 | tf_op jit(solution)/shard_map/all_to_all | solution.py:410
  15.0 11.4 %copy-start.1 = (f32[2]{0:T(128)S(1)}, f32[2]{0:T(128)}, u32[]{:S(2)}) copy-start(f32[2]{0:T(128)} %ar_ref.3) | copy-start | bytes 28
  22.2 9.4 %all-to-all-start.1 = ((f32[8,8,384]{2,1,0:T(8,128)}), f32[8,8,384]{2,1,0:T(8,128)S(1)}, u32[]{:S(2)}, u32[]{:S(2)}) async-start(f32[8,8,384]{2,1,0:T(8,128)} %bitcast.7), calls=%async_computation.1 | async-start | bytes 196608 | tf_op jit(solution)/shard_map/all_to_all | solution.py:410
  33.7 8.7 %all-to-all-start.2 = ((f32[8,8,384]{2,1,0:T(8,128)}), f32[8,8,384]{2,1,0:T(8,128)S(1)}, u32[]{:S(2)}, u32[]{:S(2)}) async-start(f32[8,8,384]{2,1,0:T(8,128)} %bitcast.9), calls=%async_computation.2 | async-start | bytes 196608 | tf_op jit(solution)/shard_map/all_to_all | solution.py:410
  42.4 7.8 %collective-permute-start.2 = (f32[8,128]{1,0:T(8,128)S(1)}, f32[8,128]{1,0:T(8,128)S(1)}, u32[]{:S(2)}, u32[]{:S(2)}) collective-permute-start(f32[8,128]{1,0:T(8,128)S(1)} %bitcast_reduce_fusion.refs_0_), channel_id=1, source_target_pairs={{0,24},{8,0},{16,8},{24,16},{1,25},{9,1},{17,9},{25,17},{2,26},{10... | collective-permute-start | bytes 12296 | tf_op jit(solution)/shard_map/ppermute | solution.py:472
  46.0 4.5 %collective-permute-start.1 = (f32[8,128]{1,0:T(8,128)S(1)}, f32[8,128]{1,0:T(8,128)S(1)}, u32[]{:S(2)}, u32[]{:S(2)}) collective-permute-start(f32[8,128]{1,0:T(8,128)S(1)} %bitcast_reduce_fusion.refs_0_), channel_id=1, source_target_pairs={{0,16},{8,24},{16,0},{24,8},{1,17},{9,25},{17,1},{25,9},{2,18},{10... | collective-permute-start | bytes 12296 | tf_op jit(solution)/shard_map/ppermute | solution.py:472
  46.0 5.4 %collective-permute-start = (f32[8,128]{1,0:T(8,128)S(1)}, f32[8,128]{1,0:T(8,128)S(1)}, u32[]{:S(2)}, u32[]{:S(2)}) collective-permute-start(f32[8,128]{1,0:T(8,128)S(1)} %bitcast_reduce_fusion.refs_0_), channel_id=1, source_target_pairs={{0,8},{8,16},{16,24},{24,0},{1,9},{9,17},{17,25},{25,1},{2,10},{10... | collective-permute-start | bytes 12296 | tf_op jit(solution)/shard_map/ppermute | solution.py:472
  50.2 6.8 %copy-start = (f32[256,256]{1,0:T(8,128)S(1)}, f32[256,256]{1,0:T(8,128)}, u32[]{:S(2)}) copy-start(f32[256,256]{1,0:T(8,128)} %get-tuple-element.21.new_hbm.new_ref) | copy-start | bytes 786436
  53.6 8.1 %all-to-all-start.3 = ((f32[8,8,128]{2,1,0:T(8,128)}), f32[8,8,128]{2,1,0:T(8,128)S(1)}, u32[]{:S(2)}, u32[]{:S(2)}) async-start(f32[8,8,128]{2,1,0:T(8,128)} %bitcast.12), calls=%async_computation.3 | async-start | bytes 65536 | tf_op jit(solution)/shard_map/all_to_all | solution.py:410

commit v3 on v2

v3 whole, which is shorter than its diff:
```python
import jax
import jax.numpy as jnp
from jax import lax
from jax.experimental import pallas as pl
from jax.experimental.pallas import tpu as pltpu
from jax.sharding import PartitionSpec as P

CAP = 8
RIDGE = 1.0
LANES = 128
F32 = jnp.float32
BF16 = jnp.bfloat16
VMEM_BYTES = 40 << 20
CHUNK = 2048
TURN = 512
UNROLL = 128
PAD = 8


def nn(a, b):
    return lax.dot_general(a, b, (((1,), (0,)), ((), ())), preferred_element_type=F32)


def nt(a, b):
    return lax.dot_general(a, b, (((1,), (1,)), ((), ())), preferred_element_type=F32)


def split(x, terms):
    parts = []
    for _ in range(terms):
        part = x.astype(BF16)
        parts.append(part)
        x = x - part.astype(F32)
    return parts


def stack(table, terms=3):
    return jnp.concatenate([table] * terms, axis=1)


def select_rows(table, x, terms=3):
    return nn(stack(table, terms), jnp.concatenate(split(x, terms), axis=0))


def iota(shape, dim):
    return lax.broadcasted_iota(jnp.int32, shape, dim)


def to_column(row):
    n = row.shape[1]
    return jnp.sum(jnp.where(iota((n, n), 0) == iota((n, n), 1), row, jnp.zeros_like(row)), axis=1, keepdims=True)


def to_row(column):
    n = column.shape[0]
    return jnp.sum(jnp.where(iota((n, n), 0) == iota((n, n), 1), column, jnp.zeros_like(column)), axis=0, keepdims=True)


def shift_lanes(x, count):
    return jnp.where(iota(x.shape, len(x.shape) - 1) >= count, pltpu.roll(x, count, len(x.shape) - 1), 0.0)


def pieces(width):
    return [slice(start, start + CHUNK) for start in range(0, width, CHUNK)]


def fetch(source, target, sem):
    copy = pltpu.make_async_copy(source, target, sem)
    copy.start()
    return copy


def fetch_columns(*copies):
    return [
        [fetch(source.at[:, here], target.at[:, here], sems.at[k]) for source, target, sems in copies]
        for k, here in enumerate(pieces(copies[0][0].shape[1]))
    ]


def pack_kernel(tile_ref, bfp_hbm, bidx_hbm, bown_hbm, boff_hbm, old_hbm, fp_hbm, idx_hbm, send_ref, pick_ref, pick_t_ref, place_ref,
                fp_ref, idx_ref, bfp_ref, bidx_ref, bown_ref, boff_ref, old_ref, sems):
    copies = [
        fetch(source, target, sems.at[k])
        for k, (source, target) in enumerate(
            ((boff_hbm, boff_ref), (bown_hbm, bown_ref), (bfp_hbm, bfp_ref), (bidx_hbm, bidx_ref), (old_hbm, old_ref), (fp_hbm, fp_ref), (idx_hbm, idx_ref))
        )
    ]
    slots = send_ref.shape[0]
    tiles = slots // CAP
    border, support = bfp_ref.shape
    owned = old_ref.shape[0]
    copies[0].wait()
    copies[1].wait()
    target = boff_ref[...] + (tile_ref[0] + 1)
    target = jnp.where(target >= tiles, target - tiles, target)
    target_col = to_column(target)
    same = target_col == target
    before = iota((border, border), 0) < iota((border, border), 1)
    rank = jnp.sum(jnp.where(jnp.logical_and(same, before), 1, 0), axis=0, keepdims=True)
    slot = target * CAP + rank
    owner = bown_ref[...]
    place_t = iota((slots, border), 0) == slot
    place = iota((border, slots), 1) == to_column(slot)
    owner_col = jnp.sum(jnp.where(place_t, owner + 1, 0), axis=1, keepdims=True) - 1
    owner_row = jnp.sum(jnp.where(place, to_column(owner) + 1, 0), axis=0, keepdims=True) - 1
    pick = jnp.where(iota((slots, owned), 1) == owner_col, 1.0, 0.0).astype(BF16)
    pick_ref[...] = pick
    pick_t_ref[...] = jnp.where(iota((owned, slots), 0) == owner_row, 1.0, 0.0).astype(BF16)
    place_ref[...] = jnp.where(place, 1.0, 0.0).astype(BF16)
    place_t = jnp.where(place_t, 1.0, 0.0).astype(BF16)
    copies[2].wait()
    send_ref[:, :support] = select_rows(place_t, bfp_ref[...])
    copies[3].wait()
    send_ref[:, support:2 * support] = select_rows(place_t, bidx_ref[...].astype(F32), 2)
    copies[4].wait()
    send_ref[:, 2 * support:] = select_rows(pick, old_ref[...])
    copies[5].wait()
    copies[6].wait()


def scatter_rows(values_ref, index_ref, grid_ref, rows, stride, first=0):
    cells = grid_ref.shape[0] // stride
    support = values_ref.shape[1]
    hi_range = iota((cells, support), 0).astype(BF16)
    lo_range = iota((LANES, support), 0).astype(BF16)
    zero = jnp.zeros((cells, support), BF16)
    none = jnp.zeros((LANES, support), BF16)
    one = jnp.ones((LANES, support), BF16)

    def factors(row):
        index = index_ref[pl.ds(row, 1), :]
        value = values_ref[pl.ds(row, 1), :]
        high = jnp.broadcast_to((index >> 7).astype(F32), (cells, support)).astype(BF16)
        low = jnp.broadcast_to((index & 127).astype(F32), (LANES, support)).astype(BF16)
        coarse = value.astype(BF16).astype(F32)
        top = jnp.broadcast_to(coarse, (cells, support)).astype(BF16)
        rest = jnp.broadcast_to(value - coarse, (cells, support)).astype(BF16)
        hit = high == hi_range
        return jnp.where(hit, top, zero), jnp.where(hit, rest, zero), jnp.where(low == lo_range, one, none)

    for k in range(0, rows, 2):
        row = first + k
        top, rest, right = factors(row)
        top_next, rest_next, right_next = factors(row + 1)
        left = jnp.concatenate([
            jnp.concatenate([top, rest, zero, zero], axis=0),
            jnp.concatenate([zero, zero, top_next, rest_next], axis=0),
        ], axis=1)
        made = nt(left, jnp.concatenate([right, right_next], axis=1))
        grid_ref[pl.ds(k, cells, stride=stride), :] = made[:cells] + made[cells:2 * cells]
        grid_ref[pl.ds(k + 1, cells, stride=stride), :] = made[2 * cells:3 * cells] + made[3 * cells:]


def prepare_kernel(movie_hbm, fp_ref, idx_ref, spatial_hbm, dense_hbm, movie_t_hbm, seen_hbm,
                   movie_ref, dense_ref, movie_t_ref, grid_ref, spatial_ref, seen_ref, movie_sem, sems, dense_sems, out_sems):
    owned = fp_ref.shape[0]
    voxels, frames = movie_hbm.shape
    groups = dense_sems.shape[0]
    rows = owned // groups
    stride = grid_ref.shape[0] // (voxels // LANES)
    first = fetch(spatial_hbm, spatial_ref, sems.at[0])
    load = fetch(movie_hbm, movie_ref, movie_sem)
    eye = jnp.where(iota((frames, frames), 0) == iota((frames, frames), 1), 1.0, 0.0).astype(BF16)
    stores = []
    first.wait()
    for group in range(groups):
        mine = slice(group * rows, (group + 1) * rows)
        scatter_rows(fp_ref, idx_ref, grid_ref, rows, stride, group * rows)
        for start in range(mine.start, mine.stop, 8):
            seen_ref[start:start + 8, :] = pick_rows(spatial_ref, idx_ref[start:start + 8, :], slice(0, 1))
        for cell in range(voxels // LANES):
            dense_ref[mine, cell * LANES:(cell + 1) * LANES] = grid_ref[cell * stride:cell * stride + rows, :].astype(BF16)
        stores.append(fetch(dense_ref.at[mine], dense_hbm.at[mine], dense_sems.at[group]))
        if group == 0:
            load.wait()
            for k, here in enumerate(pieces(voxels)):
                movie_t_ref[:, here] = nt(eye, movie_ref[here, :]).astype(BF16)
                stores.append(fetch(movie_t_ref.at[:, here], movie_t_hbm.at[:, here], out_sems.at[k]))
    stores.append(fetch(seen_ref, seen_hbm, sems.at[1]))
    for copy in stores:
        copy.wait()


def transposed_parts(x):
    return jnp.concatenate([jnp.transpose(part.astype(F32)).astype(BF16) for part in split(x, 3)], axis=1)


def project_kernel(recv_ref, movie_t_hbm, dense_hbm, old_hbm, spatial_hbm, trace_hbm, resid_hbm, dense_in_hbm, proj_ref,
                   movie_t_ref, dense_ref, old_ref, spatial_ref, trace_ref, resid_ref, values_ref, idx_ref,
                   grid_ref, in_sems, movie_sems, dense_sems, resid_sems, out_sem):
    slots = recv_ref.shape[0]
    owned = dense_hbm.shape[0]
    frames, voxels = movie_t_hbm.shape
    support = values_ref.shape[1]
    stride = slots + PAD
    first = [fetch(spatial_hbm, spatial_ref, in_sems.at[1]), fetch(old_hbm, old_ref, in_sems.at[0]), fetch(trace_hbm, trace_ref, in_sems.at[2])]
    loads = fetch_columns((dense_hbm, dense_ref.at[:owned], dense_sems), (movie_t_hbm, movie_t_ref, movie_sems))
    values_ref[...] = recv_ref[:, :support]
    idx_ref[...] = recv_ref[:, support:2 * support].astype(jnp.int32)
    scatter_rows(values_ref, idx_ref, grid_ref, slots, stride)
    for copy in first:
        copy.wait()
    both_t = jnp.concatenate([jnp.transpose(old_ref[...]).astype(BF16), transposed_parts(recv_ref[:, 2 * support:])], axis=1)
    back = to_column(trace_ref[...])
    seen_in = jnp.zeros((slots, LANES), F32)
    for cell in range(voxels // LANES):
        at = cell * LANES
        part = grid_ref[cell * stride:cell * stride + slots, :].astype(BF16)
        for copy in range(3):
            dense_ref[owned + copy * slots:owned + (copy + 1) * slots, at:at + LANES] = part
        seen_in += part.astype(F32) * spatial_ref[:, at:at + LANES]
    mine = dense_ref.at[owned:owned + slots]
    stores = [fetch(mine, dense_in_hbm, out_sem)]
    for k, here in enumerate(pieces(voxels)):
        for copy in loads[k]:
            copy.wait()
        recon = nn(both_t, dense_ref[:, here]) + back * spatial_ref[:, here]
        resid_ref[:, here] = (movie_t_ref[:, here].astype(F32) - recon).astype(BF16)
        stores.append(fetch(resid_ref.at[:, here], resid_hbm.at[:, here], resid_sems.at[k]))
        part = nt(mine[:, here], resid_ref[:, here])
        total = part if k == 0 else total + part
    proj_ref[:, :frames] = total
    proj_ref[:, frames:] = jnp.broadcast_to(jnp.sum(seen_in, axis=1, keepdims=True), (slots, LANES))
    for copy in stores:
        copy.wait()


def own_kernel(ar_ref, dense_hbm, resid_hbm, movie_t_hbm, spatial_hbm, fp_hbm, old_hbm, send_ref, pick_t_ref, start_ref, scale_ref, weight_ref, base_ref, impulse_ref,
               dense_ref, resid_ref, movie_t_ref, spatial_ref, fp_ref, old_ref, in_sems):
    frames, voxels = resid_hbm.shape
    owned, support = fp_hbm.shape
    first = [fetch(fp_hbm, fp_ref, in_sems.at[0]), fetch(old_hbm, old_ref, in_sems.at[1]), fetch(spatial_hbm, spatial_ref, in_sems.at[4])]
    dense_load = fetch(dense_hbm, dense_ref, in_sems.at[2])
    movie_load = fetch(movie_t_hbm, movie_t_ref, in_sems.at[5])
    resid_load = fetch(resid_hbm, resid_ref, in_sems.at[3])
    near, far = ar_ref[0], ar_ref[1]
    response = jnp.where(iota((8, frames), 1) == 0, 1.0, 0.0)
    step = 1
    while step < frames:
        change = near * shift_lanes(response, step)
        if 2 * step < frames:
            change = change - far * shift_lanes(response, 2 * step)
        response = response + change
        near, far = near * near + 2.0 * far, -far * far
        step *= 2
    wide = jnp.broadcast_to(response[0:1], (frames, frames))
    wide = pltpu.roll(wide, 0, 1, stride=1, stride_axis=0)
    high, mid, low = split(jnp.where(iota((frames, frames), 1) >= iota((frames, frames), 0), wide, 0.0), 3)
    impulse_ref[...] = jnp.concatenate([high, mid, low, high, mid, high], axis=0)
    for copy in first:
        copy.wait()
    border_fp = send_ref[:, :support]
    square = jnp.broadcast_to(jnp.sum(border_fp * border_fp, axis=1, keepdims=True), (send_ref.shape[0], LANES))
    fp = fp_ref[...]
    share = 1.0 / (jnp.sum(fp * fp, axis=1, keepdims=True) + select_rows(pick_t_ref[...], square)[:, 0:1])
    scale_ref[...] = jnp.broadcast_to(share, (owned, LANES))
    dense_load.wait()
    weight = jnp.zeros((owned, LANES), F32)
    for at in range(0, voxels, LANES):
        weight += dense_ref[:, at:at + LANES].astype(F32) * spatial_ref[:, at:at + LANES]
    weight_ref[...] = jnp.broadcast_to(jnp.sum(weight, axis=1, keepdims=True), (owned, LANES))
    movie_load.wait()
    seen = jnp.zeros((frames, LANES), F32)
    for at in range(0, voxels, LANES):
        seen += movie_t_ref[:, at:at + LANES].astype(F32) * spatial_ref[:, at:at + LANES]
    seen = to_row(jnp.sum(seen, axis=1, keepdims=True))
    norm = jnp.sum(spatial_ref[...] * spatial_ref[...], axis=1, keepdims=True)
    row = iota((8, LANES), 0)
    base_ref[...] = jnp.where(row == 0, seen[:, :LANES], jnp.where(row == 1, seen[:, LANES:], jnp.where(row == 2, norm, 0.0)))
    resid_load.wait()
    start_ref[...] = old_ref[...] + nt(dense_ref[...], resid_ref[...]) * share


def trace_kernel(ar_ref, back_ref, start_ref, scale_ref, weight_ref, base_ref, impulse_ref, pick_ref, pick_t_ref, new_ref, send_ref, part_ref):
    frames = start_ref.shape[1]
    returned = select_rows(pick_t_ref[...], back_ref[...])
    raw = start_ref[...] + returned[:, :frames] * scale_ref[:, 0:1]
    spikes = jnp.maximum(raw - ar_ref[0] * shift_lanes(raw, 1) - ar_ref[1] * shift_lanes(raw, 2), 0.0)
    high, mid, low = split(spikes, 3)
    new = nn(jnp.concatenate([high, high, high, mid, mid, low], axis=1), impulse_ref[...])
    new_ref[...] = new
    send_ref[...] = select_rows(pick_ref[...], new)
    used = weight_ref[:, 0:1] * new.astype(BF16).astype(F32) + returned[:, frames:frames + 1] * new
    used = jnp.sum(used, axis=0, keepdims=True)
    base = base_ref[...]
    row = iota((8, LANES), 0)
    part_ref[...] = base - jnp.where(row == 0, used[:, :LANES], jnp.where(row == 1, used[:, LANES:], 0.0))


def pick_rows(grad_ref, index, rows):
    high = index >> 7
    low = index & 127
    picked = jnp.zeros(index.shape, F32)
    for cell in range(grad_ref.shape[1] // LANES):
        grad = jnp.broadcast_to(grad_ref[rows, cell * LANES:(cell + 1) * LANES], index.shape)
        found = jnp.take_along_axis(grad, low, axis=1, mode="promise_in_bounds")
        picked = jnp.where(high == cell, found, picked)
    return picked


def pick_support(grad_ref, idx_ref, out, rows):
    @pl.loop(0, rows // 64)
    def _(group):
        for k in range(8):
            here = pl.ds(pl.multiple_of(group * 64 + k * 8, 8), 8)
            out(here, pick_rows(grad_ref, idx_ref[here, :], slice(0, 1) if grad_ref.shape[0] == 1 else here))


def rest_own_kernel(movie_t_hbm, dense_hbm, new_hbm, spatial_hbm, trace_hbm, recv_ref, rest_hbm, seen_ref,
                    movie_t_ref, dense_ref, new_ref, spatial_ref, trace_ref, idx_ref, rest_ref, sems, movie_sems, dense_sems, out_sems):
    voxels = movie_t_hbm.shape[1]
    slots, support = idx_ref.shape
    first = [fetch(new_hbm, new_ref, sems.at[0]), fetch(spatial_hbm, spatial_ref, sems.at[1]), fetch(trace_hbm, trace_ref, sems.at[2])]
    loads = fetch_columns((dense_hbm, dense_ref, dense_sems), (movie_t_hbm, movie_t_ref, movie_sems))
    idx_ref[...] = recv_ref[:, support:2 * support].astype(jnp.int32)
    for copy in first:
        copy.wait()
    new_t = jnp.transpose(new_ref[...]).astype(BF16)
    back = to_column(trace_ref[...])
    stores = []
    for k, here in enumerate(pieces(voxels)):
        for copy in loads[k]:
            copy.wait()
        recon = nn(new_t, dense_ref[:, here]) + back * spatial_ref[:, here]
        rest_ref[:, here] = (movie_t_ref[:, here].astype(F32) - recon).astype(BF16)
        stores.append(fetch(rest_ref.at[:, here], rest_hbm.at[:, here], out_sems.at[k]))

    def out(here, picked):
        seen_ref[here, :] = picked

    pick_support(spatial_ref, idx_ref, out, slots)
    for copy in stores:
        copy.wait()


def against_rest(low, new):
    shared = nt(low, new.astype(BF16))
    for part in split(new, 3)[1:]:
        shared = shared + nt(low, part)
    return jnp.concatenate([low] + split(-shared, 2), axis=1)


def fetch_rest(rest_hbm, dense_in_hbm, both_ref, sems, in_sems):
    frames, slots = rest_hbm.shape[0], dense_in_hbm.shape[0]
    return fetch_columns(
        (rest_hbm, both_ref.at[:frames], sems),
        *[(dense_in_hbm, both_ref.at[frames + copy * slots:frames + (copy + 1) * slots], each) for copy, each in enumerate(in_sems)],
    )


def border_kernel(recv0_ref, recv_ref, seen_ref, *refs):
    *totals, rest_hbm, dense_in_hbm, send_ref, both_ref, grad_ref, idx_ref, sems, sems_near, sems_far = refs
    in_sems = (sems_near, sems_far)
    slots, support = seen_ref.shape
    loads = fetch_rest(rest_hbm, dense_in_hbm, both_ref, sems, in_sems)
    new = recv_ref[...]
    left = against_rest(new.astype(BF16), new)
    idx_ref[...] = recv0_ref[:, support:2 * support].astype(jnp.int32)
    send_ref[:, support:2 * support] = seen_ref[...]
    total = totals[0][...]
    for other in totals[1:]:
        total = total + other[...]
    for tile in range(slots // CAP):
        send_ref[tile * CAP:(tile + 1) * CAP, 2 * support:] = total
    for k, here in enumerate(pieces(both_ref.shape[1])):
        for copy in loads[k]:
            copy.wait()
        grad_ref[:, here] = nn(left, both_ref[:, here])

    def out(here, picked):
        send_ref[here, :support] = picked

    pick_support(grad_ref, idx_ref, out, slots)


def footprint_kernel(recv_ref, rest_hbm, dense_in_hbm, new_hbm, fp_hbm, idx_hbm, seen_hbm, send_hbm, send_new_hbm, trace_hbm,
                     base_ref, slope_ref, low_ref, border_ref, share_ref, sent_ref, old_ref,
                     both_ref, new_ref, fp_ref, idx_ref, seen_ref, send_ref, send_new_ref, grad_ref, part_ref, first_sems, sems, *in_sems):
    slots = recv_ref.shape[0]
    owned, support = fp_ref.shape
    first = [
        fetch(source, target, first_sems.at[k])
        for k, (source, target) in enumerate((
            (new_hbm, new_ref), (fp_hbm, fp_ref), (idx_hbm, idx_ref), (seen_hbm, seen_ref), (send_hbm, send_ref), (send_new_hbm, send_new_ref),
            (trace_hbm, old_ref),
        ))
    ]
    loads = fetch_rest(rest_hbm, dense_in_hbm, both_ref, sems, in_sems)
    for copy in first:
        copy.wait()
    new = new_ref[...]
    low = new.astype(BF16)
    low_ref[...] = low
    left = against_rest(low, recv_ref[...])
    part_ref[...] = jnp.broadcast_to(1.0 / (jnp.sum(new * new, axis=1, keepdims=True) + RIDGE), (owned, support))
    sent = send_new_ref[...]
    sent_ref[...] = sent.astype(BF16)
    share_ref[...] = jnp.broadcast_to(1.0 / (jnp.sum(sent * sent, axis=1, keepdims=True) + RIDGE), (slots, support))
    border_ref[...] = send_ref[:, :support]
    for k, here in enumerate(pieces(both_ref.shape[1])):
        for copy in loads[k]:
            copy.wait()
        grad_ref[:, here] = nn(left, both_ref[:, here])

    def out(here, picked):
        base_ref[here, :] = fp_ref[here, :] + picked * part_ref[here, :]
        slope_ref[here, :] = seen_ref[here, :] * part_ref[here, :]

    pick_support(grad_ref, idx_ref, out, owned)


def finish_kernel(rows_ref, base_ref, slope_ref, low_ref, border_ref, share_ref, sent_ref, old_ref, place_ref, out_ref, border_out_ref, back_ref):
    slots, support = border_ref.shape
    total = rows_ref[:CAP, 2 * support:]
    for tile in range(1, slots // CAP):
        total = total + rows_ref[tile * CAP:(tile + 1) * CAP, 2 * support:]
    back = total[0:2] / total[2:3, 0:1]
    back_ref[...] = back
    change = jnp.concatenate([back[0:1], back[1:2]], axis=1) - old_ref[...]
    along = jnp.sum(low_ref[...].astype(F32) * change, axis=1, keepdims=True)
    out_ref[...] = jnp.maximum(base_ref[...] - along * slope_ref[...], 0.0)
    along = jnp.sum(sent_ref[...].astype(F32) * change, axis=1, keepdims=True)
    grad = rows_ref[:, :support] - along * rows_ref[:, support:2 * support]
    border_out_ref[...] = select_rows(place_ref[...], jnp.maximum(border_ref[...] + grad * share_ref[...], 0.0))


def call(kernel, name, micros, ins, outs, scratch, *args):
    space = {"s": pltpu.SMEM, "v": pltpu.VMEM, "h": pltpu.HBM}
    shapes = [pltpu.HBM(shape, dtype) if where == "h" else jax.ShapeDtypeStruct(shape, dtype) for where, shape, dtype in outs]
    args = [pltpu.with_memory_space_constraint(arg, pltpu.HBM) if where == "h" else arg for where, arg in zip(ins, args)]
    places = [pl.BlockSpec(memory_space=space[where]) for where, _, _ in outs]
    many = len(outs) > 1
    return pl.pallas_call(
        kernel,
        out_shape=shapes if many else shapes[0],
        in_specs=[pl.BlockSpec(memory_space=space[where]) for where in ins],
        out_specs=places if many else places[0],
        scratch_shapes=list(scratch),
        cost_estimate=pl.CostEstimate(flops=0, bytes_accessed=int(micros * 3.5e6), transcendentals=0),
        compiler_params=pltpu.CompilerParams(vmem_limit_bytes=VMEM_BYTES),
        name=name,
    )(*args)


def exchange(rows, tiles):
    width = rows.shape[1]
    moved = lax.all_to_all(rows.reshape(tiles, CAP, width), "tile", split_axis=0, concat_axis=0, tiled=True)
    return moved.reshape(tiles * CAP, width)


def other_regions(total, regions):
    return [lax.ppermute(total, "region", [(i, (i + shift) % regions) for i in range(regions)]) for shift in range(1, regions)]


def body(movie, footprint, support_idx, trace_old, ar_coef, border_fp, border_idx, border_owner, border_offset, back_spatial, back_trace):
    tiles = lax.axis_size("tile")
    regions = lax.axis_size("region")
    tile = lax.axis_index("tile").astype(jnp.int32).reshape(1)
    voxels, frames = movie.shape
    owned, support = footprint.shape
    border = border_fp.shape[0]
    slots = tiles * CAP
    cells = voxels // LANES
    spatial = back_spatial.reshape(1, voxels)
    V, dma, i32 = pltpu.VMEM, pltpu.SemaphoreType.DMA, jnp.int32
    n = voxels // CHUNK
    groups = owned // UNROLL
    wide = frames + LANES

    send, pick, pick_t, place, footprint_near, support_near = call(
        pack_kernel, "pack", 2, "shhhhhhh",
        [("v", (slots, 2 * support + frames), F32), ("v", (slots, owned), BF16), ("v", (owned, slots), BF16), ("v", (border, slots), BF16),
         ("v", (owned, support), F32), ("v", (owned, support), i32)],
        [V((border, support), F32), V((border, support), i32), V((1, border), i32), V((1, border), i32), V((owned, frames), F32), dma((7,))],
        tile, border_fp, border_idx, border_owner.reshape(1, border), border_offset.reshape(1, border), trace_old, footprint, support_idx,
    )
    recv = exchange(send, tiles)
    dense, movie_t, seen_own = call(
        prepare_kernel, "prepare", 7, "hvvh",
        [("h", (owned, voxels), BF16), ("h", (frames, voxels), BF16), ("h", (owned, support), F32)],
        [V((voxels, frames), BF16), V((owned, voxels), BF16), V((frames, voxels), BF16),
         V((cells * (UNROLL + PAD), LANES), F32), V((1, voxels), F32), V((owned, support), F32), dma, dma((2,)), dma((groups,)), dma((n,))],
        movie, footprint_near, support_near, spatial,
    )
    resid, dense_in, proj_in = call(
        project_kernel, "project", 5, "vhhhhh",
        [("h", (frames, voxels), BF16), ("h", (slots, voxels), BF16), ("v", (slots, wide), F32)],
        [V((frames, voxels), BF16), V((owned + 3 * slots, voxels), BF16), V((owned, frames), F32), V((1, voxels), F32), V((1, frames), F32),
         V((frames, voxels), BF16), V((slots, support), F32), V((slots, support), i32),
         V((cells * (slots + PAD), LANES), F32), dma((3,)), dma((n,)), dma((n,)), dma((n,)), dma],
        recv, movie_t, dense, trace_old, spatial, back_trace.reshape(1, frames),
    )
    returned = exchange(proj_in, tiles)
    start, scale, weight, base, impulse = call(
        own_kernel, "own", 4, "shhhhhhvv",
        [("v", (owned, frames), F32), ("v", (owned, LANES), F32), ("v", (owned, LANES), F32), ("v", (CAP, LANES), F32), ("v", (6 * frames, frames), BF16)],
        [V((owned, voxels), BF16), V((frames, voxels), BF16), V((frames, voxels), BF16), V((1, voxels), F32), V((owned, support), F32),
         V((owned, frames), F32), dma((6,))],
        ar_coef, dense, resid, movie_t, spatial, footprint, trace_old, send, pick_t,
    )
    trace_new, send_new, part = call(
        trace_kernel, "trace", 2, "svvvvvvvv",
        [("v", (owned, frames), F32), ("v", (slots, frames), F32), ("v", (CAP, LANES), F32)], [],
        ar_coef, returned, start, scale, weight, base, impulse, pick, pick_t,
    )
    recv_new = exchange(send_new, tiles)
    totals = [part] + other_regions(part, regions)
    row_trace = back_trace.reshape(1, frames)
    rest, seen = call(
        rest_own_kernel, "rest_own", 4, "hhhhhv", [("h", (frames, voxels), BF16), ("v", (slots, support), F32)],
        [V((frames, voxels), BF16), V((owned, voxels), BF16), V((owned, frames), F32), V((1, voxels), F32), V((1, frames), F32), V((slots, support), i32),
         V((frames, voxels), BF16), dma((3,)), dma((n,)), dma((n,)), dma((n,))],
        movie_t, dense, trace_new, spatial, row_trace, recv,
    )
    recv_new, seen = lax.optimization_barrier((recv_new, seen))
    both = 2 * slots + frames
    send_back = call(
        border_kernel, "border", 4, "vvv" + "v" * regions + "hh", [("v", (slots, 2 * support + LANES), F32)],
        [V((both, voxels), BF16), V((slots, voxels), F32), V((slots, support), i32), dma((n,)), dma((n,)), dma((n,))],
        recv, recv_new, seen, *totals, rest, dense_in,
    )
    back_rows = exchange(send_back, tiles)
    parts = call(
        footprint_kernel, "footprint", 5, "vhhhhhhhhh",
        [("v", (owned, support), F32), ("v", (owned, support), F32), ("v", (owned, frames), BF16), ("v", (slots, support), F32), ("v", (slots, support), F32),
         ("v", (slots, frames), BF16), ("v", (1, frames), F32)],
        [V((both, voxels), BF16), V((owned, frames), F32), V((owned, support), F32), V((owned, support), i32), V((owned, support), F32),
         V((slots, 2 * support + frames), F32), V((slots, frames), F32), V((owned, voxels), F32), V((owned, support), F32),
         dma((7,)), dma((n,)), dma((n,)), dma((n,))],
        recv_new, rest, dense_in, trace_new, footprint, support_idx, seen_own, send, send_new, row_trace,
    )
    footprint_new, border_new, back = call(
        finish_kernel, "finish", 1, "vvvvvvvvv",
        [("v", (owned, support), F32), ("v", (border, support), F32), ("v", (2, LANES), F32)], [],
        back_rows, *parts, place,
    )
    return (trace_new, footprint_new, border_new, back.reshape(frames))


def solution(mesh):
    row = P(("region", "tile"), None)
    flat = P(("region", "tile"))
    return jax.shard_map(
        body,
        mesh=mesh,
        in_specs=(row, row, row, row, P(), row, row, flat, row, flat, P()),
        out_specs=(row, row, row, P()),
        check_vma=False,
    )
```

time: 63.2 us -> 58.3 us (0.922)
  waiting for transfers between devices: 4 us -> 0.64 us
  Pallas kernels: 36.9 us -> 34 us
  starting transfers between devices: 20.9 us -> 22.2 us
    pallas_call x10 -> x9, Pallas kernels: 36.9 us -> 34 us  [call(): pl.pallas_call(kernel, out_shape=shapes if many else shapes[0], in_specs=...]
    all_to_all x4, waiting for transfers between devices: 2.77 us -> 0.22 us  [exchange(): lax.all_to_all(rows.reshape(tiles, CAP, width), 'tile', split_axis=0, con...]
    all_to_all x4, starting transfers between devices: 16.3 us -> 17.6 us  [exchange(): lax.all_to_all(rows.reshape(tiles, CAP, width), 'tile', split_axis=0, con...]
    ppermute x3, waiting for transfers between devices: 1.23 us -> 0.42 us  [other_regions(): lax.ppermute(total, 'region', [(i, (i + shift) % regions) for i in range(...]
  transfers between devices with their start and end apart: 7 -> 7, of which waited for: 5 -> 2; matrix products, arithmetic and copies ran while one was open for 0% -> 0% of each run, Pallas kernels for 36% -> 35%
where the time goes in v3:
time: 58.3 us; the launch traced here: 57.5 us
  Pallas kernels  34 us (58%)
  starting transfers between devices  22.2 us (38%)
  between operations  0.74 us (1%)
  waiting for transfers between devices  0.64 us (1%)
    pallas_call x9, Pallas kernels, call(): pl.pallas_call(kernel, out_shape=shapes if many else shapes[0], in_specs=...  34 us
    all_to_all x4, starting transfers between devices, exchange(): lax.all_to_all(rows.reshape(tiles, CAP, width), 'tile', split_axis=0, con...  17.6 us
    ppermute x3, starting transfers between devices, other_regions(): lax.ppermute(total, 'region', [(i, (i + shift) % regions) for i in range(...  4.62 us
  transfers between devices with their start and end apart: 7, of which 2 were waited for; matrix products, arithmetic and copies ran while one was open for 0% of the time, Pallas kernels for 35%

profile of v3, /device:TPU:0, one launch (start us, length us, event | category | flops | bytes accessed | tf_op | source)
XLA Modules:
  0.0 57.5 jit_solution(2147124541922327976)
XLA Ops:
  0.6 2.2 %pack.1 = (f32[64,512]{1,0:T(8,128)}, bf16[64,256]{1,0:T(8,128)(2,1)S(1)}, bf16[256,64]{1,0:T(8,128)(2,1)S(1)}, bf16[48,64]{1,0:T(8,128)(2,1)S(1)}, f32[256,128]{1,0:T(8,128)S(1)}, /*index=5*/s32[256,128]{1,0:T(8,128)S(1)}) custom-call(s32[1]{0:T(128)} %bitcast.tile_ref, f32[48,128]{1,0:T(8,128)} %bfp_hbm.1, s32[48,128]{1,0:T(8,128)} %bidx_hbm.1, ...), custom_call_target="tpu_custom_call" | custom-call | bytes 7000000 | tf_op jit(solution)/shard_map/pack/pallas_call | solution.py:433
  2.8 5.2 %all-to-all-start = ((f32[8,8,512]{2,1,0:T(8,128)}), f32[8,8,512]{2,1,0:T(8,128)S(1)}, u32[]{:S(2)}, u32[]{:S(2)}) async-start(f32[8,8,512]{2,1,0:T(8,128)} %bitcast.3), calls=%async_computation | async-start | bytes 262144 | tf_op jit(solution)/shard_map/all_to_all | solution.py:447
  8.0 5.3 %prepare.1 = (bf16[256,4096]{1,0:T(8,128)(2,1)}, bf16[256,4096]{1,0:T(8,128)(2,1)}, f32[256,128]{1,0:T(8,128)}) custom-call(bf16[4096,256]{1,0:T(8,128)(2,1)} %movie_hbm.1, f32[256,128]{1,0:T(8,128)S(1)} %get-tuple-element.39.fp_ref, s32[256,128]{1,0:T(8,128)S(1)} %get-tuple-element.40.idx_ref, f32[1,4096]{1,0:T(1,128)} %bitcast.21), custom_call_target="tpu_custom_call" | custom-call | bytes 24500000 | tf_op jit(solution)/shard_map/prepare/pallas_call | solution.py:433
  13.3 0.2 all-to-all-done
  13.5 5.8 %project.1 = (bf16[256,4096]{1,0:T(8,128)(2,1)}, bf16[64,4096]{1,0:T(8,128)(2,1)}, f32[64,384]{1,0:T(8,128)}) custom-call(f32[64,512]{1,0:T(8,128)S(1)} %bitcast.14, bf16[256,4096]{1,0:T(8,128)(2,1)} %get-tuple-element.41.movie_t_hbm, bf16[256,4096]{1,0:T(8,128)(2,1)} %get-tuple-element.42.dense_hbm, f32[256,256]{1,0:T(8,128)} %old_hbm.5, ...), custom_call_target="tpu_custom_call" | custom-call | bytes 17500000 | tf_op jit(solution)/shard_map/project/pallas_call | solution.py:433
  19.4 4.0 %all-to-all-start.1 = ((f32[8,8,384]{2,1,0:T(8,128)}), f32[8,8,384]{2,1,0:T(8,128)S(1)}, u32[]{:S(2)}, u32[]{:S(2)}) async-start(f32[8,8,384]{2,1,0:T(8,128)} %bitcast.7), calls=%async_computation.1 | async-start | bytes 196608 | tf_op jit(solution)/shard_map/all_to_all | solution.py:447
  23.4 0.0 copy-done
  23.4 5.2 %own.1 = (f32[256,256]{1,0:T(8,128)S(1)}, f32[256,128]{1,0:T(8,128)S(1)}, f32[256,128]{1,0:T(8,128)S(1)}, f32[8,128]{1,0:T(8,128)S(1)}, bf16[1536,256]{1,0:T(8,128)(2,1)S(1)}) custom-call(f32[2]{0:T(128)S(1)} %copy-done, bf16[256,4096]{1,0:T(8,128)(2,1)} %get-tuple-element.42.dense_hbm, bf16[256,4096]{1,0:T(8,128)(2,1)} %get-tuple-element.44.resid_hbm, ...), custom_call_target="tpu_custom_call" | custom-call | bytes 14000000 | tf_op jit(solution)/shard_map/own/pallas_call | solution.py:433
  28.6 0.0 all-to-all-done.1
  28.6 2.1 %trace.1 = (f32[256,256]{1,0:T(8,128)}, f32[64,256]{1,0:T(8,128)}, f32[8,128]{1,0:T(8,128)S(1)}) custom-call(f32[2]{0:T(128)S(1)} %copy-done, f32[64,384]{1,0:T(8,128)S(1)} %bitcast.20, f32[256,256]{1,0:T(8,128)S(1)} %get-tuple-element.46.start_ref, f32[256,128]{1,0:T(8,128)S(1)} %get-tuple-element.47.scale_ref, ...), custom_call_target="tpu_custom_call" | custom-call | bytes 7000000 | tf_op jit(solution)/shard_map/trace/pallas_call | solution.py:433
  30.7 4.2 %all-to-all-start.2 = ((f32[8,8,256]{2,1,0:T(8,128)}), f32[8,8,256]{2,1,0:T(8,128)S(1)}, u32[]{:S(2)}, u32[]{:S(2)}) async-start(f32[8,8,256]{2,1,0:T(8,128)} %bitcast.9), calls=%async_computation.2 | async-start | bytes 131072 | tf_op jit(solution)/shard_map/all_to_all | solution.py:447
  34.9 3.6 %collective-permute-start.2 = (f32[8,128]{1,0:T(8,128)S(1)}, f32[8,128]{1,0:T(8,128)S(1)}, u32[]{:S(2)}, u32[]{:S(2)}) collective-permute-start(f32[8,128]{1,0:T(8,128)S(1)} %get-tuple-element.57.refs_0_), channel_id=1, source_target_pairs={{0,24},{8,0},{16,8},{24,16},{1,25},{9,1},{17,9},{25,17},{2,26},{10... | collective-permute-start | bytes 12296 | tf_op jit(solution)/shard_map/ppermute | solution.py:452
  38.5 0.0 collective-permute-start.1
  38.5 1.0 %collective-permute-start = (f32[8,128]{1,0:T(8,128)S(1)}, f32[8,128]{1,0:T(8,128)S(1)}, u32[]{:S(2)}, u32[]{:S(2)}) collective-permute-start(f32[8,128]{1,0:T(8,128)S(1)} %get-tuple-element.57.refs_0_), channel_id=1, source_target_pairs={{0,8},{8,16},{16,24},{24,0},{1,9},{9,17},{17,25},{25,1},{2,10},{10... | collective-permute-start | bytes 12296 | tf_op jit(solution)/shard_map/ppermute | solution.py:452
  39.6 3.9 %rest_own.1 = (bf16[256,4096]{1,0:T(8,128)(2,1)}, f32[64,128]{1,0:T(8,128)S(1)}) custom-call(bf16[256,4096]{1,0:T(8,128)(2,1)} %get-tuple-element.41.movie_t_hbm, bf16[256,4096]{1,0:T(8,128)(2,1)} %get-tuple-element.42.dense_hbm, f32[256,256]{1,0:T(8,128)} %get-tuple-element.34.new_hbm, f32[1,4096]{1,0:T(1,128)} %bitcast.24, f32[1,256]{1,0:T(1,128)} %bitcast.26, ...), custom_call_target="tpu_custom_call" | custom-call | bytes 14000000 | tf_op jit(solution)/shard_map/rest_own/pallas_call | solution.py:433
  43.5 0.0 all-to-all-done.2
  43.5 0.0 collective-permute-done.2.refs_3_
  43.5 0.0 collective-permute-done.1.refs_2_
  43.5 0.4 collective-permute-done.refs_1_
  44.0 3.0 %border.1 = f32[64,384]{1,0:T(8,128)} custom-call(f32[64,512]{1,0:T(8,128)S(1)} %bitcast.16, f32[64,256]{1,0:T(8,128)S(1)} %bitcast.17, f32[64,128]{1,0:T(8,128)S(1)} %get-tuple-element.56.seen_ref, f32[8,128]{1,0:T(8,128)S(1)} %get-tuple-element.57.refs_0_, f32[8,128]{1,0:T(8,128)S(1)} %collective-permute-done.refs_1_, ...), custom_call_target="tpu_custom_call" | custom-call | bytes 14000000 | tf_op jit(solution)/shard_map/border/pallas_call | solution.py:433
  47.0 4.2 %all-to-all-start.3 = ((f32[8,8,384]{2,1,0:T(8,128)}), f32[8,8,384]{2,1,0:T(8,128)S(1)}, u32[]{:S(2)}, u32[]{:S(2)}) async-start(f32[8,8,384]{2,1,0:T(8,128)} %bitcast.11), calls=%async_computation.3 | async-start | bytes 196608 | tf_op jit(solution)/shard_map/all_to_all | solution.py:447
  51.2 5.4 %footprint.1 = (f32[256,128]{1,0:T(8,128)S(1)}, f32[256,128]{1,0:T(8,128)S(1)}, bf16[256,256]{1,0:T(8,128)(2,1)S(1)}, f32[64,128]{1,0:T(8,128)S(1)}, f32[64,128]...) custom-call(f32[64,256]{1,0:T(8,128)S(1)} %bitcast.18, ...), custom_call_target="tpu_custom_call" | custom-call | bytes 17500000 | tf_op jit(solution)/shard_map/footprint/pallas_call | solution.py:433
  56.6 0.0 all-to-all-done.3
  56.6 0.9 %finish.1 = (f32[256,128]{1,0:T(8,128)}, f32[48,128]{1,0:T(8,128)}, f32[2,128]{1,0:T(2,128)}) custom-call(f32[64,384]{1,0:T(8,128)S(1)} %bitcast.19, f32[256,128]{1,0:T(8,128)S(1)} %get-tuple-element.61.base_ref, f32[256,128]{1,0:T(8,128)S(1)} %get-tuple-element.62.slope_ref, bf16[256,256]{1,0:T(8,128)(2,1)S(1)} %get-tuple-element.63.low_ref, ...), custom_call_target="tpu_custom_call" | custom-call | bytes 3500000 | tf_op jit(solution)/shard_map/finish/pallas_call | solution.py:433
  (1 shorter events, 0.0 us)
Async XLA Ops:
  2.8 10.7 %all-to-all-start = ((f32[8,8,512]{2,1,0:T(8,128)}), f32[8,8,512]{2,1,0:T(8,128)S(1)}, u32[]{:S(2)}, u32[]{:S(2)}) async-start(f32[8,8,512]{2,1,0:T(8,128)} %bitcast.3), calls=%async_computation | async-start | bytes 262144 | tf_op jit(solution)/shard_map/all_to_all | solution.py:447
  13.5 9.8 %copy-start = (f32[2]{0:T(128)S(1)}, f32[2]{0:T(128)}, u32[]{:S(2)}) copy-start(f32[2]{0:T(128)} %ar_ref.3) | copy-start | bytes 28
  19.4 9.2 %all-to-all-start.1 = ((f32[8,8,384]{2,1,0:T(8,128)}), f32[8,8,384]{2,1,0:T(8,128)S(1)}, u32[]{:S(2)}, u32[]{:S(2)}) async-start(f32[8,8,384]{2,1,0:T(8,128)} %bitcast.7), calls=%async_computation.1 | async-start | bytes 196608 | tf_op jit(solution)/shard_map/all_to_all | solution.py:447
  30.7 12.8 %all-to-all-start.2 = ((f32[8,8,256]{2,1,0:T(8,128)}), f32[8,8,256]{2,1,0:T(8,128)S(1)}, u32[]{:S(2)}, u32[]{:S(2)}) async-start(f32[8,8,256]{2,1,0:T(8,128)} %bitcast.9), calls=%async_computation.2 | async-start | bytes 131072 | tf_op jit(solution)/shard_map/all_to_all | solution.py:447
  34.9 8.6 %collective-permute-start.2 = (f32[8,128]{1,0:T(8,128)S(1)}, f32[8,128]{1,0:T(8,128)S(1)}, u32[]{:S(2)}, u32[]{:S(2)}) collective-permute-start(f32[8,128]{1,0:T(8,128)S(1)} %get-tuple-element.57.refs_0_), channel_id=1, source_target_pairs={{0,24},{8,0},{16,8},{24,16},{1,25},{9,1},{17,9},{25,17},{2,26},{10... | collective-permute-start | bytes 12296 | tf_op jit(solution)/shard_map/ppermute | solution.py:452
  38.5 5.0 %collective-permute-start.1 = (f32[8,128]{1,0:T(8,128)S(1)}, f32[8,128]{1,0:T(8,128)S(1)}, u32[]{:S(2)}, u32[]{:S(2)}) collective-permute-start(f32[8,128]{1,0:T(8,128)S(1)} %get-tuple-element.57.refs_0_), channel_id=1, source_target_pairs={{0,16},{8,24},{16,0},{24,8},{1,17},{9,25},{17,1},{25,9},{2,18},{10... | collective-permute-start | bytes 12296 | tf_op jit(solution)/shard_map/ppermute | solution.py:452
  38.5 5.4 %collective-permute-start = (f32[8,128]{1,0:T(8,128)S(1)}, f32[8,128]{1,0:T(8,128)S(1)}, u32[]{:S(2)}, u32[]{:S(2)}) collective-permute-start(f32[8,128]{1,0:T(8,128)S(1)} %get-tuple-element.57.refs_0_), channel_id=1, source_target_pairs={{0,8},{8,16},{16,24},{24,0},{1,9},{9,17},{17,25},{25,1},{2,10},{10... | collective-permute-start | bytes 12296 | tf_op jit(solution)/shard_map/ppermute | solution.py:452
  47.0 9.7 %all-to-all-start.3 = ((f32[8,8,384]{2,1,0:T(8,128)}), f32[8,8,384]{2,1,0:T(8,128)S(1)}, u32[]{:S(2)}, u32[]{:S(2)}) async-start(f32[8,8,384]{2,1,0:T(8,128)} %bitcast.11), calls=%async_computation.3 | async-start | bytes 196608 | tf_op jit(solution)/shard_map/all_to_all | solution.py:447

commit v4 on v3

--- a/solution.py
+++ b/solution.py
@@ -11,8 +11,6 @@
 F32 = jnp.float32
 BF16 = jnp.bfloat16
 VMEM_BYTES = 40 << 20
-CHUNK = 2048
-TURN = 512
 UNROLL = 128
 PAD = 8
 
@@ -60,8 +58,9 @@
     return jnp.where(iota(x.shape, len(x.shape) - 1) >= count, pltpu.roll(x, count, len(x.shape) - 1), 0.0)
 
 
-def pieces(width):
-    return [slice(start, start + CHUNK) for start in range(0, width, CHUNK)]
+def pieces(width, count):
+    step = width // count
+    return [slice(start, start + step) for start in range(0, width, step)]
 
 
 def fetch(source, target, sem):
@@ -73,7 +72,7 @@
 def fetch_columns(*copies):
     return [
         [fetch(source.at[:, here], target.at[:, here], sems.at[k]) for source, target, sems in copies]
-        for k, here in enumerate(pieces(copies[0][0].shape[1]))
+        for k, here in enumerate(pieces(copies[0][0].shape[1], copies[0][2].shape[0]))
     ]
 
 
@@ -118,8 +117,7 @@
     copies[6].wait()
 
 
-def scatter_rows(values_ref, index_ref, grid_ref, rows, stride, first=0):
-    cells = grid_ref.shape[0] // stride
+def scatter_rows(values_ref, index_ref, grid_ref, cells, rows, stride, first=0):
     support = values_ref.shape[1]
     hi_range = iota((cells, support), 0).astype(BF16)
     lo_range = iota((LANES, support), 0).astype(BF16)
@@ -151,13 +149,14 @@
         grid_ref[pl.ds(k + 1, cells, stride=stride), :] = made[2 * cells:3 * cells] + made[3 * cells:]
 
 
-def prepare_kernel(movie_hbm, fp_ref, idx_ref, spatial_hbm, dense_hbm, movie_t_hbm, seen_hbm,
-                   movie_ref, dense_ref, movie_t_ref, grid_ref, spatial_ref, seen_ref, movie_sem, sems, dense_sems, out_sems):
+def prepare_kernel(movie_hbm, fp_ref, idx_ref, spatial_hbm, dense_hbm, movie_t_hbm, seen_hbm, movie_t_ref,
+                   movie_ref, dense_ref, grid_ref, spatial_ref, seen_ref, movie_sem, sems, dense_sems, out_sems):
     owned = fp_ref.shape[0]
     voxels, frames = movie_hbm.shape
     groups = dense_sems.shape[0]
     rows = owned // groups
-    stride = grid_ref.shape[0] // (voxels // LANES)
+    cells = voxels // LANES
+    stride = rows + PAD
     first = fetch(spatial_hbm, spatial_ref, sems.at[0])
     load = fetch(movie_hbm, movie_ref, movie_sem)
     eye = jnp.where(iota((frames, frames), 0) == iota((frames, frames), 1), 1.0, 0.0).astype(BF16)
@@ -165,15 +164,15 @@
     first.wait()
     for group in range(groups):
         mine = slice(group * rows, (group + 1) * rows)
-        scatter_rows(fp_ref, idx_ref, grid_ref, rows, stride, group * rows)
+        scatter_rows(fp_ref, idx_ref, grid_ref, cells, rows, stride, group * rows)
         for start in range(mine.start, mine.stop, 8):
             seen_ref[start:start + 8, :] = pick_rows(spatial_ref, idx_ref[start:start + 8, :], slice(0, 1))
-        for cell in range(voxels // LANES):
+        for cell in range(cells):
             dense_ref[mine, cell * LANES:(cell + 1) * LANES] = grid_ref[cell * stride:cell * stride + rows, :].astype(BF16)
         stores.append(fetch(dense_ref.at[mine], dense_hbm.at[mine], dense_sems.at[group]))
         if group == 0:
             load.wait()
-            for k, here in enumerate(pieces(voxels)):
+            for k, here in enumerate(pieces(voxels, out_sems.shape[0])):
                 movie_t_ref[:, here] = nt(eye, movie_ref[here, :]).astype(BF16)
                 stores.append(fetch(movie_t_ref.at[:, here], movie_t_hbm.at[:, here], out_sems.at[k]))
     stores.append(fetch(seen_ref, seen_hbm, sems.at[1]))
@@ -185,22 +184,23 @@
     return jnp.concatenate([jnp.transpose(part.astype(F32)).astype(BF16) for part in split(x, 3)], axis=1)
 
 
-def project_kernel(recv_ref, movie_t_hbm, dense_hbm, old_hbm, spatial_hbm, trace_hbm, resid_hbm, dense_in_hbm, proj_ref,
-                   movie_t_ref, dense_ref, old_ref, spatial_ref, trace_ref, resid_ref, values_ref, idx_ref,
-                   grid_ref, in_sems, movie_sems, dense_sems, resid_sems, out_sem):
+def project_kernel(recv_ref, movie_t_ref, dense_hbm, old_hbm, spatial_hbm, trace_hbm, resid_hbm, dense_in_hbm, proj_ref,
+                   dense_ref, old_ref, spatial_ref, trace_ref, resid_ref, values_ref, idx_ref,
+                   grid_ref, in_sems, dense_sems, resid_sems, out_sem):
     slots = recv_ref.shape[0]
     owned = dense_hbm.shape[0]
-    frames, voxels = movie_t_hbm.shape
+    frames, voxels = movie_t_ref.shape
     support = values_ref.shape[1]
     stride = slots + PAD
     first = [fetch(spatial_hbm, spatial_ref, in_sems.at[1]), fetch(old_hbm, old_ref, in_sems.at[0]), fetch(trace_hbm, trace_ref, in_sems.at[2])]
-    loads = fetch_columns((dense_hbm, dense_ref.at[:owned], dense_sems), (movie_t_hbm, movie_t_ref, movie_sems))
+    loads = fetch_columns((dense_hbm, dense_ref.at[:owned], dense_sems))
+    in_t = transposed_parts(recv_ref[:, 2 * support:])
     values_ref[...] = recv_ref[:, :support]
     idx_ref[...] = recv_ref[:, support:2 * support].astype(jnp.int32)
-    scatter_rows(values_ref, idx_ref, grid_ref, slots, stride)
+    scatter_rows(values_ref, idx_ref, grid_ref, voxels // LANES, slots, stride)
     for copy in first:
         copy.wait()
-    both_t = jnp.concatenate([jnp.transpose(old_ref[...]).astype(BF16), transposed_parts(recv_ref[:, 2 * support:])], axis=1)
+    both_t = jnp.concatenate([jnp.transpose(old_ref[...]).astype(BF16), in_t], axis=1)
     back = to_column(trace_ref[...])
     seen_in = jnp.zeros((slots, LANES), F32)
     for cell in range(voxels // LANES):
@@ -211,7 +211,7 @@
         seen_in += part.astype(F32) * spatial_ref[:, at:at + LANES]
     mine = dense_ref.at[owned:owned + slots]
     stores = [fetch(mine, dense_in_hbm, out_sem)]
-    for k, here in enumerate(pieces(voxels)):
+    for k, here in enumerate(pieces(voxels, len(loads))):
         for copy in loads[k]:
             copy.wait()
         recon = nn(both_t, dense_ref[:, here]) + back * spatial_ref[:, here]
@@ -306,8 +306,8 @@
             out(here, pick_rows(grad_ref, idx_ref[here, :], slice(0, 1) if grad_ref.shape[0] == 1 else here))
 
 
-def rest_own_kernel(movie_t_hbm, dense_hbm, new_hbm, spatial_hbm, trace_hbm, recv_ref, rest_hbm, seen_ref,
-                    movie_t_ref, dense_ref, new_ref, spatial_ref, trace_ref, idx_ref, rest_ref, sems, movie_sems, dense_sems, out_sems):
+def rest_own_kernel(movie_t_hbm, dense_hbm, new_hbm, spatial_hbm, trace_hbm, recv_ref, rest_hbm, seen_ref, rest_ref,
+                    movie_t_ref, dense_ref, new_ref, spatial_ref, trace_ref, idx_ref, sems, movie_sems, dense_sems, out_sems):
     voxels = movie_t_hbm.shape[1]
     slots, support = idx_ref.shape
     first = [fetch(new_hbm, new_ref, sems.at[0]), fetch(spatial_hbm, spatial_ref, sems.at[1]), fetch(trace_hbm, trace_ref, sems.at[2])]
@@ -318,7 +318,7 @@
     new_t = jnp.transpose(new_ref[...]).astype(BF16)
     back = to_column(trace_ref[...])
     stores = []
-    for k, here in enumerate(pieces(voxels)):
+    for k, here in enumerate(pieces(voxels, len(loads))):
         for copy in loads[k]:
             copy.wait()
         recon = nn(new_t, dense_ref[:, here]) + back * spatial_ref[:, here]
@@ -349,23 +349,24 @@
 
 
 def border_kernel(recv0_ref, recv_ref, seen_ref, *refs):
-    *totals, rest_hbm, dense_in_hbm, send_ref, both_ref, grad_ref, idx_ref, sems, sems_near, sems_far = refs
-    in_sems = (sems_near, sems_far)
+    *totals, rest_ref, dense_in_hbm, send_ref, both_ref, grad_ref, idx_ref, sems = refs
+    frames = rest_ref.shape[0]
     slots, support = seen_ref.shape
-    loads = fetch_rest(rest_hbm, dense_in_hbm, both_ref, sems, in_sems)
+    loads = [fetch(dense_in_hbm, both_ref.at[copy * slots:(copy + 1) * slots], sems.at[copy]) for copy in range(2)]
     new = recv_ref[...]
     left = against_rest(new.astype(BF16), new)
     idx_ref[...] = recv0_ref[:, support:2 * support].astype(jnp.int32)
     send_ref[:, support:2 * support] = seen_ref[...]
-    total = totals[0][...]
-    for other in totals[1:]:
-        total = total + other[...]
+    terms = [ref[...] for ref in totals]
+    while len(terms) > 1:
+        terms = [a + b for a, b in zip(terms[::2], terms[1::2])] + terms[len(terms) // 2 * 2:]
+    total = terms[0]
     for tile in range(slots // CAP):
         send_ref[tile * CAP:(tile + 1) * CAP, 2 * support:] = total
-    for k, here in enumerate(pieces(both_ref.shape[1])):
-        for copy in loads[k]:
-            copy.wait()
-        grad_ref[:, here] = nn(left, both_ref[:, here])
+    grad_ref[...] = nn(left[:, :frames], rest_ref[...])
+    for copy in loads:
+        copy.wait()
+    grad_ref[...] += nn(left[:, frames:], both_ref[...])
 
     def out(here, picked):
         send_ref[here, :support] = picked
@@ -397,7 +398,7 @@
     sent_ref[...] = sent.astype(BF16)
     share_ref[...] = jnp.broadcast_to(1.0 / (jnp.sum(sent * sent, axis=1, keepdims=True) + RIDGE), (slots, support))
     border_ref[...] = send_ref[:, :support]
-    for k, here in enumerate(pieces(both_ref.shape[1])):
+    for k, here in enumerate(pieces(both_ref.shape[1], len(loads))):
         for copy in loads[k]:
             copy.wait()
         grad_ref[:, here] = nn(left, both_ref[:, here])
@@ -449,7 +450,9 @@
 
 
 def other_regions(total, regions):
-    return [lax.ppermute(total, "region", [(i, (i + shift) % regions) for i in range(regions)]) for shift in range(1, regions)]
+    if regions & (regions - 1):
+        return [lax.ppermute(total, "region", [(i, (i + shift) % regions) for i in range(regions)]) for shift in range(1, regions)]
+    return [lax.ppermute(total, "region", [(i, i ^ mask) for i in range(regions)]) for mask in range(1, regions)]
 
 
 def body(movie, footprint, support_idx, trace_old, ar_coef, border_fp, border_idx, border_owner, border_offset, back_spatial, back_trace):
@@ -463,7 +466,6 @@
     cells = voxels // LANES
     spatial = back_spatial.reshape(1, voxels)
     V, dma, i32 = pltpu.VMEM, pltpu.SemaphoreType.DMA, jnp.int32
-    n = voxels // CHUNK
     groups = owned // UNROLL
     wide = frames + LANES
 
@@ -475,20 +477,20 @@
         tile, border_fp, border_idx, border_owner.reshape(1, border), border_offset.reshape(1, border), trace_old, footprint, support_idx,
     )
     recv = exchange(send, tiles)
-    dense, movie_t, seen_own = call(
+    dense, movie_t, seen_own, movie_near = call(
         prepare_kernel, "prepare", 7, "hvvh",
-        [("h", (owned, voxels), BF16), ("h", (frames, voxels), BF16), ("h", (owned, support), F32)],
-        [V((voxels, frames), BF16), V((owned, voxels), BF16), V((frames, voxels), BF16),
-         V((cells * (UNROLL + PAD), LANES), F32), V((1, voxels), F32), V((owned, support), F32), dma, dma((2,)), dma((groups,)), dma((n,))],
+        [("h", (owned, voxels), BF16), ("h", (frames, voxels), BF16), ("h", (owned, support), F32), ("v", (frames, voxels), BF16)],
+        [V((voxels, frames), BF16), V((owned, voxels), BF16),
+         V(((cells + 1) * (UNROLL + PAD), LANES), F32), V((1, voxels), F32), V((owned, support), F32), dma, dma((2,)), dma((groups,)), dma((2,))],
         movie, footprint_near, support_near, spatial,
     )
     resid, dense_in, proj_in = call(
-        project_kernel, "project", 5, "vhhhhh",
+        project_kernel, "project", 5, "vvhhhh",
         [("h", (frames, voxels), BF16), ("h", (slots, voxels), BF16), ("v", (slots, wide), F32)],
-        [V((frames, voxels), BF16), V((owned + 3 * slots, voxels), BF16), V((owned, frames), F32), V((1, voxels), F32), V((1, frames), F32),
+        [V((owned + 3 * slots, voxels), BF16), V((owned, frames), F32), V((1, voxels), F32), V((1, frames), F32),
          V((frames, voxels), BF16), V((slots, support), F32), V((slots, support), i32),
-         V((cells * (slots + PAD), LANES), F32), dma((3,)), dma((n,)), dma((n,)), dma((n,)), dma],
-        recv, movie_t, dense, trace_old, spatial, back_trace.reshape(1, frames),
+         V(((cells + 1) * (slots + PAD), LANES), F32), dma((3,)), dma((2,)), dma((2,)), dma],
+        recv, movie_near, dense, trace_old, spatial, back_trace.reshape(1, frames),
     )
     returned = exchange(proj_in, tiles)
     start, scale, weight, base, impulse = call(
@@ -504,20 +506,20 @@
         ar_coef, returned, start, scale, weight, base, impulse, pick, pick_t,
     )
     recv_new = exchange(send_new, tiles)
-    totals = [part] + other_regions(part, regions)
+    totals = ([part] + other_regions(part, regions))[::-1]
     row_trace = back_trace.reshape(1, frames)
-    rest, seen = call(
-        rest_own_kernel, "rest_own", 4, "hhhhhv", [("h", (frames, voxels), BF16), ("v", (slots, support), F32)],
+    rest, seen, rest_near = call(
+        rest_own_kernel, "rest_own", 4, "hhhhhv", [("h", (frames, voxels), BF16), ("v", (slots, support), F32), ("v", (frames, voxels), BF16)],
         [V((frames, voxels), BF16), V((owned, voxels), BF16), V((owned, frames), F32), V((1, voxels), F32), V((1, frames), F32), V((slots, support), i32),
-         V((frames, voxels), BF16), dma((3,)), dma((n,)), dma((n,)), dma((n,))],
+         dma((3,)), dma((2,)), dma((2,)), dma((2,))],
         movie_t, dense, trace_new, spatial, row_trace, recv,
     )
     recv_new, seen = lax.optimization_barrier((recv_new, seen))
     both = 2 * slots + frames
     send_back = call(
-        border_kernel, "border", 4, "vvv" + "v" * regions + "hh", [("v", (slots, 2 * support + LANES), F32)],
-        [V((both, voxels), BF16), V((slots, voxels), F32), V((slots, support), i32), dma((n,)), dma((n,)), dma((n,))],
-        recv, recv_new, seen, *totals, rest, dense_in,
+        border_kernel, "border", 4, "vvv" + "v" * regions + "vh", [("v", (slots, 2 * support + LANES), F32)],
+        [V((2 * slots, voxels), BF16), V((slots, voxels), F32), V((slots, support), i32), dma((2,))],
+        recv, recv_new, seen, *totals, rest_near, dense_in,
     )
     back_rows = exchange(send_back, tiles)
     parts = call(
@@ -526,7 +528,7 @@
          ("v", (slots, frames), BF16), ("v", (1, frames), F32)],
         [V((both, voxels), BF16), V((owned, frames), F32), V((owned, support), F32), V((owned, support), i32), V((owned, support), F32),
          V((slots, 2 * support + frames), F32), V((slots, frames), F32), V((owned, voxels), F32), V((owned, support), F32),
-         dma((7,)), dma((n,)), dma((n,)), dma((n,))],
+         dma((7,)), dma((1,)), dma((1,)), dma((1,))],
         recv_new, rest, dense_in, trace_new, footprint, support_idx, seen_own, send, send_new, row_trace,
     )
     footprint_new, border_new, back = call(

time: 58.3 us -> 56.4 us (0.967)
  Pallas kernels: 34 us -> 32.6 us
    pallas_call x9, Pallas kernels: 34 us -> 32.6 us  [call(): pl.pallas_call(kernel, out_shape=shapes if many else shapes[0], in_specs=...]
where the time goes in v4:
time: 56.4 us; the launch traced here: 55.6 us
  Pallas kernels  32.6 us (58%)
  starting transfers between devices  21.7 us (38%)
  between operations  0.74 us (1%)
  waiting for transfers between devices  0.57 us (1%)
    pallas_call x9, Pallas kernels, call(): pl.pallas_call(kernel, out_shape=shapes if many else shapes[0], in_specs=...  32.6 us
    all_to_all x4, starting transfers between devices, exchange(): lax.all_to_all(rows.reshape(tiles, CAP, width), 'tile', split_axis=0, con...  17.3 us
    ppermute x3, starting transfers between devices, other_regions(): lax.ppermute(total, 'region', [(i, i ^ mask) for i in range(regions)])  4.39 us
  transfers between devices with their start and end apart: 7, of which 2 were waited for; matrix products, arithmetic and copies ran while one was open for 0% of the time, Pallas kernels for 35%

profile of v4, /device:TPU:0, one launch (start us, length us, event | category | flops | bytes accessed | tf_op | source)
XLA Modules:
  0.0 55.6 jit_solution(9701971465691450656)
XLA Ops:
  0.6 2.2 %pack.1 = (f32[64,512]{1,0:T(8,128)}, bf16[64,256]{1,0:T(8,128)(2,1)S(1)}, bf16[256,64]{1,0:T(8,128)(2,1)S(1)}, bf16[48,64]{1,0:T(8,128)(2,1)S(1)}, f32[256,128]{1,0:T(8,128)S(1)}, /*index=5*/s32[256,128]{1,0:T(8,128)S(1)}) custom-call(s32[1]{0:T(128)} %bitcast.tile_ref, f32[48,128]{1,0:T(8,128)} %bfp_hbm.1, s32[48,128]{1,0:T(8,128)} %bidx_hbm.1, ...), custom_call_target="tpu_custom_call" | custom-call | bytes 7000000 | tf_op jit(solution)/shard_map/pack/pallas_call | solution.py:434
  2.8 5.2 %all-to-all-start = ((f32[8,8,512]{2,1,0:T(8,128)}), f32[8,8,512]{2,1,0:T(8,128)S(1)}, u32[]{:S(2)}, u32[]{:S(2)}) async-start(f32[8,8,512]{2,1,0:T(8,128)} %bitcast.3), calls=%async_computation | async-start | bytes 262144 | tf_op jit(solution)/shard_map/all_to_all | solution.py:448
  8.0 5.0 %prepare.1 = (bf16[256,4096]{1,0:T(8,128)(2,1)}, bf16[256,4096]{1,0:T(8,128)(2,1)}, f32[256,128]{1,0:T(8,128)}, bf16[256,4096]{1,0:T(8,128)(2,1)S(1)}) custom-call(bf16[4096,256]{1,0:T(8,128)(2,1)} %movie_hbm.1, f32[256,128]{1,0:T(8,128)S(1)} %get-tuple-element.41.fp_ref, s32[256,128]{1,0:T(8,128)S(1)} %get-tuple-element.42.idx_ref, f32[1,4096]{1,0:T(1,128)} %bitcast.21), custom_call_target="tpu_custom_call" | custom-call | bytes 24500000 | tf_op jit(solution)/shard_map/prepare/pallas_call | solution.py:434
  13.1 0.5 all-to-all-done
  13.5 5.5 %project.1 = (bf16[256,4096]{1,0:T(8,128)(2,1)}, bf16[64,4096]{1,0:T(8,128)(2,1)}, f32[64,384]{1,0:T(8,128)}) custom-call(f32[64,512]{1,0:T(8,128)S(1)} %bitcast.14, bf16[256,4096]{1,0:T(8,128)(2,1)S(1)} %get-tuple-element.43.movie_t_ref, bf16[256,4096]{1,0:T(8,128)(2,1)} %get-tuple-element.44.dense_hbm, f32[256,256]{1,0:T(8,128)} %old_hbm.5, ...), custom_call_target="tpu_custom_call" | custom-call | bytes 17500000 | tf_op jit(solution)/shard_map/project/pallas_call | solution.py:434
  19.1 3.7 %all-to-all-start.1 = ((f32[8,8,384]{2,1,0:T(8,128)}), f32[8,8,384]{2,1,0:T(8,128)S(1)}, u32[]{:S(2)}, u32[]{:S(2)}) async-start(f32[8,8,384]{2,1,0:T(8,128)} %bitcast.7), calls=%async_computation.1 | async-start | bytes 196608 | tf_op jit(solution)/shard_map/all_to_all | solution.py:448
  22.8 0.0 copy-done
  22.8 5.2 %own.1 = (f32[256,256]{1,0:T(8,128)S(1)}, f32[256,128]{1,0:T(8,128)S(1)}, f32[256,128]{1,0:T(8,128)S(1)}, f32[8,128]{1,0:T(8,128)S(1)}, bf16[1536,256]{1,0:T(8,128)(2,1)S(1)}) custom-call(f32[2]{0:T(128)S(1)} %copy-done, bf16[256,4096]{1,0:T(8,128)(2,1)} %get-tuple-element.44.dense_hbm, bf16[256,4096]{1,0:T(8,128)(2,1)} %get-tuple-element.46.resid_hbm, ...), custom_call_target="tpu_custom_call" | custom-call | bytes 14000000 | tf_op jit(solution)/shard_map/own/pallas_call | solution.py:434
  28.1 0.0 all-to-all-done.1
  28.1 2.1 %trace.1 = (f32[256,256]{1,0:T(8,128)}, f32[64,256]{1,0:T(8,128)}, f32[8,128]{1,0:T(8,128)S(1)}) custom-call(f32[2]{0:T(128)S(1)} %copy-done, f32[64,384]{1,0:T(8,128)S(1)} %bitcast.20, f32[256,256]{1,0:T(8,128)S(1)} %get-tuple-element.49.start_ref, f32[256,128]{1,0:T(8,128)S(1)} %get-tuple-element.50.scale_ref, ...), custom_call_target="tpu_custom_call" | custom-call | bytes 7000000 | tf_op jit(solution)/shard_map/trace/pallas_call | solution.py:434
  30.2 4.2 %all-to-all-start.2 = ((f32[8,8,256]{2,1,0:T(8,128)}), f32[8,8,256]{2,1,0:T(8,128)S(1)}, u32[]{:S(2)}, u32[]{:S(2)}) async-start(f32[8,8,256]{2,1,0:T(8,128)} %bitcast.9), calls=%async_computation.2 | async-start | bytes 131072 | tf_op jit(solution)/shard_map/all_to_all | solution.py:448
  34.4 3.6 %collective-permute-start = (f32[8,128]{1,0:T(8,128)S(1)}, f32[8,128]{1,0:T(8,128)S(1)}, u32[]{:S(2)}, u32[]{:S(2)}) collective-permute-start(f32[8,128]{1,0:T(8,128)S(1)} %get-tuple-element.60.refs_3_), channel_id=1, source_target_pairs={{0,24},{8,16},{16,8},{24,0},{1,25},{9,17},{17,9},{25,1},{2,26},{10... | collective-permute-start | bytes 12296 | tf_op jit(solution)/shard_map/ppermute | solution.py:455
  38.0 0.0 collective-permute-start.1
  38.0 0.8 %collective-permute-start.2 = (f32[8,128]{1,0:T(8,128)S(1)}, f32[8,128]{1,0:T(8,128)S(1)}, u32[]{:S(2)}, u32[]{:S(2)}) collective-permute-start(f32[8,128]{1,0:T(8,128)S(1)} %get-tuple-element.60.refs_3_), channel_id=1, source_target_pairs={{0,8},{8,0},{16,24},{24,16},{1,9},{9,1},{17,25},{25,17},{2,10},{10... | collective-permute-start | bytes 12296 | tf_op jit(solution)/shard_map/ppermute | solution.py:455
  38.8 3.9 %rest_own.1 = (bf16[256,4096]{1,0:T(8,128)(2,1)}, f32[64,128]{1,0:T(8,128)S(1)}, bf16[256,4096]{1,0:T(8,128)(2,1)S(1)}) custom-call(bf16[256,4096]{1,0:T(8,128)(2,1)} %get-tuple-element.47.movie_t_hbm, bf16[256,4096]{1,0:T(8,128)(2,1)} %get-tuple-element.44.dense_hbm, f32[256,256]{1,0:T(8,128)} %get-tuple-element.36.new_hbm, f32[1,4096]{1,0:T(1,128)} %bitcast.24, ...), custom_call_target="tpu_custom_call" | custom-call | bytes 14000000 | tf_op jit(solution)/shard_map/rest_own/pallas_call | solution.py:434
  42.7 0.0 all-to-all-done.2
  42.7 0.0 collective-permute-done.refs_0_
  42.7 0.0 collective-permute-done.1.refs_1_
  42.8 0.0 collective-permute-done.2.refs_2_
  42.8 2.6 %border.1 = f32[64,384]{1,0:T(8,128)} custom-call(f32[64,512]{1,0:T(8,128)S(1)} %bitcast.16, f32[64,256]{1,0:T(8,128)S(1)} %bitcast.17, f32[64,128]{1,0:T(8,128)S(1)} %get-tuple-element.59.seen_ref, f32[8,128]{1,0:T(8,128)S(1)} %collective-permute-done.refs_0_, f32[8,128]{1,0:T(8,128)S(1)} %collective-permute-done.1.refs_1_, ...), custom_call_target="tpu_custom_call" | custom-call | bytes 14000000 | tf_op jit(solution)/shard_map/border/pallas_call | solution.py:434
  45.4 4.2 %all-to-all-start.3 = ((f32[8,8,384]{2,1,0:T(8,128)}), f32[8,8,384]{2,1,0:T(8,128)S(1)}, u32[]{:S(2)}, u32[]{:S(2)}) async-start(f32[8,8,384]{2,1,0:T(8,128)} %bitcast.11), calls=%async_computation.3 | async-start | bytes 196608 | tf_op jit(solution)/shard_map/all_to_all | solution.py:448
  49.6 5.1 %footprint.1 = (f32[256,128]{1,0:T(8,128)S(1)}, f32[256,128]{1,0:T(8,128)S(1)}, bf16[256,256]{1,0:T(8,128)(2,1)S(1)}, f32[64,128]{1,0:T(8,128)S(1)}, f32[64,128]...) custom-call(f32[64,256]{1,0:T(8,128)S(1)} %bitcast.18, ...), custom_call_target="tpu_custom_call" | custom-call | bytes 17500000 | tf_op jit(solution)/shard_map/footprint/pallas_call | solution.py:434
  54.7 0.1 all-to-all-done.3
  54.8 0.9 %finish.1 = (f32[256,128]{1,0:T(8,128)}, f32[48,128]{1,0:T(8,128)}, f32[2,128]{1,0:T(2,128)}) custom-call(f32[64,384]{1,0:T(8,128)S(1)} %bitcast.19, f32[256,128]{1,0:T(8,128)S(1)} %get-tuple-element.65.base_ref, f32[256,128]{1,0:T(8,128)S(1)} %get-tuple-element.66.slope_ref, bf16[256,256]{1,0:T(8,128)(2,1)S(1)} %get-tuple-element.67.low_ref, ...), custom_call_target="tpu_custom_call" | custom-call | bytes 3500000 | tf_op jit(solution)/shard_map/finish/pallas_call | solution.py:434
  (1 shorter events, 0.0 us)
Async XLA Ops:
  2.8 10.7 %all-to-all-start = ((f32[8,8,512]{2,1,0:T(8,128)}), f32[8,8,512]{2,1,0:T(8,128)S(1)}, u32[]{:S(2)}, u32[]{:S(2)}) async-start(f32[8,8,512]{2,1,0:T(8,128)} %bitcast.3), calls=%async_computation | async-start | bytes 262144 | tf_op jit(solution)/shard_map/all_to_all | solution.py:448
  13.5 9.3 %copy-start = (f32[2]{0:T(128)S(1)}, f32[2]{0:T(128)}, u32[]{:S(2)}) copy-start(f32[2]{0:T(128)} %ar_ref.3) | copy-start | bytes 28
  19.1 9.0 %all-to-all-start.1 = ((f32[8,8,384]{2,1,0:T(8,128)}), f32[8,8,384]{2,1,0:T(8,128)S(1)}, u32[]{:S(2)}, u32[]{:S(2)}) async-start(f32[8,8,384]{2,1,0:T(8,128)} %bitcast.7), calls=%async_computation.1 | async-start | bytes 196608 | tf_op jit(solution)/shard_map/all_to_all | solution.py:448
  30.2 12.5 %all-to-all-start.2 = ((f32[8,8,256]{2,1,0:T(8,128)}), f32[8,8,256]{2,1,0:T(8,128)S(1)}, u32[]{:S(2)}, u32[]{:S(2)}) async-start(f32[8,8,256]{2,1,0:T(8,128)} %bitcast.9), calls=%async_computation.2 | async-start | bytes 131072 | tf_op jit(solution)/shard_map/all_to_all | solution.py:448
  34.4 8.4 %collective-permute-start = (f32[8,128]{1,0:T(8,128)S(1)}, f32[8,128]{1,0:T(8,128)S(1)}, u32[]{:S(2)}, u32[]{:S(2)}) collective-permute-start(f32[8,128]{1,0:T(8,128)S(1)} %get-tuple-element.60.refs_3_), channel_id=1, source_target_pairs={{0,24},{8,16},{16,8},{24,0},{1,25},{9,17},{17,9},{25,1},{2,26},{10... | collective-permute-start | bytes 12296 | tf_op jit(solution)/shard_map/ppermute | solution.py:455
  38.0 4.7 %collective-permute-start.1 = (f32[8,128]{1,0:T(8,128)S(1)}, f32[8,128]{1,0:T(8,128)S(1)}, u32[]{:S(2)}, u32[]{:S(2)}) collective-permute-start(f32[8,128]{1,0:T(8,128)S(1)} %get-tuple-element.60.refs_3_), channel_id=1, source_target_pairs={{0,16},{8,24},{16,0},{24,8},{1,17},{9,25},{17,1},{25,9},{2,18},{10... | collective-permute-start | bytes 12296 | tf_op jit(solution)/shard_map/ppermute | solution.py:455
  38.0 4.8 %collective-permute-start.2 = (f32[8,128]{1,0:T(8,128)S(1)}, f32[8,128]{1,0:T(8,128)S(1)}, u32[]{:S(2)}, u32[]{:S(2)}) collective-permute-start(f32[8,128]{1,0:T(8,128)S(1)} %get-tuple-element.60.refs_3_), channel_id=1, source_target_pairs={{0,8},{8,0},{16,24},{24,16},{1,9},{9,1},{17,25},{25,17},{2,10},{10... | collective-permute-start | bytes 12296 | tf_op jit(solution)/shard_map/ppermute | solution.py:455
  45.4 9.4 %all-to-all-start.3 = ((f32[8,8,384]{2,1,0:T(8,128)}), f32[8,8,384]{2,1,0:T(8,128)S(1)}, u32[]{:S(2)}, u32[]{:S(2)}) async-start(f32[8,8,384]{2,1,0:T(8,128)} %bitcast.11), calls=%async_computation.3 | async-start | bytes 196608 | tf_op jit(solution)/shard_map/all_to_all | solution.py:448

commit v5 on v4

--- a/solution.py
+++ b/solution.py
@@ -149,8 +149,8 @@
         grid_ref[pl.ds(k + 1, cells, stride=stride), :] = made[2 * cells:3 * cells] + made[3 * cells:]
 
 
-def prepare_kernel(movie_hbm, fp_ref, idx_ref, spatial_hbm, dense_hbm, movie_t_hbm, seen_hbm, movie_t_ref,
-                   movie_ref, dense_ref, grid_ref, spatial_ref, seen_ref, movie_sem, sems, dense_sems, out_sems):
+def prepare_kernel(movie_hbm, fp_ref, idx_ref, spatial_hbm, old_hbm, trace_hbm, dense_hbm, movie_t_hbm, seen_hbm, movie_t_ref, old_t_ref, back_ref,
+                   movie_ref, dense_ref, grid_ref, spatial_ref, seen_ref, old_ref, trace_ref, movie_sem, sems, dense_sems, out_sems):
     owned = fp_ref.shape[0]
     voxels, frames = movie_hbm.shape
     groups = dense_sems.shape[0]
@@ -159,6 +159,7 @@
     stride = rows + PAD
     first = fetch(spatial_hbm, spatial_ref, sems.at[0])
     load = fetch(movie_hbm, movie_ref, movie_sem)
+    later = [fetch(old_hbm, old_ref, sems.at[2]), fetch(trace_hbm, trace_ref, sems.at[3])]
     eye = jnp.where(iota((frames, frames), 0) == iota((frames, frames), 1), 1.0, 0.0).astype(BF16)
     stores = []
     first.wait()
@@ -172,6 +173,10 @@
         stores.append(fetch(dense_ref.at[mine], dense_hbm.at[mine], dense_sems.at[group]))
         if group == 0:
             load.wait()
+            for copy in later:
+                copy.wait()
+            old_t_ref[...] = jnp.transpose(old_ref[...]).astype(BF16)
+            back_ref[...] = jnp.broadcast_to(to_column(trace_ref[...]), back_ref.shape)
             for k, here in enumerate(pieces(voxels, out_sems.shape[0])):
                 movie_t_ref[:, here] = nt(eye, movie_ref[here, :]).astype(BF16)
                 stores.append(fetch(movie_t_ref.at[:, here], movie_t_hbm.at[:, here], out_sems.at[k]))
@@ -184,15 +189,15 @@
     return jnp.concatenate([jnp.transpose(part.astype(F32)).astype(BF16) for part in split(x, 3)], axis=1)
 
 
-def project_kernel(recv_ref, movie_t_ref, dense_hbm, old_hbm, spatial_hbm, trace_hbm, resid_hbm, dense_in_hbm, proj_ref,
-                   dense_ref, old_ref, spatial_ref, trace_ref, resid_ref, values_ref, idx_ref,
+def project_kernel(recv_ref, movie_t_ref, dense_hbm, old_t_ref, spatial_hbm, back_ref, resid_hbm, dense_in_hbm, proj_ref,
+                   dense_ref, spatial_ref, resid_ref, values_ref, idx_ref,
                    grid_ref, in_sems, dense_sems, resid_sems, out_sem):
     slots = recv_ref.shape[0]
     owned = dense_hbm.shape[0]
     frames, voxels = movie_t_ref.shape
     support = values_ref.shape[1]
     stride = slots + PAD
-    first = [fetch(spatial_hbm, spatial_ref, in_sems.at[1]), fetch(old_hbm, old_ref, in_sems.at[0]), fetch(trace_hbm, trace_ref, in_sems.at[2])]
+    first = [fetch(spatial_hbm, spatial_ref, in_sems.at[0])]
     loads = fetch_columns((dense_hbm, dense_ref.at[:owned], dense_sems))
     in_t = transposed_parts(recv_ref[:, 2 * support:])
     values_ref[...] = recv_ref[:, :support]
@@ -200,8 +205,8 @@
     scatter_rows(values_ref, idx_ref, grid_ref, voxels // LANES, slots, stride)
     for copy in first:
         copy.wait()
-    both_t = jnp.concatenate([jnp.transpose(old_ref[...]).astype(BF16), in_t], axis=1)
-    back = to_column(trace_ref[...])
+    both_t = jnp.concatenate([old_t_ref[...], in_t], axis=1)
+    back = back_ref[:, 0:1]
     seen_in = jnp.zeros((slots, LANES), F32)
     for cell in range(voxels // LANES):
         at = cell * LANES
@@ -477,20 +482,21 @@
         tile, border_fp, border_idx, border_owner.reshape(1, border), border_offset.reshape(1, border), trace_old, footprint, support_idx,
     )
     recv = exchange(send, tiles)
-    dense, movie_t, seen_own, movie_near = call(
-        prepare_kernel, "prepare", 7, "hvvh",
-        [("h", (owned, voxels), BF16), ("h", (frames, voxels), BF16), ("h", (owned, support), F32), ("v", (frames, voxels), BF16)],
+    dense, movie_t, seen_own, movie_near, old_t, back_column = call(
+        prepare_kernel, "prepare", 7, "hvvhhh",
+        [("h", (owned, voxels), BF16), ("h", (frames, voxels), BF16), ("h", (owned, support), F32), ("v", (frames, voxels), BF16),
+         ("v", (frames, owned), BF16), ("v", (frames, LANES), F32)],
         [V((voxels, frames), BF16), V((owned, voxels), BF16),
-         V(((cells + 1) * (UNROLL + PAD), LANES), F32), V((1, voxels), F32), V((owned, support), F32), dma, dma((2,)), dma((groups,)), dma((2,))],
-        movie, footprint_near, support_near, spatial,
+         V(((cells + 1) * (UNROLL + PAD), LANES), F32), V((1, voxels), F32), V((owned, support), F32), V((owned, frames), F32), V((1, frames), F32), dma, dma((4,)), dma((groups,)), dma((2,))],
+        movie, footprint_near, support_near, spatial, trace_old, back_trace.reshape(1, frames),
     )
     resid, dense_in, proj_in = call(
-        project_kernel, "project", 5, "vvhhhh",
+        project_kernel, "project", 5, "vvhvhv",
         [("h", (frames, voxels), BF16), ("h", (slots, voxels), BF16), ("v", (slots, wide), F32)],
-        [V((owned + 3 * slots, voxels), BF16), V((owned, frames), F32), V((1, voxels), F32), V((1, frames), F32),
+        [V((owned + 3 * slots, voxels), BF16), V((1, voxels), F32),
          V((frames, voxels), BF16), V((slots, support), F32), V((slots, support), i32),
-         V(((cells + 1) * (slots + PAD), LANES), F32), dma((3,)), dma((2,)), dma((2,)), dma],
-        recv, movie_near, dense, trace_old, spatial, back_trace.reshape(1, frames),
+         V(((cells + 1) * (slots + PAD), LANES), F32), dma((1,)), dma((2,)), dma((2,)), dma],
+        recv, movie_near, dense, old_t, spatial, back_column,
     )
     returned = exchange(proj_in, tiles)
     start, scale, weight, base, impulse = call(

time: 56.4 us -> 57.6 us (1.021)
  waiting for transfers between devices: 0.57 us -> 1.67 us
    ppermute x3, waiting for transfers between devices: 0.01 us -> 1.2 us  [other_regions(): lax.ppermute(total, 'region', [(i, i ^ mask) for i in range(regions)])]
  transfers between devices with their start and end apart: 7 -> 7, of which waited for: 2 -> 3; matrix products, arithmetic and copies ran while one was open for 0% -> 0% of each run, Pallas kernels for 35% -> 34%
where the time goes in v5:
time: 57.6 us; the launch traced here: 56.9 us
  Pallas kernels  32.7 us (57%)
  starting transfers between devices  21.8 us (38%)
  waiting for transfers between devices  1.67 us (3%)
  between operations  0.73 us (1%)
    pallas_call x9, Pallas kernels, call(): pl.pallas_call(kernel, out_shape=shapes if many else shapes[0], in_specs=...  32.7 us
    all_to_all x4, starting transfers between devices, exchange(): lax.all_to_all(rows.reshape(tiles, CAP, width), 'tile', split_axis=0, con...  17.4 us
    ppermute x3, starting transfers between devices, other_regions(): lax.ppermute(total, 'region', [(i, i ^ mask) for i in range(regions)])  4.39 us
    ppermute x3, waiting for transfers between devices, other_regions(): lax.ppermute(total, 'region', [(i, i ^ mask) for i in range(regions)])  1.2 us
  transfers between devices with their start and end apart: 7, of which 3 were waited for; matrix products, arithmetic and copies ran while one was open for 0% of the time, Pallas kernels for 34%

profile of v5, /device:TPU:0, one launch (start us, length us, event | category | flops | bytes accessed | tf_op | source)
XLA Modules:
  0.0 56.9 jit_solution(3098517289077244490)
XLA Ops:
  0.6 2.2 %pack.1 = (f32[64,512]{1,0:T(8,128)}, bf16[64,256]{1,0:T(8,128)(2,1)S(1)}, bf16[256,64]{1,0:T(8,128)(2,1)S(1)}, bf16[48,64]{1,0:T(8,128)(2,1)S(1)}, f32[256,128]{1,0:T(8,128)S(1)}, /*index=5*/s32[256,128]{1,0:T(8,128)S(1)}) custom-call(s32[1]{0:T(128)} %bitcast.tile_ref, f32[48,128]{1,0:T(8,128)} %bfp_hbm.1, s32[48,128]{1,0:T(8,128)} %bidx_hbm.1, ...), custom_call_target="tpu_custom_call" | custom-call | bytes 7000000 | tf_op jit(solution)/shard_map/pack/pallas_call | solution.py:439
  2.8 5.2 %all-to-all-start = ((f32[8,8,512]{2,1,0:T(8,128)}), f32[8,8,512]{2,1,0:T(8,128)S(1)}, u32[]{:S(2)}, u32[]{:S(2)}) async-start(f32[8,8,512]{2,1,0:T(8,128)} %bitcast.3), calls=%async_computation | async-start | bytes 262144 | tf_op jit(solution)/shard_map/all_to_all | solution.py:453
  8.0 5.1 %prepare.1 = (bf16[256,4096]{1,0:T(8,128)(2,1)}, bf16[256,4096]{1,0:T(8,128)(2,1)}, f32[256,128]{1,0:T(8,128)}, bf16[256,4096]{1,0:T(8,128)(2,1)S(1)}, bf16[256,...) custom-call(bf16[4096,256]{1,0:T(8,128)(2,1)} %movie_hbm.1, f32[256,128]{1,0:T(8,128)S(1)} %get-tuple-element.43.fp_ref, ...), custom_call_target="tpu_custom_call" | custom-call | bytes 24500000 | tf_op jit(solution)/shard_map/prepare/pallas_call | solution.py:439
  13.2 0.4 all-to-all-done
  13.5 5.5 %project.1 = (bf16[256,4096]{1,0:T(8,128)(2,1)}, bf16[64,4096]{1,0:T(8,128)(2,1)}, f32[64,384]{1,0:T(8,128)}) custom-call(f32[64,512]{1,0:T(8,128)S(1)} %bitcast.14, bf16[256,4096]{1,0:T(8,128)(2,1)S(1)} %get-tuple-element.45.movie_t_ref, bf16[256,4096]{1,0:T(8,128)(2,1)} %get-tuple-element.46.dense_hbm, bf16[256,256]{1,0:T(8,128)(2,1)S(1)} %get-tuple-element.47.old_t_ref, ...), custom_call_target="tpu_custom_call" | custom-call | bytes 17500000 | tf_op jit(solution)/shard_map/project/pallas_call | solution.py:439
  19.0 3.8 %all-to-all-start.1 = ((f32[8,8,384]{2,1,0:T(8,128)}), f32[8,8,384]{2,1,0:T(8,128)S(1)}, u32[]{:S(2)}, u32[]{:S(2)}) async-start(f32[8,8,384]{2,1,0:T(8,128)} %bitcast.7), calls=%async_computation.1 | async-start | bytes 196608 | tf_op jit(solution)/shard_map/all_to_all | solution.py:453
  22.9 0.0 copy-done
  22.9 5.2 %own.1 = (f32[256,256]{1,0:T(8,128)S(1)}, f32[256,128]{1,0:T(8,128)S(1)}, f32[256,128]{1,0:T(8,128)S(1)}, f32[8,128]{1,0:T(8,128)S(1)}, bf16[1536,256]{1,0:T(8,128)(2,1)S(1)}) custom-call(f32[2]{0:T(128)S(1)} %copy-done, bf16[256,4096]{1,0:T(8,128)(2,1)} %get-tuple-element.46.dense_hbm, bf16[256,4096]{1,0:T(8,128)(2,1)} %get-tuple-element.50.resid_hbm, ...), custom_call_target="tpu_custom_call" | custom-call | bytes 14000000 | tf_op jit(solution)/shard_map/own/pallas_call | solution.py:439
  28.1 0.0 all-to-all-done.1
  28.1 2.1 %trace.1 = (f32[256,256]{1,0:T(8,128)}, f32[64,256]{1,0:T(8,128)}, f32[8,128]{1,0:T(8,128)S(1)}) custom-call(f32[2]{0:T(128)S(1)} %copy-done, f32[64,384]{1,0:T(8,128)S(1)} %bitcast.20, f32[256,256]{1,0:T(8,128)S(1)} %get-tuple-element.53.start_ref, f32[256,128]{1,0:T(8,128)S(1)} %get-tuple-element.54.scale_ref, ...), custom_call_target="tpu_custom_call" | custom-call | bytes 7000000 | tf_op jit(solution)/shard_map/trace/pallas_call | solution.py:439
  30.3 4.2 %all-to-all-start.2 = ((f32[8,8,256]{2,1,0:T(8,128)}), f32[8,8,256]{2,1,0:T(8,128)S(1)}, u32[]{:S(2)}, u32[]{:S(2)}) async-start(f32[8,8,256]{2,1,0:T(8,128)} %bitcast.9), calls=%async_computation.2 | async-start | bytes 131072 | tf_op jit(solution)/shard_map/all_to_all | solution.py:453
  34.5 1.6 %collective-permute-start.2 = (f32[8,128]{1,0:T(8,128)S(1)}, f32[8,128]{1,0:T(8,128)S(1)}, u32[]{:S(2)}, u32[]{:S(2)}) collective-permute-start(f32[8,128]{1,0:T(8,128)S(1)} %get-tuple-element.64.refs_3_), channel_id=1, source_target_pairs={{0,8},{8,0},{16,24},{24,16},{1,9},{9,1},{17,25},{25,17},{2,10},{10... | collective-permute-start | bytes 12296 | tf_op jit(solution)/shard_map/ppermute | solution.py:460
  36.0 2.6 %collective-permute-start.1 = (f32[8,128]{1,0:T(8,128)S(1)}, f32[8,128]{1,0:T(8,128)S(1)}, u32[]{:S(2)}, u32[]{:S(2)}) collective-permute-start(f32[8,128]{1,0:T(8,128)S(1)} %get-tuple-element.64.refs_3_), channel_id=1, source_target_pairs={{0,16},{8,24},{16,0},{24,8},{1,17},{9,25},{17,1},{25,9},{2,18},{10... | collective-permute-start | bytes 12296 | tf_op jit(solution)/shard_map/ppermute | solution.py:460
  38.6 0.2 collective-permute-start
  38.8 3.9 %rest_own.1 = (bf16[256,4096]{1,0:T(8,128)(2,1)}, f32[64,128]{1,0:T(8,128)S(1)}, bf16[256,4096]{1,0:T(8,128)(2,1)S(1)}) custom-call(bf16[256,4096]{1,0:T(8,128)(2,1)} %get-tuple-element.51.movie_t_hbm, bf16[256,4096]{1,0:T(8,128)(2,1)} %get-tuple-element.46.dense_hbm, f32[256,256]{1,0:T(8,128)} %get-tuple-element.38.new_hbm, f32[1,4096]{1,0:T(1,128)} %bitcast.24, ...), custom_call_target="tpu_custom_call" | custom-call | bytes 14000000 | tf_op jit(solution)/shard_map/rest_own/pallas_call | solution.py:439
  42.8 0.0 all-to-all-done.2
  42.8 0.0 collective-permute-done.2.refs_2_
  42.8 0.0 collective-permute-done.1.refs_1_
  42.8 1.2 %collective-permute-done.refs_0_ = f32[8,128]{1,0:T(8,128)S(1)} collective-permute-done((f32[8,128]{1,0:T(8,128)S(1)}, f32[8,128]{1,0:T(8,128)S(1)}, u32[]{:S(2)}, u32[]{:S(2)}) %collective-permute-start) | collective-permute-done | bytes 4128 | tf_op jit(solution)/shard_map/ppermute | solution.py:460
  44.0 2.6 %border.1 = f32[64,384]{1,0:T(8,128)} custom-call(f32[64,512]{1,0:T(8,128)S(1)} %bitcast.16, f32[64,256]{1,0:T(8,128)S(1)} %bitcast.17, f32[64,128]{1,0:T(8,128)S(1)} %get-tuple-element.63.seen_ref, f32[8,128]{1,0:T(8,128)S(1)} %collective-permute-done.refs_0_, f32[8,128]{1,0:T(8,128)S(1)} %collective-permute-done.1.refs_1_, ...), custom_call_target="tpu_custom_call" | custom-call | bytes 14000000 | tf_op jit(solution)/shard_map/border/pallas_call | solution.py:439
  46.6 4.2 %all-to-all-start.3 = ((f32[8,8,384]{2,1,0:T(8,128)}), f32[8,8,384]{2,1,0:T(8,128)S(1)}, u32[]{:S(2)}, u32[]{:S(2)}) async-start(f32[8,8,384]{2,1,0:T(8,128)} %bitcast.11), calls=%async_computation.3 | async-start | bytes 196608 | tf_op jit(solution)/shard_map/all_to_all | solution.py:453
  50.8 5.1 %footprint.1 = (f32[256,128]{1,0:T(8,128)S(1)}, f32[256,128]{1,0:T(8,128)S(1)}, bf16[256,256]{1,0:T(8,128)(2,1)S(1)}, f32[64,128]{1,0:T(8,128)S(1)}, f32[64,128]...) custom-call(f32[64,256]{1,0:T(8,128)S(1)} %bitcast.18, ...), custom_call_target="tpu_custom_call" | custom-call | bytes 17500000 | tf_op jit(solution)/shard_map/footprint/pallas_call | solution.py:439
  55.9 0.1 all-to-all-done.3
  56.0 0.9 %finish.1 = (f32[256,128]{1,0:T(8,128)}, f32[48,128]{1,0:T(8,128)}, f32[2,128]{1,0:T(2,128)}) custom-call(f32[64,384]{1,0:T(8,128)S(1)} %bitcast.19, f32[256,128]{1,0:T(8,128)S(1)} %get-tuple-element.69.base_ref, f32[256,128]{1,0:T(8,128)S(1)} %get-tuple-element.70.slope_ref, bf16[256,256]{1,0:T(8,128)(2,1)S(1)} %get-tuple-element.71.low_ref, ...), custom_call_target="tpu_custom_call" | custom-call | bytes 3500000 | tf_op jit(solution)/shard_map/finish/pallas_call | solution.py:439
  (1 shorter events, 0.0 us)
Async XLA Ops:
  2.8 10.7 %all-to-all-start = ((f32[8,8,512]{2,1,0:T(8,128)}), f32[8,8,512]{2,1,0:T(8,128)S(1)}, u32[]{:S(2)}, u32[]{:S(2)}) async-start(f32[8,8,512]{2,1,0:T(8,128)} %bitcast.3), calls=%async_computation | async-start | bytes 262144 | tf_op jit(solution)/shard_map/all_to_all | solution.py:453
  13.5 9.3 %copy-start = (f32[2]{0:T(128)S(1)}, f32[2]{0:T(128)}, u32[]{:S(2)}) copy-start(f32[2]{0:T(128)} %ar_ref.3) | copy-start | bytes 28
  19.0 9.1 %all-to-all-start.1 = ((f32[8,8,384]{2,1,0:T(8,128)}), f32[8,8,384]{2,1,0:T(8,128)S(1)}, u32[]{:S(2)}, u32[]{:S(2)}) async-start(f32[8,8,384]{2,1,0:T(8,128)} %bitcast.7), calls=%async_computation.1 | async-start | bytes 196608 | tf_op jit(solution)/shard_map/all_to_all | solution.py:453
  30.3 12.5 %all-to-all-start.2 = ((f32[8,8,256]{2,1,0:T(8,128)}), f32[8,8,256]{2,1,0:T(8,128)S(1)}, u32[]{:S(2)}, u32[]{:S(2)}) async-start(f32[8,8,256]{2,1,0:T(8,128)} %bitcast.9), calls=%async_computation.2 | async-start | bytes 131072 | tf_op jit(solution)/shard_map/all_to_all | solution.py:453
  34.5 8.4 %collective-permute-start.2 = (f32[8,128]{1,0:T(8,128)S(1)}, f32[8,128]{1,0:T(8,128)S(1)}, u32[]{:S(2)}, u32[]{:S(2)}) collective-permute-start(f32[8,128]{1,0:T(8,128)S(1)} %get-tuple-element.64.refs_3_), channel_id=1, source_target_pairs={{0,8},{8,0},{16,24},{24,16},{1,9},{9,1},{17,25},{25,17},{2,10},{10... | collective-permute-start | bytes 12296 | tf_op jit(solution)/shard_map/ppermute | solution.py:460
  36.0 6.8 %collective-permute-start.1 = (f32[8,128]{1,0:T(8,128)S(1)}, f32[8,128]{1,0:T(8,128)S(1)}, u32[]{:S(2)}, u32[]{:S(2)}) collective-permute-start(f32[8,128]{1,0:T(8,128)S(1)} %get-tuple-element.64.refs_3_), channel_id=1, source_target_pairs={{0,16},{8,24},{16,0},{24,8},{1,17},{9,25},{17,1},{25,9},{2,18},{10... | collective-permute-start | bytes 12296 | tf_op jit(solution)/shard_map/ppermute | solution.py:460
  38.6 5.4 %collective-permute-start = (f32[8,128]{1,0:T(8,128)S(1)}, f32[8,128]{1,0:T(8,128)S(1)}, u32[]{:S(2)}, u32[]{:S(2)}) collective-permute-start(f32[8,128]{1,0:T(8,128)S(1)} %get-tuple-element.64.refs_3_), channel_id=1, source_target_pairs={{0,24},{8,16},{16,8},{24,0},{1,25},{9,17},{17,9},{25,1},{2,26},{10... | collective-permute-start | bytes 12296 | tf_op jit(solution)/shard_map/ppermute | solution.py:460
  46.6 9.4 %all-to-all-start.3 = ((f32[8,8,384]{2,1,0:T(8,128)}), f32[8,8,384]{2,1,0:T(8,128)S(1)}, u32[]{:S(2)}, u32[]{:S(2)}) async-start(f32[8,8,384]{2,1,0:T(8,128)} %bitcast.11), calls=%async_computation.3 | async-start | bytes 196608 | tf_op jit(solution)/shard_map/all_to_all | solution.py:453
